TPU v7x, 512 devices: a whole 4x4x16 slice. The times are simulated.
512 devices in a mesh: ctx: 32 (over y_lo, z), fsdp: 16 (over y_hi, x, core).
Axes of the slice: x: 4, y: 4 (y_hi: 2, y_lo: 2; y = y_hi * 2 + y_lo), z: 16, core: 2. Of those that a mesh axis runs over, the one named last changes fastest.
Arguments:
- sig_raw: bfloat16 [4096, 8192], P('ctx', 'fsdp'), may hold values from -6 to 6
- map_raw: bfloat16 [4096, 2048], P('ctx'), may hold values from -1.796875 to 1.796875
- step_size_logits: float32 [4096, 128], P('ctx', 'fsdp'), may hold values from -5.4 to 21.5
- d_out: bfloat16 [4096, 8192], P('ctx', 'fsdp'), may hold values from -6 to 6
- sig_taps: float32 [4, 8192], P(None, 'fsdp'), may hold values from -3 to 3
- map_taps: float32 [4, 2048], P(None, 'fsdp'), may hold values from -3 to 3
- sig_bias: float32 [8192], P('fsdp'), may hold values from -3 to 3
- map_bias: float32 [2048], P('fsdp'), may hold values from -0.6 to 0.6
- a_log: float32 [128], P('fsdp'), as said below
- dt_bias: float32 [128], P('fsdp'), may hold values from -5 to -4.2
- skip_gain: float32 [128], P('fsdp'), may hold values from 0.1 to 3
Outputs:
- d_sig: float32 [4096, 8192], P('ctx', 'fsdp')
- d_map: float32 [4096, 2048], P('ctx', 'fsdp')
- d_dt: float32 [4096, 128], P('ctx', 'fsdp')
- d_sig_taps: float32 [4, 8192], P(None, 'fsdp')
- d_map_taps: float32 [4, 2048], P(None, 'fsdp')
- d_sig_bias: float32 [8192], P('fsdp')
- d_map_bias: float32 [2048], P('fsdp')
- d_a_log: float32 [128], P('fsdp')
- scaled_timestep_shift_grad: float32 [128], P('fsdp')
- d_skip: float32 [128], P('fsdp')
Inputs may be any that keep to these rules, and one draw needn't show every extreme that they name: Each head's rate exp(a_log) lies either between 2 and 4 or between 30 / 4096 and 200 / 4096.
All inputs are finite; a program needn't handle non-finite values.
Results may differ from a plain program's by a relative error of at most 0.0066.
Values may be sent and summed in bfloat16 or wider, within the bound.
A program may use at most 128 MiB of HBM per device.

v0:
```python
import math

import jax
import jax.numpy as jnp
from jax import lax
from jax.sharding import PartitionSpec as P

HEADS = 128
HDIM = 64
STATE = 128
GROUPS = 8


def prefix(part, axis, combine, identity, reverse):
    count = lax.axis_size(axis)
    place = lax.axis_index(axis)
    ahead = count - 1 - place if reverse else place
    gathered = jax.tree.map(lambda a: lax.all_gather(a, axis), part)
    state = jax.tree.map(lambda a, e: jnp.zeros_like(a) + jnp.asarray(e, a.dtype), part, identity)

    def one(lap, state):
        source = count - 1 - lap if reverse else lap
        return combine(
            state, jax.tree.map(lambda a: lax.dynamic_index_in_dim(a, source, 0, False), gathered)
        )

    return lax.fori_loop(0, ahead, one, state)


def broadcast(x, axis, root):
    mine = lax.axis_index(axis) == root
    return lax.psum(jnp.where(mine, x, jnp.zeros_like(x)), axis)


def extended(block, sides, width):
    for axis, dim in sides:
        count = lax.axis_size(axis)
        forward = [(i, i + 1) for i in range(count - 1)]
        backward = [(target, source) for source, target in forward]
        low = lax.ppermute(
            lax.slice_in_dim(block, block.shape[dim] - width, None, axis=dim), axis, forward
        )
        high = lax.ppermute(lax.slice_in_dim(block, 0, width, axis=dim), axis, backward)
        block = jnp.concatenate([low, block, high], axis=dim)
    return block


def ein(form, left, right):
    return jnp.einsum(form, left, right, preferred_element_type=jnp.float32)


def silu_slope(value):
    sig = jax.nn.sigmoid(value)
    return sig * (1.0 + value * (1.0 - sig))


def block_parts(activated, dt_rows, a_log, dt_bias, groups):
    length = activated.shape[0]
    heads = dt_rows.shape[1]
    inner = heads * HDIM
    shared = groups * STATE
    ratio = heads // groups
    signal = activated[:, :inner].reshape(length, heads, HDIM)
    input_map = activated[:, inner : inner + shared].reshape(length, groups, STATE)
    output_map = activated[:, inner + shared :].reshape(length, groups, STATE)
    input_heads = jnp.repeat(input_map, ratio, axis=1)
    output_heads = jnp.repeat(output_map, ratio, axis=1)
    step = jax.nn.softplus(dt_rows + dt_bias)
    rate = -jnp.exp(a_log)
    row_ids = lax.broadcasted_iota(jnp.int32, (length, length), 0)
    col_ids = lax.broadcasted_iota(jnp.int32, (length, length), 1)
    lower = (row_ids >= col_ids).astype(jnp.float32)
    decay_sum = jnp.dot(lower, step * rate, precision=lax.Precision.HIGHEST)
    to_end = jnp.exp(decay_sum[-1][None, :] - decay_sum)
    scaled = (signal.astype(jnp.float32) * step[:, :, None]).astype(jnp.bfloat16)
    weighted = (scaled.astype(jnp.float32) * to_end[:, :, None]).astype(jnp.bfloat16)
    local = ein("qhp,qhn->hpn", weighted, input_heads)
    return (
        signal,
        input_map,
        output_map,
        input_heads,
        output_heads,
        step,
        rate,
        lower,
        decay_sum,
        scaled,
        to_end,
        weighted,
        local,
    )


def entry_grad(parts, d_rows):
    decay_sum = parts[8]
    output_heads = parts[4]
    scaled_grad = (d_rows.astype(jnp.float32) * jnp.exp(decay_sum)[:, :, None]).astype(jnp.bfloat16)
    return (scaled_grad, ein("thp,thn->hpn", scaled_grad, output_heads))


def block_grads(parts, d_rows, scaled_grad, h_in, carried, skip_gain, dt_rows, dt_bias):
    (
        signal,
        input_map,
        output_map,
        input_heads,
        output_heads,
        step,
        rate,
        lower,
        decay_sum,
        scaled,
        to_end,
        weighted,
        local,
    ) = parts
    length = d_rows.shape[0]
    heads = d_rows.shape[1]
    groups = input_map.shape[1]
    width_state = input_map.shape[2]
    ratio = heads // groups
    grad_f = d_rows.astype(jnp.float32)
    signal_f = signal.astype(jnp.float32)
    grad_skip = jnp.sum(grad_f * signal_f, axis=(0, 2))
    h_low = h_in.astype(jnp.bfloat16)
    carried_low = carried.astype(jnp.bfloat16)
    offset = jnp.exp(decay_sum)[:, :, None] * ein("thn,hpn->thp", output_heads, h_low)
    grad_sum = jnp.sum(grad_f * offset, axis=2)
    out_heads_grad = ein("thp,hpn->thn", scaled_grad, h_low)
    grad_weighted = ein("shn,hpn->shp", input_heads, carried_low)
    in_heads_grad = ein("shp,hpn->shn", weighted, carried_low)
    back = jnp.sum(grad_weighted * scaled.astype(jnp.float32), axis=2) * to_end
    end_term = jnp.exp(decay_sum[-1]) * jnp.sum(h_in * carried, axis=(1, 2))
    last_row = (lax.broadcasted_iota(jnp.int32, (length, 1), 0) == length - 1).astype(jnp.float32)
    grad_sum = grad_sum - back + last_row * (jnp.sum(back, axis=0) + end_term)[None, :]
    spread = decay_sum.T[:, :, None] - decay_sum.T[:, None, :]
    decay = jnp.where(lower[None] > 0, jnp.exp(jnp.minimum(spread, 0.0)), 0.0)
    score = ein("tgn,sgn->gts", output_map, input_map)
    mix = jnp.repeat(score, ratio, axis=0) * decay
    grad_mix = ein("thp,shp->hts", d_rows, scaled)
    grad_scaled = grad_weighted * to_end[:, :, None] + ein(
        "hts,thp->shp", mix.astype(jnp.bfloat16), d_rows
    )
    product = grad_mix * mix
    grad_sum = grad_sum + (jnp.sum(product, axis=2) - jnp.sum(product, axis=1)).T
    grad_score = jnp.sum((grad_mix * decay).reshape(groups, ratio, length, length), axis=1).astype(
        jnp.bfloat16
    )
    grad_outmap = ein("gts,sgn->tgn", grad_score, input_map) + jnp.sum(
        out_heads_grad.reshape(length, groups, ratio, width_state), axis=2
    )
    grad_in = ein("gts,tgn->sgn", grad_score, output_map) + jnp.sum(
        in_heads_grad.reshape(length, groups, ratio, width_state), axis=2
    )
    grad_log = jnp.dot(lower.T, grad_sum, precision=lax.Precision.HIGHEST)
    descent_increment = grad_log * rate + jnp.sum(grad_scaled * signal_f, axis=2)
    grad_signal = skip_gain[None, :, None] * grad_f + grad_scaled * step[:, :, None]
    grad_dt = descent_increment * jax.nn.sigmoid(dt_rows + dt_bias)
    decay_log_gradient = jnp.sum(grad_log * step, axis=0) * rate
    grad_act = jnp.concatenate(
        [
            grad_signal.reshape(length, heads * HDIM),
            grad_in.reshape(length, groups * width_state),
            grad_outmap.reshape(length, groups * width_state),
        ],
        axis=1,
    )
    return (grad_act, grad_dt, decay_log_gradient, jnp.sum(grad_dt, axis=0), grad_skip)


def link(earlier, later):
    return (earlier[0] + later[0], jnp.exp(later[0])[:, None, None] * earlier[1] + later[1])


def link_blocks(lower_pair, upper_pair):
    zero_rate = jnp.zeros_like(lower_pair[0])
    zero_state = jnp.zeros_like(lower_pair[1])
    below = prefix(lower_pair, "ctx", link, (zero_rate, zero_state), False)
    beyond = prefix(upper_pair, "ctx", link, (zero_rate, zero_state), True)
    total = jax.tree.map(
        lambda part: broadcast(part, "ctx", lax.axis_size("ctx") - 1), link(below, lower_pair)
    )
    return jnp.stack([below[1], link(total, beyond)[1]])


def conv_back(grad_pre, wide_grad, kernel_taps, padded, at_end, length):
    rim = kernel_taps.shape[0] - 1
    after = jnp.stack(
        [jnp.where(at_end, grad_pre[1, :rim], wide_grad[3 * rim : 4 * rim]), wide_grad[0:rim]]
    )
    padded_next = jnp.concatenate([grad_pre, after], axis=1)
    grad_raw = jnp.zeros(grad_pre.shape, jnp.float32)
    for tap in range(rim + 1):
        grad_raw = (
            grad_raw
            + kernel_taps[tap][None, None, :] * padded_next[:, rim - tap : rim - tap + length]
        )
    tap_grads = jnp.stack(
        [jnp.sum(grad_pre * padded[:, tap : tap + length], axis=(0, 1)) for tap in range(rim + 1)]
    )
    return (grad_raw, tap_grads, jnp.sum(grad_pre, axis=(0, 1)))


def first_rows(grad_pre, rim):
    return jnp.concatenate([grad_pre[0, :rim], grad_pre[1, :rim]], axis=0)


def shards(
    sig_raw,
    map_raw,
    step_size_logits,
    d_out,
    sig_taps,
    map_taps,
    sig_bias,
    map_bias,
    a_log,
    dt_bias,
    skip_gain,
):
    all_map_taps, all_map_bias = (
        lax.all_gather(map_taps, "fsdp", axis=1, tiled=True),
        lax.all_gather(map_bias, "fsdp", axis=0, tiled=True),
    )
    kernel_taps = jnp.concatenate([sig_taps, all_map_taps], axis=1)
    kernel_bias = jnp.concatenate([sig_bias, all_map_bias], axis=0)
    kernel = kernel_taps.shape[0]
    rim = kernel - 1
    length = sig_raw.shape[0] // 2
    sig_width = sig_raw.shape[1]
    map_width = map_raw.shape[1]
    width = sig_width + map_width
    heads_here = step_size_logits.shape[1]
    ratio = HEADS // GROUPS
    group_count = max(1, heads_here // ratio)
    first_group = lax.axis_index("fsdp") * heads_here // ratio
    fsdp_count = lax.axis_size("fsdp")
    owned = map_width // fsdp_count
    map_start = lax.axis_index("fsdp") * owned
    raw_rows = jnp.concatenate([sig_raw, map_raw], axis=1).reshape(2, length, width)
    tails = jnp.concatenate([raw_rows[1, length - rim :], raw_rows[0, length - rim :]], axis=0)
    wide = extended(tails, (("ctx", 0),), rim)
    at_end = lax.axis_index("ctx") == lax.axis_size("ctx") - 1
    before = jnp.stack(
        [wide[0:rim], jnp.where(at_end, raw_rows[0, length - rim :], wide[3 * rim : 4 * rim])]
    )
    padded = jnp.concatenate([before, raw_rows], axis=1).astype(jnp.float32)
    preact = kernel_bias[None, None, :] + jnp.zeros((2, length, width), jnp.float32)
    for tap in range(kernel):
        preact = preact + kernel_taps[tap][None, None, :] * padded[:, tap : tap + length]
    activated = jax.nn.silu(preact).astype(jnp.bfloat16)
    maps_all = activated[:, :, sig_width:].reshape(2, length, 2, GROUPS, STATE)
    maps_mine = lax.dynamic_slice_in_dim(maps_all, first_group, group_count, 3)
    local_act = jnp.concatenate(
        [activated[:, :, :sig_width], maps_mine.reshape(2, length, 2 * group_count * STATE)], axis=2
    )
    dt_rows = step_size_logits.reshape(2, length, heads_here)
    grad_rows = d_out.reshape(2, length, heads_here, HDIM)

    def parts_of(act_block, dt_block):
        return block_parts(act_block, dt_block, a_log, dt_bias, group_count)

    parts = jax.vmap(parts_of)(local_act, dt_rows)
    scaled_grad, state_grad = jax.vmap(entry_grad)(parts, grad_rows)
    ends = parts[8][:, -1]
    h_ins = link_blocks((ends[0], parts[12][0]), (ends[1], parts[12][1]))
    carried_pair = link_blocks((ends[1], state_grad[1]), (ends[0], state_grad[0]))
    carried = jnp.stack([carried_pair[1], carried_pair[0]])
    grad_act, grad_dt, decay_log_gradient, grad_dtb, grad_skip = jax.vmap(
        block_grads, in_axes=(0, 0, 0, 0, 0, None, 0, None)
    )(parts, grad_rows, scaled_grad, h_ins, carried, skip_gain, dt_rows, dt_bias)
    slope = silu_slope(preact)
    grad_pre_sig = grad_act[:, :, :sig_width] * slope[:, :, :sig_width]
    grad_mine = grad_act[:, :, sig_width:].reshape(2, length, 2, group_count, STATE)
    zero_index = jnp.zeros((), jnp.int32)
    placed = lax.dynamic_update_slice(
        jnp.zeros((2, length, 2, GROUPS, STATE), jnp.float32),
        grad_mine,
        (zero_index, zero_index, zero_index, first_group, zero_index),
    )
    map_term = placed.reshape(2, length, map_width)
    map_owned = lax.psum_scatter(map_term, "fsdp", scatter_dimension=2, tiled=True)
    map_slope = lax.dynamic_slice_in_dim(slope[:, :, sig_width:], map_start, owned, 2)
    grad_pre = jnp.concatenate([grad_pre_sig, map_owned * map_slope], axis=2)
    own_taps = jnp.concatenate([sig_taps, map_taps], axis=1)
    own_padded = jnp.concatenate(
        [
            padded[:, :, :sig_width],
            lax.dynamic_slice_in_dim(padded[:, :, sig_width:], map_start, owned, 2),
        ],
        axis=2,
    )
    wide_grad = extended(first_rows(grad_pre, rim), (("ctx", 0),), rim)
    grad_raw, tap_grads, bias_grads = conv_back(
        grad_pre, wide_grad, own_taps, own_padded, at_end, length
    )
    map_raw_grad = grad_raw[:, :, sig_width:]
    map_tap_grad = tap_grads[:, sig_width:]
    map_bias_grad = bias_grads[sig_width:]
    sig_raw_grad = grad_raw[:, :, :sig_width]
    sig_tap_grad = tap_grads[:, :sig_width]
    sig_bias_grad = bias_grads[:sig_width]
    reduced = lax.psum(
        (
            sig_tap_grad,
            map_tap_grad,
            sig_bias_grad,
            map_bias_grad,
            jnp.sum(decay_log_gradient, axis=0),
            jnp.sum(grad_dtb, axis=0),
            jnp.sum(grad_skip, axis=0),
        ),
        "ctx",
    )
    scale = 1.0 / math.sqrt(float(lax.axis_size("ctx") * 2 * length))
    final = jax.tree.map(lambda grad_part: grad_part * scale, reduced)
    return (
        sig_raw_grad.reshape(2 * length, sig_width),
        map_raw_grad.reshape(2 * length, owned),
        grad_dt.reshape(2 * length, heads_here),
        final[0],
        final[1],
        final[2],
        final[3],
        final[4],
        final[5],
        final[6],
    )


def solution(mesh):
    return jax.shard_map(
        shards,
        mesh=mesh,
        in_specs=(
            P("ctx", "fsdp"),
            P("ctx", None),
            P("ctx", "fsdp"),
            P("ctx", "fsdp"),
            P(None, "fsdp"),
            P(None, "fsdp"),
            P("fsdp"),
            P("fsdp"),
            P("fsdp"),
            P("fsdp"),
            P("fsdp"),
        ),
        out_specs=(
            P("ctx", "fsdp"),
            P("ctx", "fsdp"),
            P("ctx", "fsdp"),
            P(None, "fsdp"),
            P(None, "fsdp"),
            P("fsdp"),
            P("fsdp"),
            P("fsdp"),
            P("fsdp"),
            P("fsdp"),
        ),
        check_vma=False,
    )
```

profile of v0, /device:TPU:10, one launch (start us, length us, event | category | flops | bytes accessed | tf_op | source)
XLA Modules:
  0.0 1140.2 jit_solution(17790287372586400187)
XLA Ops:
  7.3 1.1 pad_maximum_fusion
  8.4 11.3 collective-permute-start.1
  19.7 1.9 collective-permute-start
  23.5 19.5 %all_gather.28 = f32[4,2048]{1,0:T(4,128)S(1)} all-gather(f32[4,128]{1,0:T(4,128)S(1)} %copy-done.35), channel_id=1, replica_groups=mesh['ctx'=32,'fsdp'=16] {'fsdp'}, dimensions={1}, use_global_device_ids=true | all-gather | bytes 34816 | tf_op jit(solution)/shard_map/all_gather | solution.py:223
  43.1 23.6 %all-gather.2 = f32[16,1,128]{2,1,0:T(1,128)S(1)} all-gather(f32[1,1,128]{2,1,0:T(1,128)S(1)} %bitcast.192), channel_id=1, replica_groups=mesh['ctx'=32,'fsdp'=16] {'fsdp'}, dimensions={0}, use_global_device_ids=true | all-gather | bytes 8704 | tf_op jit(solution)/shard_map/all_gather | solution.py:224
  67.0 2.0 add_multiply_fusion
  72.9 1.1 fusion.47
  77.3 64.7 %all-gather.1 = f32[32,1,8]{2,1,0:T(1,128)} all-gather(f32[1,1,8]{2,1,0:T(1,128)S(1)} %copy.105), channel_id=3, replica_groups=mesh['ctx'=32,'fsdp'=16] {'ctx'}, dimensions={0}, use_global_device_ids=true | all-gather | bytes 1056 | tf_op jit(solution)/shard_map/all_gather | solution.py:18
  142.0 61.2 %all-gather = f32[32,1,8]{2,1,0:T(1,128)} all-gather(f32[1,1,8]{2,1,0:T(1,128)S(1)} %copy.101), channel_id=2, replica_groups=mesh['ctx'=32,'fsdp'=16] {'ctx'}, dimensions={0}, use_global_device_ids=true | all-gather | bytes 1056 | tf_op jit(solution)/shard_map/all_gather | solution.py:18
  204.4 1.1 fusion.21
  206.3 9.2 all-gather.12.cloned.1.call-done
  215.5 28.4 %while.54 = (s32[]{:T(128)}, f32[8,64,128]{2,1,0:T(8,128)S(1)}, s32[]{:T(128)}, f32[32,8]{1,0:T(8,128)}, f32[32,8,64,128]{3,2,1,0:T(8,128)}, /*index=5*/s32[]{:T(128)}, s32[]{:T(128)}, s32[]{:T(128)}) while((s32[]{:T(128)}, f32[8,64,128]{2,1,0:T(8,128)S(1)}, s32[]{:T(128)}, f32[32,8]{1,0:T(8,128)}, f32[32,8,64,128]{3,2,1,0:T(8,128)}, ...), condition=%wide.region_7.8_spmd, body=%wide.region_6.7_spmd.sunk | while | flops 131077 | bytes 786663 | solution.py:27
  216.2 1.1 bitcast_add_fusion.16
  218.0 1.1 bitcast_add_fusion.16
  221.6 1.1 bitcast_add_fusion.16
  223.3 1.1 bitcast_add_fusion.16
  226.9 1.1 bitcast_add_fusion.16
  228.6 1.1 bitcast_add_fusion.16
  230.4 1.1 bitcast_add_fusion.16
  234.0 1.1 bitcast_add_fusion.16
  235.8 1.1 bitcast_add_fusion.16
  237.5 1.1 bitcast_add_fusion.16
  242.9 1.1 bitcast_add_fusion.16
  244.8 115.0 %all-gather.10.cloned.1.call-done = f32[32,8,64,128]{3,2,1,0:T(8,128)} async-done(((f32[1,8,64,128]{3,2,1,0:T(8,128)}), f32[32,8,64,128]{3,2,1,0:T(8,128)}) %all-gather.10.cloned.1.call-update) | async-done | bytes 8388624 | tf_op jit(solution)/shard_map/all_gather | solution.py:18
  359.8 28.3 %while.53 = (s32[]{:T(128)}, f32[8,64,128]{2,1,0:T(8,128)S(1)}, s32[]{:T(128)}, f32[32,8]{1,0:T(8,128)}, f32[32,8,64,128]{3,2,1,0:T(8,128)}, /*index=5*/s32[]{:T(128)}, s32[]{:T(128)}, s32[]{:T(128)}) while((s32[]{:T(128)}, f32[8,64,128]{2,1,0:T(8,128)S(1)}, s32[]{:T(128)}, f32[32,8]{1,0:T(8,128)}, f32[32,8,64,128]{3,2,1,0:T(8,128)}, ...), condition=%wide.region_3.4_spmd, body=%wide.region_2.3_spmd.sunk | while | flops 131077 | bytes 786663 | solution.py:27
  383.5 1.1 bitcast_add_fusion.15
  385.3 1.1 bitcast_add_fusion.15
  387.0 1.1 bitcast_add_fusion.15
  388.9 115.5 %all-gather.14.cloned.1.call-done = f32[32,8,64,128]{3,2,1,0:T(8,128)} async-done(((f32[1,8,64,128]{3,2,1,0:T(8,128)}), f32[32,8,64,128]{3,2,1,0:T(8,128)}) %all-gather.14.cloned.1.call-update) | async-done | bytes 8388624 | tf_op jit(solution)/shard_map/all_gather | solution.py:18
  504.5 26.7 %while.55 = (s32[]{:T(128)}, f32[8]{0:T(128)S(1)}, f32[8,64,128]{2,1,0:T(8,128)S(1)}, s32[]{:T(128)}, f32[32,8]{1,0:T(8,128)}, /*index=5*/f32[32,8,64,128]{3,2,1...) while((s32[]{:T(128)}, f32[8]{0:T(128)S(1)}, f32[8,64,128]{2,1,0:T(8,128)S(1)}, s32[]{:T(128)}, ...), condition=%wide.region_9.10_spmd, body=%wide.region_8.9_spmd.sunk | while | flops 131086 | bytes 786755 | solution.py:27
  515.8 1.1 bitcast_add_fusion.17
  523.0 1.1 bitcast_add_fusion.17
  531.2 117.5 %all-gather.8.cloned.1.call-done = f32[32,8,64,128]{3,2,1,0:T(8,128)} async-done(((f32[1,8,64,128]{3,2,1,0:T(8,128)}), f32[32,8,64,128]{3,2,1,0:T(8,128)}) %all-gather.8.cloned.1.call-update) | async-done | bytes 8388624 | tf_op jit(solution)/shard_map/all_gather | solution.py:18
  648.8 26.7 %while.52 = (s32[]{:T(128)}, f32[8]{0:T(128)S(1)}, f32[8,64,128]{2,1,0:T(8,128)S(1)}, s32[]{:T(128)}, f32[32,8]{1,0:T(8,128)}, /*index=5*/f32[32,8,64,128]{3,2,1...) while((s32[]{:T(128)}, f32[8]{0:T(128)S(1)}, f32[8,64,128]{2,1,0:T(8,128)S(1)}, s32[]{:T(128)}, ...), condition=%wide.region_1.2_spmd, body=%wide.region_0.1_spmd.sunk | while | flops 131086 | bytes 786755 | solution.py:27
  675.5 226.0 %all-reduce.4.cloned.1.call-done = (f32[8,64,128]{2,1,0:T(8,128)}, f32[8,64,128]{2,1,0:T(8,128)}) async-done(((f32[8,64,128]{2,1,0:T(8,128)}, f32[8,64,128]{2,1,0:T(8,128)}), (f32[8,64,128]{2,1,0:T(8,128)}, f32[8,64,128]{2,1,0:T(8,128)})) %all-reduce.4.cloned.1.call-update) | async-done | bytes 524304 | tf_op jit(solution)/shard_map/psum | solution.py:32
  901.5 1.2 add_bitcast_fusion
  903.7 2.8 dynamic_update_slice.3
  906.5 1.1 reshape.195
  908.8 1.3 copy-done.1
  910.1 1.1 slice.218
  911.5 1.3 fusion.13
  912.9 2.3 multiply_reduce_fusion
  915.2 1.3 copy.112
  917.5 72.8 %reduce-scatter.2.cloned.1.call-done = f32[2,64,128]{2,1,0:T(8,128)} async-done(((f32[2,64,2048]{2,1,0:T(8,128)}), f32[2,64,128]{2,1,0:T(8,128)}) %reduce-scatter.2.cloned.1.call-update) | async-done | bytes 65552 | tf_op jit(solution)/shard_map/reduce_scatter | solution.py:283
  991.1 6.8 collective-permute-start.2
  999.3 1.9 collective-permute-start.3
  1002.0 5.3 collective-permute-done.3
  1009.2 120.4 %all-reduce = (f32[4,512]{1,0:T(4,128)S(1)}, f32[4,128]{1,0:T(4,128)S(1)}, f32[512]{0:T(512)S(1)}, f32[128]{0:T(128)S(1)}, f32[8]{0:T(128)S(1)}, /*index=5*/f32[8]{0:T(128)S(1)}, f32[8]{0:T(128)S(1)}) all-reduce(f32[4,512]{1,0:T(4,128)S(1)} %slice.240, ...), channel_id=1, replica_groups=mesh['ctx'=32,'fsdp'=16] {'ctx'}, use_global_device_ids=true, to_apply=%region_23.24 | all-reduce | flops 3224 | bytes 25792 | tf_op jit(solution)/shard_map/psum | solution.py:304
  (324 shorter events, 116.3 us)
Async XLA Ops:
  7.2 14.5 %copy-start.39 = (f32[128,8]{0,1:T(8,128)S(1)}, f32[128,8]{0,1:T(8,128)}, u32[]{:S(2)}) copy-start(f32[128,8]{0,1:T(8,128)} %param.21) | copy-start | bytes 12292
  7.2 14.6 %copy-start.48 = (f32[8]{0:T(128)S(1)}, f32[8]{0:T(128)}, u32[]{:S(2)}) copy-start(f32[8]{0:T(128)} %param.27) | copy-start | bytes 100
  7.2 14.6 %copy-start.44 = (f32[8]{0:T(128)S(1)}, f32[8]{0:T(128)}, u32[]{:S(2)}) copy-start(f32[8]{0:T(128)} %param.28) | copy-start | bytes 100
  7.2 15.7 %copy-start.34 = (f32[4,512]{1,0:T(4,128)S(1)}, f32[4,512]{1,0:T(4,128)}, u32[]{:S(2)}) copy-start(f32[4,512]{1,0:T(4,128)} %param.23) | copy-start | bytes 24580
  7.2 16.3 %copy-start.35 = (f32[4,128]{1,0:T(4,128)S(1)}, f32[4,128]{1,0:T(4,128)}, u32[]{:S(2)}) copy-start(f32[4,128]{1,0:T(4,128)} %param.24) | copy-start | bytes 6148
  7.2 35.9 %copy-start.43 = (f32[128]{0:T(128)S(1)}, f32[128]{0:T(128)}, u32[]{:S(2)}) copy-start(f32[128]{0:T(128)} %param.26) | copy-start | bytes 1540
  7.2 59.5 %copy-start.42 = (f32[512]{0:T(512)S(1)}, f32[512]{0:T(512)}, u32[]{:S(2)}) copy-start(f32[512]{0:T(512)} %param.25) | copy-start | bytes 6148
  7.3 208.2 %all-gather.12.cloned.1.call-start = ((), (), s32[]{:S(2)}) async-start(), calls=%async_computation.3 | async-start | bytes 8650752 | tf_op jit(solution)/shard_map/all_gather | solution.py:18
  8.4 58.3 %collective-permute-start.1 = (bf16[3,2560]{1,0:T(4,128)(2,1)S(1)}, bf16[3,2560]{1,0:T(4,128)(2,1)S(1)}, u32[]{:S(2)}, u32[]{:S(2)}) collective-permute-start(bf16[3,2560]{1,0:T(4,128)(2,1)S(1)} %get-tuple-element.414), channel_id=1, source_target_pairs={{16,0},{32,16},{48,32},{64,48},{80,64},{96,80},{112,96},{128,112},... | collective-permute-start | bytes 46088 | tf_op jit(solution)/shard_map/ppermute | solution.py:43
  19.7 47.0 %collective-permute-start = (bf16[3,2560]{1,0:T(4,128)(2,1)S(1)}, bf16[3,2560]{1,0:T(4,128)(2,1)S(1)}, u32[]{:S(2)}, u32[]{:S(2)}) collective-permute-start(bf16[3,2560]{1,0:T(4,128)(2,1)S(1)} %get-tuple-element.413), channel_id=1, source_target_pairs={{0,16},{16,32},{32,48},{48,64},{64,80},{80,96},{96,112},{112,128},... | collective-permute-start | bytes 46088 | tf_op jit(solution)/shard_map/ppermute | solution.py:40
  21.8 45.2 %copy-start.46 = (f32[8]{0:T(128)}, f32[8]{0:T(128)S(1)}, u32[]{:S(2)}) copy-start(f32[8]{0:T(128)S(1)} %exponential_negate_fusion) | copy-start | bytes 100
  21.9 47.8 %copy-start.25 = (f32[2,64,8]{1,2,0:T(8,128)}, f32[2,64,8]{1,2,0:T(8,128)S(1)}, u32[]{:S(2)}) copy-start(f32[2,64,8]{1,2,0:T(8,128)S(1)} %compare_select_fusion) | copy-start | bytes 12292
  67.0 841.8 %copy-start = (f32[2,67,2560]{2,1,0:T(8,128)}, f32[2,67,2560]{2,1,0:T(8,128)S(1)}, u32[]{:S(2)}) copy-start(f32[2,67,2560]{2,1,0:T(8,128)S(1)} %maximum_convert_fusion) | copy-start | bytes 4116484
  70.1 833.1 %copy-start.2 = (bf16[2,64,8,64]{1,3,2,0:T(8,128)(2,1)}, bf16[2,64,8,64]{1,3,2,0:T(8,128)(2,1)S(1)}, u32[]{:S(2)}) copy-start(bf16[2,64,8,64]{1,3,2,0:T(8,128)(2,1)S(1)} %multiply_convert_fusion.1) | copy-start | bytes 393220
  70.2 2.3 copy-start.15
  72.4 287.3 %all-gather.10.cloned.1.call-start = ((), (), s32[]{:S(2)}) async-start(), calls=%async_computation.2 | async-start | bytes 8650752 | tf_op jit(solution)/shard_map/all_gather | solution.py:18
  72.9 131.5 %copy-start.6 = (bf16[2,64,8,64]{1,3,2,0:T(8,128)(2,1)}, bf16[2,64,8,64]{1,3,2,0:T(8,128)(2,1)S(1)}, u32[]{:S(2)}) copy-start(bf16[2,64,8,64]{1,3,2,0:T(8,128)(2,1)S(1)} %copy.99) | copy-start | bytes 393220
  72.9 130.2 %copy-start.36 = (f32[4,128]{1,0:T(4,128)S(1)}, f32[4,128]{1,0:T(4,128)}, u32[]{:S(2)}) copy-start(f32[4,128]{1,0:T(4,128)} %param.24) | copy-start | bytes 6148
  74.9 429.5 %all-gather.14.cloned.1.call-start = ((), (), s32[]{:S(2)}) async-start(), calls=%async_computation.4 | async-start | bytes 8650752 | tf_op jit(solution)/shard_map/all_gather | solution.py:18
  75.6 573.1 %all-gather.8.cloned.1.call-start = ((), (), s32[]{:S(2)}) async-start(), calls=%async_computation.1 | async-start | bytes 8650752 | tf_op jit(solution)/shard_map/all_gather | solution.py:18
  76.2 825.3 %all-reduce.4.cloned.1.call-start = ((), (), s32[]{:S(2)}) async-start(), calls=%async_computation.6 | async-start | bytes 1048576 | tf_op jit(solution)/shard_map/psum | solution.py:32
  77.3 138.2 %copy-start.37 = (pred[64,64]{0,1:T(8,128)(4,1)}, pred[64,64]{0,1:T(8,128)(4,1)S(1)}, u32[]{:S(2)}) copy-start(pred[64,64]{0,1:T(8,128)(4,1)S(1)} %copy.109) | copy-start | bytes 12292
  204.4 11.1 copy-start.22
  205.5 9.9 copy-start.18
  215.5 28.4 %copy-start.41 = (f32[8]{0:T(128)S(1)}, f32[8]{0:T(128)}, u32[]{:S(2)}) copy-start(f32[8]{0:T(128)} %get-tuple-element.349) | copy-start | bytes 100
  359.8 28.3 %copy-start.40 = (f32[8]{0:T(128)S(1)}, f32[8]{0:T(128)}, u32[]{:S(2)}) copy-start(f32[8]{0:T(128)} %get-tuple-element.348) | copy-start | bytes 100
  531.2 459.0 %reduce-scatter.2.cloned.1.call-start = ((), (), s32[]{:S(2)}) async-start(), calls=%async_computation.5 | async-start | bytes 1114112 | tf_op jit(solution)/shard_map/reduce_scatter | solution.py:283
  675.4 227.3 %copy-start.7 = (bf16[2,64,8,64]{1,3,2,0:T(8,128)(2,1)S(1)}, bf16[2,64,8,64]{1,3,2,0:T(8,128)(2,1)}, u32[]{:S(2)}) copy-start(bf16[2,64,8,64]{1,3,2,0:T(8,128)(2,1)} %copy-done.6) | copy-start | bytes 393220
  675.5 227.3 %copy-start.20 = (f32[2,64,8]{1,2,0:T(8,128)S(1)}, f32[2,64,8]{1,2,0:T(8,128)}, u32[]{:S(2)}) copy-start(f32[2,64,8]{1,2,0:T(8,128)} %get-tuple-element.430) | copy-start | bytes 12292
  675.5 227.5 %copy-start.19 = (bf16[2,64,64]{1,2,0:T(8,128)(2,1)S(1)}, bf16[2,64,64]{1,2,0:T(8,128)(2,1)}, u32[]{:S(2)}) copy-start(bf16[2,64,64]{1,2,0:T(8,128)(2,1)} %copy-done.18) | copy-start | bytes 49156
  908.8 2.4 copy-start.10
  908.8 2.7 slice-start.1
  912.9 3.8 copy-start.5
  912.9 3.7 copy-start.12
  916.8 81.2 %copy-start.27 = (f32[64,64]{1,0:T(8,128)S(1)}, f32[64,64]{1,0:T(8,128)}, u32[]{:S(2)}) copy-start(f32[64,64]{1,0:T(8,128)} %fusion.61) | copy-start | bytes 49156
  916.8 81.2 %copy-start.29 = (f32[2,64,8]{1,0,2:T(2,128)S(1)}, f32[2,64,8]{1,0,2:T(2,128)}, u32[]{:S(2)}) copy-start(f32[2,64,8]{1,0,2:T(2,128)} %copy-done.28) | copy-start | bytes 12292
  916.8 81.2 %copy-start.45 = (f32[8]{0:T(128)S(1)}, f32[8]{0:T(128)}, u32[]{:S(2)}) copy-start(f32[8]{0:T(128)} %param.28) | copy-start | bytes 100
  916.8 81.2 %copy-start.47 = (f32[8]{0:T(128)S(1)}, f32[8]{0:T(128)}, u32[]{:S(2)}) copy-start(f32[8]{0:T(128)} %copy-done.46) | copy-start | bytes 100
  916.8 81.2 %copy-start.50 = (f32[64]{0:T(128)S(1)}, f32[64]{0:T(128)}, u32[]{:S(2)}) copy-start(f32[64]{0:T(128)} %compare_convert_fusion) | copy-start | bytes 772
  916.8 81.2 %copy-start.51 = (f32[2,8,64]{2,1,0:T(8,128)S(1)}, f32[2,8,64]{2,1,0:T(8,128)}, u32[]{:S(2)}) copy-start(f32[2,8,64]{2,1,0:T(8,128)} %get-tuple-element.336) | copy-start | bytes 12292
  916.8 81.2 %copy-start.52 = (f32[2,8,64]{2,1,0:T(8,128)S(1)}, f32[2,8,64]{2,1,0:T(8,128)}, u32[]{:S(2)}) copy-start(f32[2,8,64]{2,1,0:T(8,128)} %get-tuple-element.337) | copy-start | bytes 12292
  917.4 89.9 %slice-start = ((f32[2,67,2560]{2,1,0:T(8,128)}), f32[2,67,512]{2,1,0:T(8,128)S(1)}, s32[]{:S(2)}) async-start(f32[2,67,2560]{2,1,0:T(8,128)} %copy-done), calls=%async_computation.7 | async-start | bytes 589824 | tf_op jit(solution)/shard_map/slice | solution.py:289
  917.4 89.9 %copy-start.30 = (f32[640]{0:T(1024)S(1)}, f32[640]{0:T(1024)}, u32[]{:S(2)}) copy-start(f32[640]{0:T(1024)} %get-tuple-element.344) | copy-start | bytes 7684
  917.4 89.9 %copy-start.31 = (f32[640]{0:T(1024)S(1)}, f32[640]{0:T(1024)}, u32[]{:S(2)}) copy-start(f32[640]{0:T(1024)} %get-tuple-element.345) | copy-start | bytes 7684
  917.4 89.9 %copy-start.32 = (f32[640]{0:T(1024)S(1)}, f32[640]{0:T(1024)}, u32[]{:S(2)}) copy-start(f32[640]{0:T(1024)} %get-tuple-element.346) | copy-start | bytes 7684
  917.4 89.9 %copy-start.33 = (f32[640]{0:T(1024)S(1)}, f32[640]{0:T(1024)}, u32[]{:S(2)}) copy-start(f32[640]{0:T(1024)} %get-tuple-element.347) | copy-start | bytes 7684
  991.1 8.2 collective-permute-start.2
  999.3 7.9 collective-permute-start.3
  (17 other events, 25.2 us)
Sparse Core Ops, SparseCore 0:
  72.6 142.8 all-gather.11
  217.6 142.1 all-gather.9
  361.9 142.5 all-gather.13
  506.4 142.3 all-gather.7
  651.5 249.9 all-reduce.3
  907.8 82.4 reduce-scatter.1
where the time goes:
time: 1140 us
  waiting for transfers between devices  664 us (58%)
  blocking collectives  289 us (25%)
  other arithmetic  101 us (9%)
  local copies, waits for them, and re-layouts  39.5 us (3%)
  starting transfers between devices  22.2 us (2%)
  between operations  15.1 us (1%)
    all_gather x4, waiting for transfers between devices, prefix(): gathered = jax.tree.map(lambda a: lax.all_gather(a, axis), part)  357 us
    psum x1, waiting for transfers between devices, broadcast(): return lax.psum(jnp.where(mine, x, jnp.zeros_like(x)), axis)  226 us
    all_gather x2, blocking collectives, prefix(): gathered = jax.tree.map(lambda a: lax.all_gather(a, axis), part)  126 us
    psum x1, blocking collectives, shards(): lax.psum((sig_tap_grad, map_tap_grad, sig_bias_grad, map_bias_grad, jnp.s...  120 us
    reduce_scatter x1, waiting for transfers between devices, shards(): lax.psum_scatter(map_term, 'fsdp', scatter_dimension=2, tiled=True)  72.8 us
    add x62, other arithmetic, link(): jnp.exp(later[0])[:, None, None] * earlier[1] + later[1]  65.5 us
    all_gather x1, blocking collectives, shards(): lax.all_gather(map_bias, 'fsdp', axis=0, tiled=True)  23.6 us
  transfers between devices with their start and end apart: 10, of which 8 were waited for; matrix products, arithmetic and copies ran while one was open for 11% of the time, Pallas kernels for 0%

commit v1 on v0

v1 whole, which is shorter than its diff:
```python
import functools
import math

import jax
import jax.numpy as jnp
from jax import lax
from jax.experimental import pallas as pl
from jax.experimental.pallas import tpu as pltpu
from jax.sharding import PartitionSpec as P

HEADS = 128
HDIM = 64
STATE = 128
GROUPS = 8
MESH = pl.DeviceIdType.MESH
VM = pl.BlockSpec(memory_space=pltpu.VMEM)


def ein(form, left, right):
    return jnp.einsum(form, left, right, preferred_element_type=jnp.float32)


def silu_slope(value):
    sig = jax.nn.sigmoid(value)
    return sig * (1.0 + value * (1.0 - sig))


def block_parts(activated, dt_rows, a_log, dt_bias, groups):
    length = activated.shape[0]
    heads = dt_rows.shape[1]
    inner = heads * HDIM
    shared = groups * STATE
    ratio = heads // groups
    signal = activated[:, :inner].reshape(length, heads, HDIM)
    input_map = activated[:, inner : inner + shared].reshape(length, groups, STATE)
    output_map = activated[:, inner + shared :].reshape(length, groups, STATE)
    input_heads = jnp.repeat(input_map, ratio, axis=1)
    output_heads = jnp.repeat(output_map, ratio, axis=1)
    step = jax.nn.softplus(dt_rows + dt_bias)
    rate = -jnp.exp(a_log)
    row_ids = lax.broadcasted_iota(jnp.int32, (length, length), 0)
    col_ids = lax.broadcasted_iota(jnp.int32, (length, length), 1)
    lower = (row_ids >= col_ids).astype(jnp.float32)
    decay_sum = jnp.dot(lower, step * rate, precision=lax.Precision.HIGHEST)
    to_end = jnp.exp(decay_sum[-1][None, :] - decay_sum)
    scaled = (signal.astype(jnp.float32) * step[:, :, None]).astype(jnp.bfloat16)
    weighted = (scaled.astype(jnp.float32) * to_end[:, :, None]).astype(jnp.bfloat16)
    local = ein("qhp,qhn->hpn", weighted, input_heads)
    return (
        signal,
        input_map,
        output_map,
        input_heads,
        output_heads,
        step,
        rate,
        lower,
        decay_sum,
        scaled,
        to_end,
        weighted,
        local,
    )


def entry_grad(parts, d_rows):
    decay_sum = parts[8]
    output_heads = parts[4]
    scaled_grad = (d_rows.astype(jnp.float32) * jnp.exp(decay_sum)[:, :, None]).astype(jnp.bfloat16)
    return (scaled_grad, ein("thp,thn->hpn", scaled_grad, output_heads))


def block_grads(parts, d_rows, scaled_grad, h_in, carried, skip_gain, dt_rows, dt_bias):
    (
        signal,
        input_map,
        output_map,
        input_heads,
        output_heads,
        step,
        rate,
        lower,
        decay_sum,
        scaled,
        to_end,
        weighted,
        local,
    ) = parts
    length = d_rows.shape[0]
    heads = d_rows.shape[1]
    groups = input_map.shape[1]
    width_state = input_map.shape[2]
    ratio = heads // groups
    grad_f = d_rows.astype(jnp.float32)
    signal_f = signal.astype(jnp.float32)
    grad_skip = jnp.sum(grad_f * signal_f, axis=(0, 2))
    h_low = h_in.astype(jnp.bfloat16)
    carried_low = carried.astype(jnp.bfloat16)
    offset = jnp.exp(decay_sum)[:, :, None] * ein("thn,hpn->thp", output_heads, h_low)
    grad_sum = jnp.sum(grad_f * offset, axis=2)
    out_heads_grad = ein("thp,hpn->thn", scaled_grad, h_low)
    grad_weighted = ein("shn,hpn->shp", input_heads, carried_low)
    in_heads_grad = ein("shp,hpn->shn", weighted, carried_low)
    back = jnp.sum(grad_weighted * scaled.astype(jnp.float32), axis=2) * to_end
    end_term = jnp.exp(decay_sum[-1]) * jnp.sum(h_in * carried, axis=(1, 2))
    last_row = (lax.broadcasted_iota(jnp.int32, (length, 1), 0) == length - 1).astype(jnp.float32)
    grad_sum = grad_sum - back + last_row * (jnp.sum(back, axis=0) + end_term)[None, :]
    spread = decay_sum.T[:, :, None] - decay_sum.T[:, None, :]
    decay = jnp.where(lower[None] > 0, jnp.exp(jnp.minimum(spread, 0.0)), 0.0)
    score = ein("tgn,sgn->gts", output_map, input_map)
    mix = jnp.repeat(score, ratio, axis=0) * decay
    grad_mix = ein("thp,shp->hts", d_rows, scaled)
    grad_scaled = grad_weighted * to_end[:, :, None] + ein(
        "hts,thp->shp", mix.astype(jnp.bfloat16), d_rows
    )
    product = grad_mix * mix
    grad_sum = grad_sum + (jnp.sum(product, axis=2) - jnp.sum(product, axis=1)).T
    grad_score = jnp.sum((grad_mix * decay).reshape(groups, ratio, length, length), axis=1).astype(
        jnp.bfloat16
    )
    grad_outmap = ein("gts,sgn->tgn", grad_score, input_map) + jnp.sum(
        out_heads_grad.reshape(length, groups, ratio, width_state), axis=2
    )
    grad_in = ein("gts,tgn->sgn", grad_score, output_map) + jnp.sum(
        in_heads_grad.reshape(length, groups, ratio, width_state), axis=2
    )
    grad_log = jnp.dot(lower.T, grad_sum, precision=lax.Precision.HIGHEST)
    descent_increment = grad_log * rate + jnp.sum(grad_scaled * signal_f, axis=2)
    grad_signal = skip_gain[None, :, None] * grad_f + grad_scaled * step[:, :, None]
    grad_dt = descent_increment * jax.nn.sigmoid(dt_rows + dt_bias)
    decay_log_gradient = jnp.sum(grad_log * step, axis=0) * rate
    grad_act = jnp.concatenate(
        [
            grad_signal.reshape(length, heads * HDIM),
            grad_in.reshape(length, groups * width_state),
            grad_outmap.reshape(length, groups * width_state),
        ],
        axis=1,
    )
    return (grad_act, grad_dt, decay_log_gradient, jnp.sum(grad_dt, axis=0), grad_skip)


def signal(sem, **where):
    pl.semaphore_signal(sem, inc=1, device_id=where, device_id_type=MESH)


def remote(src, dst, send_sem, recv_sem, **where):
    return pltpu.make_async_remote_copy(
        src_ref=src,
        dst_ref=dst,
        send_sem=send_sem,
        recv_sem=recv_sem,
        device_id=where,
        device_id_type=MESH,
    )


def entry_kernel(
    n_ctx, half, tail_ref, taps_ref, halo_ref, got_ref, halo_send, halo_recv, tap_send, tap_recv
):
    c = lax.axis_index("ctx")
    f = lax.axis_index("fsdp")
    up, down = lax.rem(c + 1, n_ctx), lax.rem(c + n_ctx - 1, n_ctx)
    slot = f // half
    first = 2 * (f - slot * half)
    group = f // 2
    barrier = pltpu.get_barrier_semaphore()
    signal(barrier, ctx=up)
    signal(barrier, ctx=down)
    for k in range(2):
        source = group + k * half

        @pl.when(source != f)
        def _():
            signal(barrier, fsdp=source)

    selves = jnp.where(first == f, 1, 0) + jnp.where(first + 1 == f, 1, 0)
    pl.semaphore_wait(barrier, 4 - selves)
    to_up = remote(tail_ref.at[0], halo_ref.at[0], halo_send.at[0], halo_recv.at[0], ctx=up)
    to_down = remote(tail_ref.at[1], halo_ref.at[1], halo_send.at[1], halo_recv.at[1], ctx=down)
    to_up.start()
    to_down.start()
    for k in range(2):

        @pl.when(first + k != f)
        def _():
            remote(
                taps_ref, got_ref.at[slot], tap_send.at[k], tap_recv.at[slot], fsdp=first + k
            ).start()

    for k in range(2):

        @pl.when(group + k * half == f)
        def _():
            got_ref[k] = taps_ref[...]

    for k in range(2):

        @pl.when(group + k * half != f)
        def _():
            remote(
                taps_ref, got_ref.at[k], tap_send.at[k], tap_recv.at[k], fsdp=group + k * half
            ).wait_recv()

        @pl.when(first + k != f)
        def _():
            remote(
                taps_ref, got_ref.at[slot], tap_send.at[k], tap_recv.at[slot], fsdp=first + k
            ).wait_send()

    to_up.wait()
    to_down.wait()


def entry(tails, taps):
    n_ctx = lax.axis_size("ctx")
    half = lax.axis_size("fsdp") // 2
    return pl.pallas_call(
        functools.partial(entry_kernel, n_ctx, half),
        out_shape=(
            jax.ShapeDtypeStruct(tails.shape, tails.dtype),
            jax.ShapeDtypeStruct((2,) + taps.shape, taps.dtype),
        ),
        in_specs=[VM] * 2,
        out_specs=(VM, VM),
        scratch_shapes=[pltpu.SemaphoreType.DMA((2,))] * 4,
        compiler_params=pltpu.CompilerParams(collective_id=0, has_side_effects=True),
        name="entry",
    )(tails, taps)


def exchange_kernel(
    n, rows, x_ref, g_ref, e_ref, y_ref, xr, gr, er, yo,
    xs_sem, xr_sem, gs_sem, gr_sem, es_sem, er_sem, ys_sem, yr_sem
):
    me = lax.axis_index("ctx")
    barrier = pltpu.get_barrier_semaphore()

    def other(i):
        return lax.rem(me + i, n)

    def mine(d):
        return pl.ds(pl.multiple_of(d * rows, rows), rows)

    def greet(i, _):
        signal(barrier, ctx=other(i))
        return 0

    lax.fori_loop(1, n, greet, 0)
    pl.semaphore_wait(barrier, n - 1)

    def x_copy(d):
        return remote(x_ref.at[:, mine(d)], xr.at[me], xs_sem.at[d], xr_sem.at[me], ctx=d)

    def g_copy(d):
        return remote(g_ref.at[:, mine(d)], gr.at[me], gs_sem.at[d], gr_sem.at[me], ctx=d)

    def e_copy(d):
        return remote(e_ref.at[d], er.at[me], es_sem.at[d], er_sem.at[me], ctx=d)

    def y_copy(d):
        return remote(yo.at[d], y_ref.at[:, mine(me)], ys_sem.at[d], yr_sem.at[me], ctx=d)

    def send(i, _):
        d = other(i)
        e_copy(d).start()
        g_copy(d).start()
        x_copy(d).start()
        return 0

    lax.fori_loop(1, n, send, 0)
    xr[me] = x_ref[:, mine(me)]
    gr[me] = g_ref[:, mine(me)]
    er[me] = e_ref[me]

    def arrived(i, _):
        s = other(i)
        remote(e_ref.at[s], er.at[s], es_sem.at[s], er_sem.at[s], ctx=s).wait_recv()
        remote(x_ref.at[:, mine(s)], xr.at[s], xs_sem.at[s], xr_sem.at[s], ctx=s).wait_recv()
        remote(g_ref.at[:, mine(s)], gr.at[s], gs_sem.at[s], gr_sem.at[s], ctx=s).wait_recv()
        return 0

    lax.fori_loop(1, n, arrived, 0)
    zero = jnp.zeros((rows, STATE), jnp.float32)

    def first(i, state):
        h, g = state
        yo[i, 0] = h.astype(yo.dtype)
        yo[i, 3] = g.astype(yo.dtype)
        h = er[i, 0:1, :] * h + xr[i, 0].astype(jnp.float32)
        g = er[i, 1:2, :] * g + gr[i, 1]
        return h, g

    def second(i, state):
        h, g = state
        j = n - 1 - i
        yo[j, 1] = h.astype(yo.dtype)
        yo[j, 2] = g.astype(yo.dtype)
        h = er[j, 1:2, :] * h + xr[j, 1].astype(jnp.float32)
        g = er[j, 0:1, :] * g + gr[j, 0]
        return h, g

    lax.fori_loop(0, n, second, lax.fori_loop(0, n, first, (zero, zero)))

    def back(i, _):
        y_copy(other(i)).start()
        return 0

    lax.fori_loop(1, n, back, 0)
    y_ref[:, mine(me)] = yo[me]

    def finish(i, _):
        d = other(i)
        e_copy(d).wait_send()
        g_copy(d).wait_send()
        x_copy(d).wait_send()
        y_copy(d).wait_send()
        remote(yo.at[d], y_ref.at[:, mine(d)], ys_sem.at[d], yr_sem.at[d], ctx=d).wait_recv()
        return 0

    lax.fori_loop(1, n, finish, 0)


def exchange(x, g, e):
    n = lax.axis_size("ctx")
    _, total, width = x.shape
    rows = total // n
    return pl.pallas_call(
        functools.partial(exchange_kernel, n, rows),
        out_shape=jax.ShapeDtypeStruct((4, total, width), x.dtype),
        in_specs=[VM] * 3,
        out_specs=VM,
        scratch_shapes=[
            pltpu.VMEM((n, 2, rows, width), x.dtype),
            pltpu.VMEM((n, 2, rows, width), jnp.float32),
            pltpu.VMEM((n, 2, width), jnp.float32),
            pltpu.VMEM((n, 4, rows, width), x.dtype),
        ]
        + [pltpu.SemaphoreType.DMA((n,))] * 8,
        compiler_params=pltpu.CompilerParams(
            collective_id=1, has_side_effects=True, vmem_limit_bytes=32 * 1024 * 1024
        ),
        name="exchange",
    )(x, g, e)


def owners_kernel(half, g_ref, got_ref, send_sem, recv_sem):
    f = lax.axis_index("fsdp")
    slot = f // half
    first = 2 * (f - slot * half)
    group = f // 2
    side = f - 2 * group
    barrier = pltpu.get_barrier_semaphore()
    for k in range(2):

        @pl.when(first + k != f)
        def _():
            signal(barrier, fsdp=first + k)

    selves = jnp.where(group == f, 1, 0) + jnp.where(group + half == f, 1, 0)
    pl.semaphore_wait(barrier, 2 - selves)
    for k in range(2):

        @pl.when(group + k * half != f)
        def _():
            remote(
                g_ref.at[k], got_ref.at[side], send_sem.at[k], recv_sem.at[side], fsdp=group + k * half
            ).start()

        @pl.when(group + k * half == f)
        def _():
            got_ref[side] = g_ref[k]

    for k in range(2):

        @pl.when(first + k != f)
        def _():
            remote(
                g_ref.at[k], got_ref.at[k], send_sem.at[k], recv_sem.at[k], fsdp=first + k
            ).wait_recv()

        @pl.when(group + k * half != f)
        def _():
            remote(
                g_ref.at[k], got_ref.at[side], send_sem.at[k], recv_sem.at[side], fsdp=group + k * half
            ).wait_send()


def to_owners(g):
    half = lax.axis_size("fsdp") // 2
    return pl.pallas_call(
        functools.partial(owners_kernel, half),
        out_shape=jax.ShapeDtypeStruct(g.shape, g.dtype),
        in_specs=[VM],
        out_specs=VM,
        scratch_shapes=[pltpu.SemaphoreType.DMA((2,))] * 2,
        compiler_params=pltpu.CompilerParams(collective_id=2, has_side_effects=True),
        name="owners",
    )(g)


def finish_kernel(
    n, rim_ref, part_ref, halo_ref, total_ref, parts, mine_sum,
    halo_send, halo_recv, ps_sem, pr_sem, ts_sem, tr_sem
):
    me = lax.axis_index("ctx")
    barrier = pltpu.get_barrier_semaphore()

    def other(i):
        return lax.rem(me + i, n)

    def greet(i, _):
        signal(barrier, ctx=other(i))
        return 0

    lax.fori_loop(1, n, greet, 0)
    pl.semaphore_wait(barrier, n - 1)
    up, down = other(1), other(n - 1)
    to_down = remote(rim_ref.at[0], halo_ref.at[0], halo_send.at[0], halo_recv.at[0], ctx=down)
    to_up = remote(rim_ref.at[1], halo_ref.at[1], halo_send.at[1], halo_recv.at[1], ctx=up)
    to_down.start()
    to_up.start()

    def p_copy(d):
        return remote(part_ref.at[d], parts.at[me], ps_sem.at[d], pr_sem.at[me], ctx=d)

    def t_copy(d):
        return remote(mine_sum, total_ref.at[me], ts_sem.at[d], tr_sem.at[me], ctx=d)

    def send(i, _):
        p_copy(other(i)).start()
        return 0

    lax.fori_loop(1, n, send, 0)
    parts[me] = part_ref[me]

    def arrived(i, _):
        s = other(i)
        remote(part_ref.at[s], parts.at[s], ps_sem.at[s], pr_sem.at[s], ctx=s).wait_recv()
        return 0

    lax.fori_loop(1, n, arrived, 0)
    mine_sum[...] = jnp.sum(parts[...], axis=0)

    def spread(i, _):
        t_copy(other(i)).start()
        return 0

    lax.fori_loop(1, n, spread, 0)
    total_ref[me] = mine_sum[...]

    def done(i, _):
        d = other(i)
        p_copy(d).wait_send()
        t_copy(d).wait_send()
        remote(mine_sum, total_ref.at[d], ts_sem.at[d], tr_sem.at[d], ctx=d).wait_recv()
        return 0

    lax.fori_loop(1, n, done, 0)
    to_down.wait()
    to_up.wait()


def finish(rims, part):
    n = lax.axis_size("ctx")
    return pl.pallas_call(
        functools.partial(finish_kernel, n),
        out_shape=(
            jax.ShapeDtypeStruct(rims.shape, rims.dtype),
            jax.ShapeDtypeStruct(part.shape, part.dtype),
        ),
        in_specs=[VM] * 2,
        out_specs=(VM, VM),
        scratch_shapes=[
            pltpu.VMEM(part.shape, part.dtype),
            pltpu.VMEM(part.shape[1:], part.dtype),
        ]
        + [pltpu.SemaphoreType.DMA((2,))] * 2
        + [pltpu.SemaphoreType.DMA((n,))] * 4,
        compiler_params=pltpu.CompilerParams(collective_id=3, has_side_effects=True),
        name="finish",
    )(rims, part)


def conv(rows, before, taps, bias):
    rim = before.shape[1]
    length = rows.shape[1]
    padded = jnp.concatenate([before, rows], axis=1)
    preact = bias[None, None, :] + jnp.zeros(rows.shape, jnp.float32)
    for tap in range(rim + 1):
        preact = preact + taps[tap][None, None, :] * padded[:, tap : tap + length]
    return padded, preact


def shards(
    sig_raw,
    map_raw,
    step_size_logits,
    d_out,
    sig_taps,
    map_taps,
    sig_bias,
    map_bias,
    a_log,
    dt_bias,
    skip_gain,
):
    kernel = sig_taps.shape[0]
    rim = kernel - 1
    length = sig_raw.shape[0] // 2
    sig_width = sig_raw.shape[1]
    map_width = map_raw.shape[1]
    heads_here = step_size_logits.shape[1]
    ratio = HEADS // GROUPS
    fsdp = lax.axis_index("fsdp")
    owned = map_width // lax.axis_size("fsdp")
    group_start = fsdp * heads_here // ratio * STATE
    map_start = fsdp * owned
    ctx = lax.axis_index("ctx")
    n_ctx = lax.axis_size("ctx")
    at_end = ctx == n_ctx - 1

    raw = jnp.concatenate(
        [
            sig_raw,
            lax.dynamic_slice_in_dim(map_raw, group_start, STATE, 1),
            lax.dynamic_slice_in_dim(map_raw, map_width // 2 + group_start, STATE, 1),
            lax.dynamic_slice_in_dim(map_raw, map_start, owned, 1),
        ],
        axis=1,
    )
    width = raw.shape[1]
    raw = raw.reshape(2, length, width).astype(jnp.float32)
    own_taps8 = jnp.concatenate(
        [map_taps, map_bias[None, :], jnp.zeros((8 - kernel - 1, owned), jnp.float32)], axis=0
    )
    halo, group_taps = entry(raw[:, length - 8 :], own_taps8)
    halo = halo[:, 8 - rim :]
    before = jnp.stack(
        [
            jnp.where(ctx == 0, 0.0, halo[0]),
            jnp.where(at_end, raw[0, length - rim :], halo[1]),
        ]
    )
    taps = jnp.concatenate(
        [sig_taps, group_taps[0, :kernel], group_taps[1, :kernel], map_taps], axis=1
    )
    bias = jnp.concatenate([sig_bias, group_taps[0, kernel], group_taps[1, kernel], map_bias])
    padded, preact = conv(raw, before, taps, bias)
    act_width = sig_width + 2 * STATE
    local_act = jax.nn.silu(preact[:, :, :act_width]).astype(jnp.bfloat16)
    dt_rows = step_size_logits.reshape(2, length, heads_here)
    grad_rows = d_out.reshape(2, length, heads_here, HDIM)

    def parts_of(act_block, dt_block):
        return block_parts(act_block, dt_block, a_log, dt_bias, 1)

    parts = jax.vmap(parts_of)(local_act, dt_rows)
    scaled_grad, state_grad = jax.vmap(entry_grad)(parts, grad_rows)
    ends = jnp.exp(parts[8][:, -1])
    local = parts[12].astype(jnp.bfloat16).reshape(2, heads_here * HDIM, STATE)
    state_grad = state_grad.reshape(2, heads_here * HDIM, STATE)
    decays = jnp.repeat(ends.T, n_ctx // heads_here, axis=0)[:, :, None]
    decays = jnp.broadcast_to(decays, (n_ctx, 2, STATE))
    linked = exchange(local, state_grad, decays).reshape(2, 2, heads_here, HDIM, STATE)
    h_ins = linked[0].astype(jnp.float32)
    carried = linked[1].astype(jnp.float32)
    grad_act, grad_dt, decay_log_gradient, grad_dtb, grad_skip = jax.vmap(
        block_grads, in_axes=(0, 0, 0, 0, 0, None, 0, None)
    )(parts, grad_rows, scaled_grad, h_ins, carried, skip_gain, dt_rows, dt_bias)
    map_grads = jnp.stack(
        [grad_act[:, :, sig_width : sig_width + STATE], grad_act[:, :, sig_width + STATE :]]
    )
    got = to_owners(map_grads.reshape(2, 2 * length, STATE))
    map_owned = (got[0] + got[1]).reshape(2, length, owned)
    own = jnp.concatenate([preact[:, :, :sig_width], preact[:, :, act_width:]], axis=2)
    own_padded = jnp.concatenate([padded[:, :, :sig_width], padded[:, :, act_width:]], axis=2)
    own_taps = jnp.concatenate([sig_taps, map_taps], axis=1)
    grad_pre = jnp.concatenate([grad_act[:, :, :sig_width], map_owned], axis=2) * silu_slope(own)
    own_width = sig_width + owned
    tap_grads = [
        jnp.sum(grad_pre * own_padded[:, tap : tap + length], axis=(0, 1)) for tap in range(kernel)
    ]
    tap_grads.append(jnp.sum(grad_pre, axis=(0, 1)))
    small = jnp.concatenate(
        [
            jnp.sum(decay_log_gradient, axis=0),
            jnp.sum(grad_dtb, axis=0),
            jnp.sum(grad_skip, axis=0),
        ]
    )
    flat = jnp.concatenate(tap_grads + [small])
    flat = jnp.pad(flat, (0, n_ctx * 128 - flat.shape[0])).reshape(n_ctx, 1, 128)
    rims, total = finish(grad_pre[:, :8], flat)
    after = jnp.stack(
        [
            jnp.where(at_end, grad_pre[1, :rim], rims[0, :rim]),
            jnp.where(ctx == 0, 0.0, rims[1, :rim]),
        ]
    )
    padded_next = jnp.concatenate([grad_pre, after], axis=1)
    grad_raw = jnp.zeros(grad_pre.shape, jnp.float32)
    for tap in range(kernel):
        grad_raw = (
            grad_raw
            + own_taps[tap][None, None, :] * padded_next[:, rim - tap : rim - tap + length]
        )
    scale = 1.0 / math.sqrt(float(n_ctx * 2 * length))
    total = total.reshape(-1) * scale
    body = (kernel + 1) * own_width
    table = total[:body].reshape(kernel + 1, own_width)
    tail = total[body : body + 3 * heads_here].reshape(3, heads_here)
    return (
        grad_raw[:, :, :sig_width].reshape(2 * length, sig_width),
        grad_raw[:, :, sig_width:].reshape(2 * length, owned),
        grad_dt.reshape(2 * length, heads_here),
        table[:kernel, :sig_width],
        table[:kernel, sig_width:],
        table[kernel, :sig_width],
        table[kernel, sig_width:],
        tail[0],
        tail[1],
        tail[2],
    )


def solution(mesh):
    return jax.shard_map(
        shards,
        mesh=mesh,
        in_specs=(
            P("ctx", "fsdp"),
            P("ctx", None),
            P("ctx", "fsdp"),
            P("ctx", "fsdp"),
            P(None, "fsdp"),
            P(None, "fsdp"),
            P("fsdp"),
            P("fsdp"),
            P("fsdp"),
            P("fsdp"),
            P("fsdp"),
        ),
        out_specs=(
            P("ctx", "fsdp"),
            P("ctx", "fsdp"),
            P("ctx", "fsdp"),
            P(None, "fsdp"),
            P(None, "fsdp"),
            P("fsdp"),
            P("fsdp"),
            P("fsdp"),
            P("fsdp"),
            P("fsdp"),
        ),
        check_vma=False,
    )
```

time: 1140 us -> 157 us (0.14)
  the two profiles are of different devices: /device:TPU:10 before, /device:TPU:18 now
where the time goes in v1:
time: 157 us; the launch traced here: 156 us
  Pallas kernels  130 us (83%)
  local copies, waits for them, and re-layouts  16.2 us (10%)
  other arithmetic  4.99 us (3%)
  matrix products  3.39 us (2%)
    pallas_call x1, Pallas kernels, exchange(): pl.pallas_call(functools.partial(exchange_kernel, n, rows), out_shape=jax...  72.8 us
    pallas_call x1, Pallas kernels, finish(): pl.pallas_call(functools.partial(finish_kernel, n), out_shape=(jax.ShapeD...  28.2 us
    pallas_call x1, Pallas kernels, entry(): pl.pallas_call(functools.partial(entry_kernel, n_ctx, half), out_shape=(j...  16.7 us
    pallas_call x1, Pallas kernels, to_owners(): pl.pallas_call(functools.partial(owners_kernel, half), out_shape=jax.Shap...  12.7 us
    unnamed x28, local copies, waits for them, and re-layouts  5.2 us

profile of v1, /device:TPU:18, one launch (start us, length us, event | category | flops | bytes accessed | tf_op | source)
XLA Modules:
  0.0 156.0 jit_solution(445721165561799880)
XLA Ops:
  0.7 0.6 copy-done.11
  1.4 0.6 copy-done.4
  2.0 0.7 maximum_maximum_fusion.1.taps_ref
  2.8 0.6 copy-done.10
  3.4 0.2 fusion.44
  4.2 0.6 copy-done.3
  5.0 0.8 constant_dynamic-slice_fusion.2
  5.9 0.6 slice.231.tail_ref
  6.5 16.7 %entry.1 = (f32[2,8,896]{2,1,0:T(8,128)}, f32[2,8,128]{2,1,0:T(8,128)}) custom-call(f32[2,8,896]{2,1,0:T(8,128)} %slice.231.tail_ref, f32[8,128]{1,0:T(8,128)} %maximum_maximum_fusion.1.taps_ref), custom_call_target="tpu_custom_call" | custom-call | tf_op jit(solution)/shard_map/entry/pallas_call | solution.py:218
  23.2 0.7 slice_bitcast_fusion.4
  23.9 0.7 slice_bitcast_fusion.1
  24.6 0.7 copy-done.8
  25.3 0.2 reshape.167
  25.5 0.2 copy.71
  25.8 0.8 copy-done.6
  26.6 0.2 fusion.14
  27.0 0.6 copy-done
  28.0 0.2 copy.99
  28.3 0.5 fusion.18
  29.0 0.2 convolution_convert_fusion
  29.2 0.2 fusion.35
  29.4 72.8 %exchange.1 = bf16[4,512,128]{2,1,0:T(8,128)(2,1)S(1)} custom-call(bf16[2,512,128]{2,1,0:T(8,128)(2,1)S(1)} %bitcast.103, f32[2,512,128]{2,1,0:T(8,128)S(1)} %bitcast.102, f32[32,2,128]{2,1,0:T(2,128)S(1)} %broadcast_in_dim.36.e_ref), custom_call_target="tpu_custom_call" | custom-call | tf_op jit(solution)/shard_map/exchange/pallas_call | solution.py:328
  102.2 0.2 multiply_reduce_fusion.1
  102.5 0.3 fusion.3
  102.7 0.2 convolution_bitcast_fusion.6
  103.0 0.2 fusion.4
  103.2 0.2 fusion.5
  103.4 0.3 fusion.7
  103.7 0.6 copy-done.12
  104.4 0.4 multiply_reduce_fusion
  104.8 0.2 copy.98
  105.0 0.7 pad_maximum_fusion.3.g_ref
  105.6 12.7 %owners.1 = f32[2,128,128]{2,1,0:T(8,128)} custom-call(f32[2,128,128]{2,1,0:T(8,128)} %pad_maximum_fusion.3.g_ref), custom_call_target="tpu_custom_call" | custom-call | tf_op jit(solution)/shard_map/owners/pallas_call | solution.py:391
  118.3 0.9 slice_add_fusion
  119.2 0.3 fusion.23
  120.1 0.4 fusion.66
  120.6 0.6 pad.4
  121.2 0.7 reshape.178
  121.9 0.6 slice.249.rim_ref
  122.5 28.2 %finish.1 = (f32[2,8,640]{2,1,0:T(8,128)}, f32[32,1,128]{2,1,0:T(1,128)}) custom-call(f32[2,8,640]{2,1,0:T(8,128)} %slice.249.rim_ref, f32[32,1,128]{2,1,0:T(1,128)} %bitcast.123), custom_call_target="tpu_custom_call" | custom-call | tf_op jit(solution)/shard_map/finish/pallas_call | solution.py:466
  150.8 0.8 slice_select_fusion.2
  151.6 0.6 fusion.69
  152.2 0.5 slice_bitcast_fusion.2
  152.7 0.6 slice.266
  153.3 0.6 slice.265
  153.9 0.6 slice.264
  154.7 0.6 slice.262
  155.3 0.7 slice.261
  (73 shorter events, 3.0 us)
Async XLA Ops:
  0.7 0.7 copy-start.11
  1.3 0.7 copy-start.4
  1.3 0.7 copy-start.9
  1.4 1.3 copy-start.7
  2.7 0.7 copy-start.10
  4.1 0.7 copy-start.3
  4.9 0.9 copy-start.2
  5.9 19.4 %copy-start.1 = (bf16[128,512]{1,0:T(8,128)(2,1)S(1)}, bf16[128,512]{1,0:T(8,128)(2,1)}, u32[]{:S(2)}) copy-start(bf16[128,512]{1,0:T(8,128)(2,1)} %param.14) | copy-start | bytes 393220
  24.6 0.7 copy-start.8
  25.7 0.8 copy-start.6
  26.8 0.8 copy-start
  103.7 0.7 copy-start.12
  105.6 13.6 %slice-start.1 = ((f32[2,64,896]{2,1,0:T(8,128)}), f32[2,64,512]{2,1,0:T(8,128)S(1)}, s32[]{:S(2)}) async-start(f32[2,64,896]{2,1,0:T(8,128)} %copy-done), calls=%async_computation.1 | async-start | bytes 524288 | tf_op jit(solution)/shard_map/slice | solution.py:576
  118.3 0.9 slice-start
  150.8 0.8 copy-start.5

commit v2 on v0

v2 whole, which is shorter than its diff:
```python
import functools
import math

import jax
import jax.numpy as jnp
from jax import lax
from jax.experimental import pallas as pl
from jax.experimental.pallas import tpu as pltpu
from jax.sharding import PartitionSpec as P

HEADS = 128
HDIM = 64
STATE = 128
GROUPS = 8
HERE = 8
KSIZE = 4
RIM = KSIZE - 1
BLK = 64
ROWS = 2 * BLK
SIG = HERE * HDIM
WIDE = SIG + 3 * STATE
OWN = SIG + STATE
EDGE = 8
TAIL = (KSIZE + 1) * OWN // STATE
MESH = pl.DeviceIdType.MESH
VM = pl.BlockSpec(memory_space=pltpu.VMEM)
HIGH = lax.Precision.HIGHEST
F32 = jnp.float32
BF16 = jnp.bfloat16


def signal(sem, **where):
    pl.semaphore_signal(sem, inc=1, device_id=where, device_id_type=MESH)


def remote(src, dst, send_sem, recv_sem, **where):
    return pltpu.make_async_remote_copy(
        src_ref=src,
        dst_ref=dst,
        send_sem=send_sem,
        recv_sem=recv_sem,
        device_id=where,
        device_id_type=MESH,
    )


def other(me, i, n):
    off = jnp.where(lax.rem(i, 2) == 1, (i + 1) // 2, n - i // 2)
    return lax.rem(me + off, n)


def columns(start):
    return pl.ds(pl.multiple_of(start * STATE, STATE), STATE)


def nn(a, b, precision=None):
    return lax.dot_general(
        a, b, (((1,), (0,)), ((), ())), precision=precision, preferred_element_type=F32
    )


def nt(a, b, precision=None):
    return lax.dot_general(
        a, b, (((1,), (1,)), ((), ())), precision=precision, preferred_element_type=F32
    )


def tn(a, b):
    return lax.dot_general(a, b, (((0,), (0,)), ((), ())), preferred_element_type=F32)


def sigmoid(v):
    return 1.0 / (1.0 + jnp.exp(-v))


def log1p_small(e):
    series = e * (
        1.0 + e * (-1.0 / 2 + e * (1.0 / 3 + e * (-1.0 / 4 + e * (1.0 / 5 + e * (-1.0 / 6)))))
    )
    return jnp.where(e < 0.03, series, jnp.log(1.0 + e))


def entry_kernel(
    n_ctx, half, sig_ref, map_ref, taps_in, bias_in, halo_ref, got_ref,
    tail_ref, taps_ref, halo_send, halo_recv, tap_send, tap_recv
):
    c = lax.axis_index("ctx")
    f = lax.axis_index("fsdp")
    up, down = lax.rem(c + 1, n_ctx), lax.rem(c + n_ctx - 1, n_ctx)
    slot = f // half
    first = 2 * (f - slot * half)
    group = f // 2
    barrier = pltpu.get_barrier_semaphore()
    signal(barrier, ctx=up)
    signal(barrier, ctx=down)
    for k in range(2):
        source = group + k * half

        @pl.when(source != f)
        def _():
            signal(barrier, fsdp=source)

    for b in range(2):
        rows = slice(b * BLK + BLK - EDGE, b * BLK + BLK)
        tail_ref[b, :, :SIG] = sig_ref[rows, :].astype(F32)
        for k, start in enumerate((group, GROUPS + group, f)):
            tail_ref[b, :, SIG + k * STATE : SIG + (k + 1) * STATE] = map_ref[
                rows, columns(start)
            ].astype(F32)
    taps_ref[0:KSIZE] = taps_in[...]
    taps_ref[KSIZE : KSIZE + 1] = bias_in[...]
    taps_ref[KSIZE + 1 :] = jnp.zeros((EDGE - KSIZE - 1, STATE), F32)
    selves = jnp.where(first == f, 1, 0) + jnp.where(first + 1 == f, 1, 0)
    pl.semaphore_wait(barrier, 4 - selves)
    to_up = remote(tail_ref.at[0], halo_ref.at[0], halo_send.at[0], halo_recv.at[0], ctx=up)
    to_down = remote(tail_ref.at[1], halo_ref.at[1], halo_send.at[1], halo_recv.at[1], ctx=down)
    for k in range(2):

        @pl.when(first + k != f)
        def _():
            remote(
                taps_ref, got_ref.at[slot], tap_send.at[k], tap_recv.at[slot], fsdp=first + k
            ).start()

    to_up.start()
    to_down.start()
    for k in range(2):

        @pl.when(group + k * half == f)
        def _():
            got_ref[k] = taps_ref[...]

    for k in range(2):

        @pl.when(group + k * half != f)
        def _():
            remote(
                taps_ref, got_ref.at[k], tap_send.at[k], tap_recv.at[k], fsdp=group + k * half
            ).wait_recv()

        @pl.when(first + k != f)
        def _():
            remote(
                taps_ref, got_ref.at[slot], tap_send.at[k], tap_recv.at[slot], fsdp=first + k
            ).wait_send()

    to_up.wait()
    to_down.wait()


def entry(sig_raw, map_raw, map_taps, map_bias):
    n_ctx = lax.axis_size("ctx")
    half = lax.axis_size("fsdp") // 2
    return pl.pallas_call(
        functools.partial(entry_kernel, n_ctx, half),
        out_shape=(
            jax.ShapeDtypeStruct((2, EDGE, WIDE), F32),
            jax.ShapeDtypeStruct((2, EDGE, STATE), F32),
        ),
        in_specs=[VM] * 4,
        out_specs=(VM, VM),
        scratch_shapes=[
            pltpu.VMEM((2, EDGE, WIDE), F32),
            pltpu.VMEM((EDGE, STATE), F32),
        ]
        + [pltpu.SemaphoreType.DMA((2,))] * 4,
        compiler_params=pltpu.CompilerParams(
            collective_id=0, has_side_effects=True, vmem_limit_bytes=32 * 1024 * 1024
        ),
        name="entry",
    )(sig_raw, map_raw, map_taps, map_bias)


def main_kernel(
    n, half, sig_ref, map_ref, dt_ref, dout_ref, taps_ref, bias_ref, mtaps_ref, mbias_ref,
    alog_ref, dtb_ref, skip_ref, halo_ref, gtaps_ref,
    gp, rims, total, ddt_ref,
    pad, slope, signal_ref, scaled_ref, weighted_ref, sgrad_ref, imap_ref, omap_ref, wide3, intra,
    oh, gw, drow, xs, gs, es, xr, gr, er, yo, lk, mg, mgot, part, parts, mine_sum,
    xs_sem, xr_sem, gs_sem, gr_sem, es_sem, er_sem, ys_sem, yr_sem, ms_sem, mr_sem,
    hs_sem, hr_sem, ps_sem, pr_sem, ts_sem, tr_sem
):
    me = lax.axis_index("ctx")
    f = lax.axis_index("fsdp")
    slot = f // half
    first = 2 * (f - slot * half)
    group = f // 2
    side = f - 2 * group
    share = HERE * HDIM // n
    per_head = n // HERE
    barrier = pltpu.get_barrier_semaphore()

    def greet(i, _):
        signal(barrier, ctx=other(me, i, n))
        return 0

    lax.fori_loop(1, n, greet, 0)
    for k in range(2):

        @pl.when(first + k != f)
        def _():
            signal(barrier, fsdp=first + k)

    lane = lax.broadcasted_iota(jnp.int32, (HERE, ROWS), 1)
    row_id = lax.broadcasted_iota(jnp.int32, (ROWS, ROWS), 0)
    col_id = lax.broadcasted_iota(jnp.int32, (ROWS, ROWS), 1)
    lower = ((row_id >= BLK) == (col_id >= BLK)) & (col_id <= row_id)
    lower_f = jnp.where(lower, 1.0, 0.0).astype(F32)
    eye = jnp.where(row_id == col_id, 1.0, 0.0).astype(F32)
    eye8 = eye[:HERE, :HERE]
    ones8 = jnp.ones((HERE, ROWS), F32)
    head3 = lax.broadcasted_iota(jnp.int32, (3 * HERE, 3 * SIG), 0)
    spread3 = jnp.where(
        lax.broadcasted_iota(jnp.int32, (3 * HERE, 3 * SIG), 1) // HDIM == head3, 1.0, 0.0
    ).astype(F32)
    spread1 = spread3[:HERE, :SIG]

    def in_rows(ref):
        return nt(eye8, jnp.broadcast_to(ref[...], (ROWS, HERE)), HIGH)

    def per_row(y):
        return nt(spread1, y, HIGH)

    logits = nt(eye8, dt_ref[...], HIGH) + in_rows(dtb_ref)
    rate = -jnp.exp(in_rows(alog_ref))
    step = jnp.maximum(logits, 0.0) + log1p_small(jnp.exp(-jnp.abs(logits)))
    ds = nt(step * rate, lower_f, HIGH)
    end_low = jnp.exp(ds[:, BLK - 1 : BLK])
    end_high = jnp.exp(ds[:, ROWS - 1 : ROWS])
    end = jnp.where(lane < BLK, ds[:, BLK - 1 : BLK], ds[:, ROWS - 1 : ROWS])
    to_end = jnp.exp(end - ds)
    col4 = nt(eye, jnp.concatenate([step, to_end, jnp.exp(ds), ds], axis=0), HIGH)
    ds_col = col4[:, 3 * HERE :]
    wide3[...] = nn(col4[:, : 3 * HERE], spread3, HIGH)
    end_low8 = jnp.broadcast_to(end_low, (HERE, STATE))
    end_high8 = jnp.broadcast_to(end_high, (HERE, STATE))
    for h in range(HERE):
        es[h, 0:1, :] = end_low8[h : h + 1]
        es[h, 1:2, :] = end_high8[h : h + 1]

    keep = jnp.where(me == 0, 0.0, 1.0).astype(F32)
    for b in range(2):
        rows = slice(b * BLK, (b + 1) * BLK)
        pad[b, EDGE:, :SIG] = sig_ref[rows, :].astype(F32)
        for k, start in enumerate((group, GROUPS + group, f)):
            pad[b, EDGE:, SIG + k * STATE : SIG + (k + 1) * STATE] = map_ref[
                rows, columns(start)
            ].astype(F32)
    pad[0, :EDGE] = halo_ref[0] * keep
    pad[1, :EDGE] = jnp.where(me == n - 1, pad[0, BLK:], halo_ref[1])

    def preact(b, cols, taps, bias):
        acc = bias
        for k in range(KSIZE):
            start = EDGE - RIM + k
            acc = acc + taps[k : k + 1] * pad[b, start : start + BLK, cols]
        return acc

    for b in range(2):
        rows = slice(b * BLK, (b + 1) * BLK)
        for q in range(SIG // STATE):
            cols = slice(q * STATE, (q + 1) * STATE)
            v = preact(b, cols, taps_ref[:, cols], bias_ref[:, cols])
            s = sigmoid(v)
            slope[rows, cols] = s * (1.0 + v * (1.0 - s))
            signal_b = (v * s).astype(BF16)
            signal_ref[rows, cols] = signal_b
            scaled_b = (signal_b.astype(F32) * wide3[rows, cols]).astype(BF16)
            scaled_ref[rows, cols] = scaled_b
            cols2 = slice(SIG + q * STATE, SIG + (q + 1) * STATE)
            cols3 = slice(2 * SIG + q * STATE, 2 * SIG + (q + 1) * STATE)
            weighted_ref[rows, cols] = (scaled_b.astype(F32) * wide3[rows, cols2]).astype(BF16)
            sgrad_ref[rows, cols] = (
                dout_ref[rows, cols].astype(F32) * wide3[rows, cols3]
            ).astype(BF16)
        for k, out in enumerate((imap_ref, omap_ref)):
            cols = slice(SIG + k * STATE, SIG + (k + 1) * STATE)
            v = preact(b, cols, gtaps_ref[k, :KSIZE], gtaps_ref[k, KSIZE : KSIZE + 1])
            out[rows, :] = (v * sigmoid(v)).astype(BF16)
        v = preact(b, slice(SIG + 2 * STATE, WIDE), mtaps_ref[...], mbias_ref[...])
        s = sigmoid(v)
        slope[rows, SIG:] = s * (1.0 + v * (1.0 - s))
        gs[b] = tn(sgrad_ref[rows, :], omap_ref[rows, :])
        xs[b] = tn(weighted_ref[rows, :], imap_ref[rows, :]).astype(BF16)

    def mine(d):
        return pl.ds(pl.multiple_of(d * share, share), share)

    def x_copy(d):
        return remote(xs.at[:, mine(d)], xr.at[me], xs_sem.at[d], xr_sem.at[me], ctx=d)

    def g_copy(d):
        return remote(gs.at[:, mine(d)], gr.at[me], gs_sem.at[d], gr_sem.at[me], ctx=d)

    def e_copy(d):
        return remote(es.at[d // per_head], er.at[me], es_sem.at[d], er_sem.at[me], ctx=d)

    def y_copy(d):
        return remote(yo.at[d], lk.at[:, mine(me)], ys_sem.at[d], yr_sem.at[me], ctx=d)

    selves = jnp.where(group == f, 1, 0) + jnp.where(group + half == f, 1, 0)
    pl.semaphore_wait(barrier, n - 1 + 2 - selves)

    def send(i, _):
        d = other(me, i, n)
        g_copy(d).start()
        x_copy(d).start()
        e_copy(d).start()
        return 0

    lax.fori_loop(1, n, send, 0)
    xr[me] = xs[:, mine(me)]
    gr[me] = gs[:, mine(me)]
    er[me] = es[me // per_head]

    score = nt(omap_ref[...], imap_ref[...])
    lane_row = lax.broadcasted_iota(jnp.int32, (ROWS, STATE), 1)
    grad_score = jnp.zeros((ROWS, ROWS), F32)
    for q in range(HERE // 2):
        cols = slice(q * STATE, (q + 1) * STATE)
        d_pair = dout_ref[:, cols].astype(F32)
        d_two = jnp.concatenate(
            [jnp.where(lane_row < HDIM, d_pair, 0.0), jnp.where(lane_row < HDIM, 0.0, d_pair)],
            axis=0,
        ).astype(BF16)
        grad_mix2 = nt(d_two, scaled_ref[:, cols])
        mixes = []
        for k in range(2):
            h = 2 * q + k
            grad_mix = grad_mix2[k * ROWS : (k + 1) * ROWS]
            gap = jnp.minimum(ds_col[:, h : h + 1] - ds[h : h + 1, :], 0.0)
            decay = jnp.where(lower, jnp.exp(gap), 0.0)
            mix = score * decay
            mixes.append(mix.astype(BF16))
            grad_score = grad_score + grad_mix * decay
            product = grad_mix * mix
            drow[h : h + 1, :] = nt(ones8, product, HIGH)[0:1] - jnp.sum(
                product, axis=0, keepdims=True
            )
        intra[:, cols] = tn(jnp.concatenate(mixes, axis=0), d_two)
    grad_score = grad_score.astype(BF16)
    mg[0] = tn(grad_score, omap_ref[...])
    mg[1] = nn(grad_score, imap_ref[...])

    def arrived(i, _):
        s = other(me, i, n)
        remote(es.at[s // per_head], er.at[s], es_sem.at[s], er_sem.at[s], ctx=s).wait_recv()
        remote(xs.at[:, mine(s)], xr.at[s], xs_sem.at[s], xr_sem.at[s], ctx=s).wait_recv()
        remote(gs.at[:, mine(s)], gr.at[s], gs_sem.at[s], gr_sem.at[s], ctx=s).wait_recv()
        return 0

    lax.fori_loop(1, n, arrived, 0)
    zero = jnp.zeros((share, STATE), F32)

    def out_and_up(i, state):
        h, g = state
        yo[i, 0] = h.astype(BF16)
        yo[i, 3] = g.astype(BF16)
        h = er[i, 0:1, :] * h + xr[i, 0].astype(F32)
        g = er[i, 1:2, :] * g + gr[i, 1]
        return h, g

    def out_and_down(i, state):
        h, g = state
        j = n - 1 - i
        yo[j, 1] = h.astype(BF16)
        yo[j, 2] = g.astype(BF16)
        h = er[j, 1:2, :] * h + xr[j, 1].astype(F32)
        g = er[j, 0:1, :] * g + gr[j, 0]
        return h, g

    lax.fori_loop(0, n, out_and_down, lax.fori_loop(0, n, out_and_up, (zero, zero)))

    def back(i, _):
        y_copy(other(me, i, n)).start()
        return 0

    lax.fori_loop(1, n, back, 0)
    lk[:, mine(me)] = yo[me]

    def linked(i, _):
        d = other(me, i, n)
        g_copy(d).wait_send()
        x_copy(d).wait_send()
        e_copy(d).wait_send()
        remote(yo.at[d], lk.at[:, mine(d)], ys_sem.at[d], yr_sem.at[d], ctx=d).wait_recv()
        return 0

    lax.fori_loop(1, n, linked, 0)

    for b in range(2):
        rows = slice(b * BLK, (b + 1) * BLK)
        mg[0, rows, :] = mg[0, rows, :] + nn(weighted_ref[rows, :], lk[2 + b])
        mg[1, rows, :] = mg[1, rows, :] + nn(sgrad_ref[rows, :], lk[b])

    def m_copy(k):
        return remote(
            mg.at[k], mgot.at[side], ms_sem.at[k], mr_sem.at[side], fsdp=group + k * half
        )

    for k in range(2):

        @pl.when(group + k * half != f)
        def _():
            m_copy(k).start()

        @pl.when(group + k * half == f)
        def _():
            mgot[side] = mg[k]

    end_terms = []
    for b in range(2):
        rows = slice(b * BLK, (b + 1) * BLK)
        oh[rows, :] = nt(omap_ref[rows, :], lk[b])
        gw[rows, :] = nt(imap_ref[rows, :], lk[2 + b])
        both = lk[b].astype(F32) * lk[2 + b].astype(F32)
        both = jnp.sum(both.reshape(HERE, HDIM, STATE), axis=1)
        end_terms.append(jnp.sum(both, axis=1, keepdims=True))
    step_w = wide3[:, :SIG]
    end_w = wide3[:, SIG : 2 * SIG]
    exp_w = wide3[:, 2 * SIG :]
    d_f = dout_ref[...].astype(F32)
    signal_f = signal_ref[...].astype(F32)
    gw_v = gw[...]
    back_row = per_row(gw_v * scaled_ref[...].astype(F32)) * to_end
    grad_sum = per_row(d_f * exp_w * oh[...]) - back_row + drow[...]
    back_low = jnp.sum(jnp.where(lane < BLK, back_row, 0.0), axis=1, keepdims=True)
    back_high = jnp.sum(jnp.where(lane < BLK, 0.0, back_row), axis=1, keepdims=True)
    last_low = back_low + end_low * end_terms[0]
    last_high = back_high + end_high * end_terms[1]
    grad_sum = grad_sum + jnp.where(
        lane == BLK - 1, last_low, jnp.where(lane == ROWS - 1, last_high, 0.0)
    )
    grad_log = nn(grad_sum, lower_f, HIGH)
    grad_scaled = gw_v * end_w + intra[...]
    grad_step = grad_log * rate + per_row(grad_scaled * signal_f)
    grad_dt = grad_step * sigmoid(logits)
    ddt_ref[...] = nt(eye, grad_dt, HIGH)
    skip_w = nn(jnp.broadcast_to(skip_ref[...], (HERE, HERE)), spread1, HIGH)[0:1]
    gp[:, :SIG] = (skip_w * d_f + grad_scaled * step_w) * slope[:, :SIG]
    part[...] = jnp.zeros(part.shape, F32)
    part[TAIL, 0:1, :HERE] = nt(ones8, grad_log * step, HIGH)[0:1] * (-jnp.exp(alog_ref[...]))
    part[TAIL + 1, 0:1, :HERE] = nt(ones8, grad_dt, HIGH)[0:1]
    part[TAIL + 2, 0:1, :HERE] = nt(ones8, per_row(d_f * signal_f), HIGH)[0:1]

    def sums(cols, source, at):
        for k in range(KSIZE + 1):
            acc = jnp.zeros((1, STATE), F32)
            for b in range(2):
                g = gp[b * BLK : (b + 1) * BLK, cols]
                if k < KSIZE:
                    start = EDGE - RIM + k
                    g = g * pad[b, start : start + BLK, source]
                acc = acc + jnp.sum(g, axis=0, keepdims=True)
            part[k * (OWN // STATE) + at, 0:1, :] = acc

    for q in range(SIG // STATE):
        cols = slice(q * STATE, (q + 1) * STATE)
        sums(cols, cols, q)

    for k in range(2):

        @pl.when(first + k != f)
        def _():
            remote(
                mg.at[k], mgot.at[k], ms_sem.at[k], mr_sem.at[k], fsdp=first + k
            ).wait_recv()

    gp[:, SIG:] = (mgot[0] + mgot[1]) * slope[:, SIG:]
    up, down = lax.rem(me + 1, n), lax.rem(me + n - 1, n)
    to_down = remote(gp.at[0:EDGE], rims.at[0], hs_sem.at[0], hr_sem.at[0], ctx=down)
    to_up = remote(gp.at[BLK : BLK + EDGE], rims.at[1], hs_sem.at[1], hr_sem.at[1], ctx=up)
    to_down.start()
    to_up.start()
    sums(slice(SIG, OWN), slice(SIG + 2 * STATE, WIDE), SIG // STATE)

    def p_copy(d):
        return remote(part.at[d], parts.at[me], ps_sem.at[d], pr_sem.at[me], ctx=d)

    def t_copy(d):
        return remote(mine_sum, total.at[me], ts_sem.at[d], tr_sem.at[me], ctx=d)

    def send_part(i, _):
        p_copy(other(me, i, n)).start()
        return 0

    lax.fori_loop(1, n, send_part, 0)
    parts[me] = part[me]

    def part_in(i, _):
        s = other(me, i, n)
        remote(part.at[s], parts.at[s], ps_sem.at[s], pr_sem.at[s], ctx=s).wait_recv()
        return 0

    lax.fori_loop(1, n, part_in, 0)
    mine_sum[...] = jnp.sum(parts[...], axis=0)

    def send_total(i, _):
        t_copy(other(me, i, n)).start()
        return 0

    lax.fori_loop(1, n, send_total, 0)
    total[me] = mine_sum[...]

    def done(i, _):
        d = other(me, i, n)
        y_copy(d).wait_send()
        p_copy(d).wait_send()
        t_copy(d).wait_send()
        remote(mine_sum, total.at[d], ts_sem.at[d], tr_sem.at[d], ctx=d).wait_recv()
        return 0

    lax.fori_loop(1, n, done, 0)
    for k in range(2):

        @pl.when(group + k * half != f)
        def _():
            m_copy(k).wait_send()

    to_down.wait()
    to_up.wait()


def main(*operands):
    n = lax.axis_size("ctx")
    half = lax.axis_size("fsdp") // 2
    share = HERE * HDIM // n
    dma = pltpu.SemaphoreType.DMA
    vm = pltpu.VMEM
    return pl.pallas_call(
        functools.partial(main_kernel, n, half),
        out_shape=(
            jax.ShapeDtypeStruct((ROWS, OWN), F32),
            jax.ShapeDtypeStruct((2, EDGE, OWN), F32),
            jax.ShapeDtypeStruct((n, 1, STATE), F32),
            jax.ShapeDtypeStruct((ROWS, HERE), F32),
        ),
        in_specs=[VM] * len(operands),
        out_specs=(VM,) * 4,
        scratch_shapes=[
            vm((2, EDGE + BLK, WIDE), F32),
            vm((ROWS, OWN), F32),
            vm((ROWS, SIG), BF16),
            vm((ROWS, SIG), BF16),
            vm((ROWS, SIG), BF16),
            vm((ROWS, SIG), BF16),
            vm((ROWS, STATE), BF16),
            vm((ROWS, STATE), BF16),
            vm((ROWS, 3 * SIG), F32),
            vm((ROWS, SIG), F32),
            vm((ROWS, SIG), F32),
            vm((ROWS, SIG), F32),
            vm((HERE, ROWS), F32),
            vm((2, SIG, STATE), BF16),
            vm((2, SIG, STATE), F32),
            vm((HERE, 2, STATE), F32),
            vm((n, 2, share, STATE), BF16),
            vm((n, 2, share, STATE), F32),
            vm((n, 2, STATE), F32),
            vm((n, 4, share, STATE), BF16),
            vm((4, SIG, STATE), BF16),
            vm((2, ROWS, STATE), F32),
            vm((2, ROWS, STATE), F32),
            vm((n, 1, STATE), F32),
            vm((n, 1, STATE), F32),
            vm((1, STATE), F32),
        ]
        + [dma((n,))] * 8
        + [dma((2,))] * 4
        + [dma((n,))] * 4,
        compiler_params=pltpu.CompilerParams(
            collective_id=1, has_side_effects=True, vmem_limit_bytes=48 * 1024 * 1024
        ),
        name="main",
    )(*operands)


def last_kernel(
    n, scale, gp, rims, total, ddt, taps_ref, mtaps_ref,
    dsig, dmap, ddt_out, dtaps, dmtaps, dbias, dmbias, dalog, ddtb, dskip, pad
):
    me = lax.axis_index("ctx")
    keep = jnp.where(me == 0, 0.0, 1.0).astype(F32)
    for b in range(2):
        pad[b, :BLK] = gp[b * BLK : (b + 1) * BLK]
    pad[0, BLK:] = jnp.where(me == n - 1, gp[BLK : BLK + EDGE], rims[0])
    pad[1, BLK:] = rims[1] * keep
    for b in range(2):
        rows = slice(b * BLK, (b + 1) * BLK)
        for out, taps, cols in (
            (dsig, taps_ref, slice(0, SIG)),
            (dmap, mtaps_ref, slice(SIG, OWN)),
        ):
            acc = taps[RIM : RIM + 1] * pad[b, 0:BLK, cols]
            for k in range(RIM):
                acc = acc + taps[k : k + 1] * pad[b, RIM - k : RIM - k + BLK, cols]
            out[rows, :] = acc
    ddt_out[...] = ddt[...]
    for k in range(KSIZE + 1):
        for q in range(OWN // STATE):
            row = total[k * (OWN // STATE) + q] * scale
            cols = slice(q * STATE, (q + 1) * STATE)
            if q < SIG // STATE:
                if k < KSIZE:
                    dtaps[k : k + 1, cols] = row
                else:
                    dbias[:, cols] = row
            elif k < KSIZE:
                dmtaps[k : k + 1, :] = row
            else:
                dmbias[...] = row
    for k, out in enumerate((dalog, ddtb, dskip)):
        out[...] = total[TAIL + k][:, :HERE] * scale


def last(gp, rims, total, ddt, sig_taps, map_taps):
    n = lax.axis_size("ctx")
    scale = 1.0 / math.sqrt(float(n * ROWS))
    shapes = (
        (ROWS, SIG), (ROWS, STATE), (ROWS, HERE), (KSIZE, SIG), (KSIZE, STATE),
        (1, SIG), (1, STATE), (1, HERE), (1, HERE), (1, HERE),
    )
    return pl.pallas_call(
        functools.partial(last_kernel, n, scale),
        out_shape=tuple(jax.ShapeDtypeStruct(s, F32) for s in shapes),
        in_specs=[VM] * 6,
        out_specs=(VM,) * len(shapes),
        scratch_shapes=[pltpu.VMEM((2, BLK + EDGE, OWN), F32)],
        name="last",
    )(gp, rims, total, ddt, sig_taps, map_taps)


def shards(
    sig_raw,
    map_raw,
    step_size_logits,
    d_out,
    sig_taps,
    map_taps,
    sig_bias,
    map_bias,
    a_log,
    dt_bias,
    skip_gain,
):
    bias = map_bias[None, :]
    halo, group_taps = entry(sig_raw, map_raw, map_taps, bias)
    found = main(
        sig_raw, map_raw, step_size_logits, d_out, sig_taps, sig_bias[None, :], map_taps, bias,
        a_log[None, :], dt_bias[None, :], skip_gain[None, :], halo, group_taps,
    )
    out = last(*found, sig_taps, map_taps)
    return out[:5] + tuple(a.reshape(-1) for a in out[5:])


def solution(mesh):
    return jax.shard_map(
        shards,
        mesh=mesh,
        in_specs=(
            P("ctx", "fsdp"),
            P("ctx", None),
            P("ctx", "fsdp"),
            P("ctx", "fsdp"),
            P(None, "fsdp"),
            P(None, "fsdp"),
            P("fsdp"),
            P("fsdp"),
            P("fsdp"),
            P("fsdp"),
            P("fsdp"),
        ),
        out_specs=(
            P("ctx", "fsdp"),
            P("ctx", "fsdp"),
            P("ctx", "fsdp"),
            P(None, "fsdp"),
            P(None, "fsdp"),
            P("fsdp"),
            P("fsdp"),
            P("fsdp"),
            P("fsdp"),
            P("fsdp"),
        ),
        check_vma=False,
    )
```

time: 1140 us -> 123 us (0.11)
  the two profiles are of different devices: /device:TPU:10 before, /device:TPU:26 now
where the time goes in v2:
time: 123 us; the launch traced here: 122 us
  Pallas kernels  113 us (92%)
  local copies, waits for them, and re-layouts  8.91 us (7%)
    pallas_call x1, Pallas kernels, main(): pl.pallas_call(functools.partial(main_kernel, n, half), out_shape=(jax.Sh...  96.9 us
    pallas_call x1, Pallas kernels, entry(): pl.pallas_call(functools.partial(entry_kernel, n_ctx, half), out_shape=(j...  14 us
    unnamed x36, local copies, waits for them, and re-layouts  8.91 us

profile of v2, /device:TPU:26, one launch (start us, length us, event | category | flops | bytes accessed | tf_op | source)
XLA Modules:
  0.0 122.5 jit_solution(9567920839810913649)
XLA Ops:
  0.6 0.0 copy-start.16
  0.7 0.7 copy-done.16
  1.3 0.0 copy-start.9
  1.3 0.0 copy-start.11
  1.3 0.0 copy-start.8
  1.3 0.1 copy.21.dt_ref
  1.4 0.6 copy-done.9
  2.0 0.0 copy-done.11
  2.0 0.0 copy-start
  2.0 1.0 copy-done
  3.1 0.0 copy-start.2
  3.1 0.9 copy-done.2
  4.0 0.0 copy-start.1
  4.0 0.0 copy-start.3
  4.0 14.0 %entry.1 = (f32[2,8,896]{2,1,0:T(8,128)S(1)}, f32[2,8,128]{2,1,0:T(8,128)S(1)}) custom-call(bf16[128,512]{1,0:T(8,128)(2,1)S(1)} %copy-done.2, bf16[128,2048]{1,0:T(8,128)(2,1)S(1)} %copy-done, f32[4,128]{1,0:T(4,128)S(1)} %copy-done.9, f32[1,128]{1,0:T(1,128)S(1)} %bitcast.10), custom_call_target="tpu_custom_call" | custom-call | tf_op jit(solution)/shard_map/entry/pallas_call | solution.py:154
  17.9 0.0 copy-start.12
  18.0 0.0 copy-start.13
  18.0 0.0 copy-start.14
  18.0 0.0 copy-start.15
  18.0 0.0 copy-done.8
  18.0 0.0 copy-done.1
  18.0 0.0 copy-done.3
  18.0 0.6 copy-done.12
  18.6 0.0 copy-done.13
  18.6 0.0 copy-done.14
  18.6 0.0 copy-done.15
  18.7 0.0 copy-start.5
  18.7 0.9 copy-done.5
  19.6 96.9 %main.1 = (f32[128,640]{1,0:T(8,128)S(1)}, f32[2,8,640]{2,1,0:T(8,128)S(1)}, f32[32,1,128]{2,1,0:T(1,128)S(1)}, f32[128,8]{1,0:T(8,128)S(1)}) custom-call(bf16[128,512]{1,0:T(8,128)(2,1)S(1)} %copy-done.3, bf16[128,2048]{1,0:T(8,128)(2,1)S(1)} %copy-done.1, f32[128,8]{1,0:T(8,128)S(1)} %copy.21.dt_ref, bf16[128,512]{1,0:T(8,128)(2,1)S(1)} %copy-done.5, ...), custom_call_target="tpu_custom_call" | custom-call | tf_op jit(solution)/shard_map/main/pallas_call | solution.py:530
  116.5 0.0 copy-start.4
  116.5 0.7 copy-done.4
  117.2 0.0 copy-start.6
  117.2 0.6 copy-done.6
  117.8 0.0 copy-start.7
  117.8 0.6 copy-done.7
  118.4 0.0 copy-start.10
  118.4 0.6 copy-done.10
  119.0 2.0 %last.1 = (f32[128,512]{1,0:T(8,128)}, f32[128,128]{1,0:T(8,128)}, f32[128,8]{1,0:T(8,128)}, f32[4,512]{1,0:T(4,128)}, f32[4,128]{1,0:T(4,128)}, /*index=5*/f32[...) custom-call(f32[128,640]{1,0:T(8,128)} %copy-done.4, f32[2,8,640]{2,1,0:T(8,128)} %copy-done.7, ...), custom_call_target="tpu_custom_call" | custom-call | tf_op jit(solution)/shard_map/last/pallas_call | solution.py:623
  121.0 1.5 %copy.22 = f32[128,8]{0,1:T(8,128)} copy(f32[128,8]{1,0:T(8,128)} %get-tuple-element.44) | data formatting | bytes 8192
Async XLA Ops:
  0.6 0.7 copy-start.16
  1.3 0.7 copy-start.9
  1.3 0.7 copy-start.11
  1.3 16.7 %copy-start.8 = (f32[4,512]{1,0:T(4,128)S(1)}, f32[4,512]{1,0:T(4,128)}, u32[]{:S(2)}) copy-start(f32[4,512]{1,0:T(4,128)} %taps_ref.3) | copy-start | bytes 24580
  2.0 1.0 copy-start
  3.1 0.9 copy-start.2
  4.0 14.0 %copy-start.1 = (bf16[128,2048]{1,0:T(8,128)(2,1)S(1)}, bf16[128,2048]{1,0:T(8,128)(2,1)}, u32[]{:S(2)}) copy-start(bf16[128,2048]{1,0:T(8,128)(2,1)} %map_ref.3) | copy-start | bytes 1572868
  4.0 14.1 %copy-start.3 = (bf16[128,512]{1,0:T(8,128)(2,1)S(1)}, bf16[128,512]{1,0:T(8,128)(2,1)}, u32[]{:S(2)}) copy-start(bf16[128,512]{1,0:T(8,128)(2,1)} %sig_ref.3) | copy-start | bytes 393220
  17.9 0.7 copy-start.12
  18.0 0.7 copy-start.13
  18.0 0.7 copy-start.14
  18.0 0.7 copy-start.15
  18.7 0.9 copy-start.5
  116.5 0.7 copy-start.4
  117.2 0.6 copy-start.6
  117.8 0.6 copy-start.7
  118.4 0.6 copy-start.10

commit v3 on v2

v3 whole, which is shorter than its diff:
```python
import functools
import math

import jax
import jax.numpy as jnp
from jax import lax
from jax.experimental import pallas as pl
from jax.experimental.pallas import tpu as pltpu
from jax.sharding import PartitionSpec as P

HEADS = 128
HDIM = 64
STATE = 128
GROUPS = 8
HERE = 8
KSIZE = 4
RIM = KSIZE - 1
BLK = 64
ROWS = 2 * BLK
SIG = HERE * HDIM
WIDE = SIG + 3 * STATE
OWN = SIG + STATE
EDGE = 16
RIMS = 8
TAIL = (KSIZE + 1) * OWN // STATE
MESH = pl.DeviceIdType.MESH
VM = pl.BlockSpec(memory_space=pltpu.VMEM)
HIGH = lax.Precision.HIGHEST
F32 = jnp.float32
BF16 = jnp.bfloat16


def signal(sem, **where):
    pl.semaphore_signal(sem, inc=1, device_id=where, device_id_type=MESH)


def remote(src, dst, send_sem, recv_sem, **where):
    return pltpu.make_async_remote_copy(
        src_ref=src,
        dst_ref=dst,
        send_sem=send_sem,
        recv_sem=recv_sem,
        device_id=where,
        device_id_type=MESH,
    )


def other(me, i, n):
    off = jnp.where(lax.rem(i, 2) == 1, (i + 1) // 2, n - i // 2)
    return lax.rem(me + off, n)


def columns(start):
    return pl.ds(pl.multiple_of(start * STATE, STATE), STATE)


def nn(a, b, precision=None):
    return lax.dot_general(
        a, b, (((1,), (0,)), ((), ())), precision=precision, preferred_element_type=F32
    )


def nt(a, b, precision=None):
    return lax.dot_general(
        a, b, (((1,), (1,)), ((), ())), precision=precision, preferred_element_type=F32
    )


def tn(a, b):
    return lax.dot_general(a, b, (((0,), (0,)), ((), ())), preferred_element_type=F32)


def sigmoid(v):
    return 1.0 / (1.0 + jnp.exp(-v))


def log1p_small(e):
    series = e * (
        1.0 + e * (-1.0 / 2 + e * (1.0 / 3 + e * (-1.0 / 4 + e * (1.0 / 5 + e * (-1.0 / 6)))))
    )
    return jnp.where(e < 0.03, series, jnp.log(1.0 + e))


def main_kernel(
    n, half, sig_hbm, map_hbm, dt_hbm, dout_hbm, taps_hbm, bias_hbm, mtaps_hbm, mbias_hbm,
    alog_hbm, dtb_hbm, skip_hbm,
    big, total, ddt_ref,
    sig_in, map_in, dout_ref, dt_in, dt_got, taps_ref, bias_ref, mtaps_ref, mbias_ref,
    alog_ref, dtb_ref, skip_ref, tail_own, tail_got, tap_row, gtaps_ref,
    pad, slope, signal_ref, scaled_ref, weighted_ref, sgrad_ref, imap_ref, omap_ref, wide3, intra,
    oh, gw, drow, xs, gs, es, xr, gr, er, yh, yc, lh, lc, first_local, second_sg, lk,
    mg, mgot, gpad, rims, swap, ddt_mine, ddt_got, part, parts, mine_sum,
    l_sem, n_send, n_recv, b_send, b_recv, tap_send, tap_recv,
    xs_sem, xr_sem, gs_sem, gr_sem, es_sem, er_sem, hs_sem, hr_sem, cs_sem, cr_sem,
    ms_sem, mr_sem, r_sem, w_sem, ps_sem, pr_sem, ts_sem, tr_sem
):
    me = lax.axis_index("ctx")
    f = lax.axis_index("fsdp")
    odd = lax.rem(me, 2)
    mate = me + 1 - 2 * odd
    side_ctx = lax.rem(me + n - 1 + 2 * odd, n)
    slot = f // half
    first = 2 * (f - slot * half)
    group = f // 2
    side = f - 2 * group
    share = SIG // n
    per_head = n // HERE
    kept = pl.multiple_of(odd * BLK, BLK)
    given = pl.multiple_of((1 - odd) * BLK, BLK)
    ending = pl.multiple_of((1 - odd) * BLK + BLK - EDGE, EDGE)
    starts = (group, GROUPS + group, f)
    barrier = pltpu.get_barrier_semaphore()

    def fetch(i, src, dst):
        copy = pltpu.make_async_copy(src, dst, l_sem.at[i])
        copy.start()
        return copy

    def third(k):
        return slice(k * STATE, (k + 1) * STATE)

    local = [
        fetch(0, mtaps_hbm, mtaps_ref),
        fetch(1, mbias_hbm, mbias_ref),
        fetch(2, dt_hbm, dt_in),
        fetch(3, alog_hbm, alog_ref),
        fetch(4, dtb_hbm, dtb_ref),
        fetch(5, skip_hbm, skip_ref),
        fetch(6, taps_hbm, taps_ref),
        fetch(7, bias_hbm, bias_ref),
        fetch(8, sig_hbm.at[pl.ds(kept, BLK)], sig_in.at[0:BLK]),
        fetch(9, dout_hbm.at[pl.ds(kept, BLK)], dout_ref.at[0:BLK]),
        fetch(10, sig_hbm.at[pl.ds(ending, EDGE)], tail_own.at[:, 0:SIG]),
    ]
    for k, start in enumerate(starts):
        local.append(
            fetch(
                11 + k,
                map_hbm.at[pl.ds(kept, BLK), columns(start)],
                map_in.at[0:BLK, third(k)],
            )
        )
        local.append(
            fetch(
                14 + k,
                map_hbm.at[pl.ds(ending, EDGE), columns(start)],
                tail_own.at[:, SIG + k * STATE : SIG + (k + 1) * STATE],
            )
        )

    def greet(i, _):
        signal(barrier, ctx=other(me, i, n))
        return 0

    lax.fori_loop(1, n, greet, 0)
    for k in range(2):

        @pl.when(group + k * half != f)
        def _():
            signal(barrier, fsdp=group + k * half)

        @pl.when(first + k != f)
        def _():
            signal(barrier, fsdp=first + k)

    for copy in local:
        copy.wait()
    tap_row[0:KSIZE] = mtaps_ref[...]
    tap_row[KSIZE : KSIZE + 1] = mbias_ref[...]
    tap_row[KSIZE + 1 :] = jnp.zeros((8 - KSIZE - 1, STATE), F32)
    selves = jnp.where(group == f, 1, 0) + jnp.where(group + half == f, 1, 0)
    pl.semaphore_wait(barrier, n - 1 + 4 - 2 * selves)

    for k in range(2):

        @pl.when(first + k != f)
        def _():
            remote(
                tap_row, gtaps_ref.at[slot], tap_send.at[k], tap_recv.at[slot], fsdp=first + k
            ).start()

        @pl.when(group + k * half == f)
        def _():
            gtaps_ref[k] = tap_row[...]

    def to_mate(i, src, dst):
        copy = remote(src, dst, n_send.at[i], n_recv.at[i], ctx=mate)
        copy.start()
        return copy

    def to_side(i, dst_cols):
        copy = remote(
            tail_own.at[:, dst_cols], tail_got.at[:, dst_cols], b_send.at[i], b_recv.at[i],
            ctx=side_ctx,
        )
        copy.start()
        return copy

    dt_copy = to_mate(0, dt_hbm, dt_got)
    tail_copy = to_side(0, slice(0, WIDE))
    map_copies = [
        to_mate(
            1 + k, map_hbm.at[pl.ds(given, BLK), columns(start)], map_in.at[BLK:ROWS, third(k)]
        )
        for k, start in enumerate(starts)
    ]
    sig_copy = to_mate(4, sig_hbm.at[pl.ds(given, BLK)], sig_in.at[BLK:ROWS])
    dout_copy = to_mate(5, dout_hbm.at[pl.ds(given, BLK)], dout_ref.at[BLK:ROWS])

    lane = lax.broadcasted_iota(jnp.int32, (HERE, ROWS), 1)
    row_id = lax.broadcasted_iota(jnp.int32, (ROWS, ROWS), 0)
    col_id = lax.broadcasted_iota(jnp.int32, (ROWS, ROWS), 1)
    lower = ((row_id >= BLK) == (col_id >= BLK)) & (col_id <= row_id)
    lower_f = jnp.where(lower, 1.0, 0.0).astype(F32)
    eye = jnp.where(row_id == col_id, 1.0, 0.0).astype(F32)
    eye8 = eye[:HERE, :HERE]
    ones8 = jnp.ones((HERE, ROWS), F32)
    head3 = lax.broadcasted_iota(jnp.int32, (3 * HERE, 3 * SIG), 0)
    spread3 = jnp.where(
        lax.broadcasted_iota(jnp.int32, (3 * HERE, 3 * SIG), 1) // HDIM == head3, 1.0, 0.0
    ).astype(F32)
    spread1 = spread3[:HERE, :SIG]

    def in_rows(ref):
        return nt(eye8, jnp.broadcast_to(ref[...], (ROWS, HERE)), HIGH)

    def per_row(y):
        return nt(spread1, y, HIGH)

    def turned(x):
        return pltpu.roll(x, BLK, 1)

    def preact(r, rows, cols, taps, bias):
        acc = bias
        for k in range(KSIZE):
            start = EDGE - RIM + k + r
            acc = acc + taps[k : k + 1] * pad[start : start + rows, cols]
        return acc

    def sig_rows(r, count):
        rows = slice(r, r + count)
        for q in range(SIG // STATE):
            cols = third(q)
            v = preact(r, count, cols, taps_ref[:, cols], bias_ref[:, cols])
            s = sigmoid(v)
            slope[rows, cols] = s * (1.0 + v * (1.0 - s))
            signal_ref[rows, cols] = (v * s).astype(BF16)

    pad[EDGE : EDGE + BLK, :SIG] = sig_in[:BLK, :].astype(F32)
    pad[EDGE : EDGE + BLK, SIG:] = map_in[:BLK, :].astype(F32)
    sig_rows(EDGE, BLK - EDGE)
    dt_copy.wait()
    own, got = dt_in[...], dt_got[...]
    own = jnp.where(odd == 0, own, turned(own))
    got = jnp.where(odd == 0, turned(got), got)
    logits = jnp.where(lane < BLK, own, got) + in_rows(dtb_ref)
    rate = -jnp.exp(in_rows(alog_ref))
    step = jnp.maximum(logits, 0.0) + log1p_small(jnp.exp(-jnp.abs(logits)))
    ds = nt(step * rate, lower_f, HIGH)
    end_low = jnp.exp(ds[:, BLK - 1 : BLK])
    end_high = jnp.exp(ds[:, ROWS - 1 : ROWS])
    end = jnp.where(lane < BLK, ds[:, BLK - 1 : BLK], ds[:, ROWS - 1 : ROWS])
    to_end = jnp.exp(end - ds)
    col4 = nt(eye, jnp.concatenate([step, to_end, jnp.exp(ds), ds], axis=0), HIGH)
    ds_col = col4[:, 3 * HERE :]
    wide3[...] = nn(col4[:, : 3 * HERE], spread3, HIGH)
    end_low8 = jnp.broadcast_to(end_low, (HERE, STATE))
    end_high8 = jnp.broadcast_to(end_high, (HERE, STATE))
    both_ends = end_low8 * end_high8
    for h in range(HERE):
        es[h] = both_ends[h : h + 1]

    for k in range(2):

        @pl.when(group + k * half != f)
        def _():
            remote(
                tap_row, gtaps_ref.at[k], tap_send.at[k], tap_recv.at[k], fsdp=group + k * half
            ).wait_recv()

        @pl.when(first + k != f)
        def _():
            remote(
                tap_row, gtaps_ref.at[slot], tap_send.at[k], tap_recv.at[slot], fsdp=first + k
            ).wait_send()

    tail_copy.wait()
    for copy in map_copies:
        copy.wait()
    keep = jnp.where(me == 0, 0.0, 1.0).astype(F32)
    before = jnp.where(me == n - 1, tail_own[...].astype(F32), tail_got[...].astype(F32))
    pad[:EDGE] = before * keep
    pad[EDGE + BLK :, SIG:] = map_in[BLK:, :].astype(F32)
    for k, out in enumerate((imap_ref, omap_ref)):
        cols = slice(SIG + k * STATE, SIG + (k + 1) * STATE)
        v = preact(0, ROWS, cols, gtaps_ref[k, :KSIZE], gtaps_ref[k, KSIZE : KSIZE + 1])
        out[...] = (v * sigmoid(v)).astype(BF16)
    v = preact(0, ROWS, slice(SIG + 2 * STATE, WIDE), mtaps_ref[...], mbias_ref[...])
    s = sigmoid(v)
    slope[:, SIG:] = s * (1.0 + v * (1.0 - s))
    sig_copy.wait()
    pad[EDGE + BLK :, :SIG] = sig_in[BLK:, :].astype(F32)
    sig_rows(0, EDGE)
    sig_rows(BLK, BLK)
    dout_copy.wait()
    for q in range(SIG // STATE):
        cols = third(q)
        cols2 = slice(SIG + q * STATE, SIG + (q + 1) * STATE)
        cols3 = slice(2 * SIG + q * STATE, 2 * SIG + (q + 1) * STATE)
        scaled_b = (signal_ref[:, cols].astype(F32) * wide3[:, cols]).astype(BF16)
        scaled_ref[:, cols] = scaled_b
        weighted_ref[:, cols] = (scaled_b.astype(F32) * wide3[:, cols2]).astype(BF16)
        sgrad_ref[:, cols] = (dout_ref[:, cols].astype(F32) * wide3[:, cols3]).astype(BF16)
    low, high = slice(0, BLK), slice(BLK, ROWS)
    second_sg[...] = tn(sgrad_ref[high, :], omap_ref[high, :])
    gs[...] = tn(sgrad_ref[low, :], omap_ref[low, :])
    first_local[...] = tn(weighted_ref[low, :], imap_ref[low, :])
    second_local = tn(weighted_ref[high, :], imap_ref[high, :])
    for h in range(HERE):
        at = slice(h * HDIM, (h + 1) * HDIM)
        gs[at, :] = gs[at, :] + end_low8[h : h + 1] * second_sg[at, :]
        xs[at, :] = (end_high8[h : h + 1] * first_local[at, :] + second_local[at, :]).astype(BF16)

    def mine(d):
        return pl.ds(pl.multiple_of(d * share, share), share)

    def x_copy(d):
        return remote(xs.at[mine(d)], xr.at[me], xs_sem.at[d], xr_sem.at[me], ctx=d)

    def g_copy(d):
        return remote(gs.at[mine(d)], gr.at[me], gs_sem.at[d], gr_sem.at[me], ctx=d)

    def e_copy(d):
        return remote(es.at[d // per_head], er.at[me], es_sem.at[d], er_sem.at[me], ctx=d)

    def h_copy(d):
        return remote(yh.at[d], lh.at[mine(me)], hs_sem.at[d], hr_sem.at[me], ctx=d)

    def c_copy(d):
        return remote(yc.at[d], lc.at[mine(me)], cs_sem.at[d], cr_sem.at[me], ctx=d)

    def send(i, _):
        d = other(me, i, n)
        g_copy(d).start()
        x_copy(d).start()
        e_copy(d).start()
        return 0

    lax.fori_loop(1, n, send, 0)
    xr[me] = xs[mine(me)]
    gr[me] = gs[mine(me)]
    er[me] = es[me // per_head]

    score = nt(omap_ref[...], imap_ref[...])
    lane_row = lax.broadcasted_iota(jnp.int32, (ROWS, STATE), 1)
    grad_score = jnp.zeros((ROWS, ROWS), F32)
    for q in range(HERE // 2):
        cols = third(q)
        d_pair = dout_ref[:, cols].astype(F32)
        d_two = jnp.concatenate(
            [jnp.where(lane_row < HDIM, d_pair, 0.0), jnp.where(lane_row < HDIM, 0.0, d_pair)],
            axis=0,
        ).astype(BF16)
        grad_mix2 = nt(d_two, scaled_ref[:, cols])
        mixes = []
        for k in range(2):
            h = 2 * q + k
            grad_mix = grad_mix2[k * ROWS : (k + 1) * ROWS]
            gap = jnp.minimum(ds_col[:, h : h + 1] - ds[h : h + 1, :], 0.0)
            decay = jnp.where(lower, jnp.exp(gap), 0.0)
            mix = score * decay
            mixes.append(mix.astype(BF16))
            grad_score = grad_score + grad_mix * decay
            product = grad_mix * mix
            drow[h : h + 1, :] = nt(ones8, product, HIGH)[0:1] - jnp.sum(
                product, axis=0, keepdims=True
            )
        intra[:, cols] = tn(jnp.concatenate(mixes, axis=0), d_two)
    grad_score = grad_score.astype(BF16)
    mg[0] = tn(grad_score, omap_ref[...])
    mg[1] = nn(grad_score, imap_ref[...])

    def arrived(i, _):
        s = other(me, i, n)
        remote(es.at[s // per_head], er.at[s], es_sem.at[s], er_sem.at[s], ctx=s).wait_recv()
        remote(xs.at[mine(s)], xr.at[s], xs_sem.at[s], xr_sem.at[s], ctx=s).wait_recv()
        remote(gs.at[mine(s)], gr.at[s], gs_sem.at[s], gr_sem.at[s], ctx=s).wait_recv()
        return 0

    lax.fori_loop(1, n, arrived, 0)
    zero = jnp.zeros((share, STATE), F32)

    def holder(i):
        return jnp.where(i < n // 2, 2 * i, 2 * (n - 1 - i) + 1)

    def chain(i, state):
        h, g = state
        up, down = holder(i), holder(n - 1 - i)
        yh[up] = h.astype(BF16)
        yc[down] = g
        h = er[up] * h + xr[up].astype(F32)
        g = er[down] * g + gr[down]
        return h, g

    lax.fori_loop(0, n, chain, (zero, zero))

    def back(i, _):
        d = other(me, i, n)
        c_copy(d).start()
        h_copy(d).start()
        return 0

    lax.fori_loop(1, n, back, 0)
    lh[mine(me)] = yh[me]
    lc[mine(me)] = yc[me]

    def linked(i, _):
        d = other(me, i, n)
        g_copy(d).wait_send()
        x_copy(d).wait_send()
        e_copy(d).wait_send()
        remote(yh.at[d], lh.at[mine(d)], hs_sem.at[d], hr_sem.at[d], ctx=d).wait_recv()
        remote(yc.at[d], lc.at[mine(d)], cs_sem.at[d], cr_sem.at[d], ctx=d).wait_recv()
        return 0

    lax.fori_loop(1, n, linked, 0)
    lk[0] = lh[...]
    lk[3] = lc[...].astype(BF16)
    for h in range(HERE):
        at = slice(h * HDIM, (h + 1) * HDIM)
        lk[1, at, :] = (end_low8[h : h + 1] * lh[at, :].astype(F32) + first_local[at, :]).astype(
            BF16
        )
        lk[2, at, :] = (second_sg[at, :] + end_high8[h : h + 1] * lc[at, :]).astype(BF16)

    for b, rows in enumerate((low, high)):
        mg[0, rows, :] = mg[0, rows, :] + nn(weighted_ref[rows, :], lk[2 + b])
        mg[1, rows, :] = mg[1, rows, :] + nn(sgrad_ref[rows, :], lk[b])

    def m_copy(k):
        return remote(
            mg.at[k], mgot.at[side], ms_sem.at[k], mr_sem.at[side], fsdp=group + k * half
        )

    for k in range(2):

        @pl.when(group + k * half != f)
        def _():
            m_copy(k).start()

        @pl.when(group + k * half == f)
        def _():
            mgot[side] = mg[k]

    end_terms = []
    for b, rows in enumerate((low, high)):
        oh[rows, :] = nt(omap_ref[rows, :], lk[b])
        gw[rows, :] = nt(imap_ref[rows, :], lk[2 + b])
        both = lk[b].astype(F32) * lk[2 + b].astype(F32)
        both = jnp.sum(both.reshape(HERE, HDIM, STATE), axis=1)
        end_terms.append(jnp.sum(both, axis=1, keepdims=True))
    step_w = wide3[:, :SIG]
    end_w = wide3[:, SIG : 2 * SIG]
    exp_w = wide3[:, 2 * SIG :]
    d_f = dout_ref[...].astype(F32)
    signal_f = signal_ref[...].astype(F32)
    gw_v = gw[...]
    back_row = per_row(gw_v * scaled_ref[...].astype(F32)) * to_end
    grad_sum = per_row(d_f * exp_w * oh[...]) - back_row + drow[...]
    back_low = jnp.sum(jnp.where(lane < BLK, back_row, 0.0), axis=1, keepdims=True)
    back_high = jnp.sum(jnp.where(lane < BLK, 0.0, back_row), axis=1, keepdims=True)
    last_low = back_low + end_low * end_terms[0]
    last_high = back_high + end_high * end_terms[1]
    grad_sum = grad_sum + jnp.where(
        lane == BLK - 1, last_low, jnp.where(lane == ROWS - 1, last_high, 0.0)
    )
    grad_log = nn(grad_sum, lower_f, HIGH)
    grad_scaled = gw_v * end_w + intra[...]
    grad_step = grad_log * rate + per_row(grad_scaled * signal_f)
    grad_dt = grad_step * sigmoid(logits)
    ddt_mine[...] = grad_dt
    ddt_copy = remote(ddt_mine, ddt_got, w_sem.at[0], w_sem.at[1], ctx=mate)
    ddt_copy.start()
    skip_w = nn(jnp.broadcast_to(skip_ref[...], (HERE, HERE)), spread1, HIGH)[0:1]
    gpad[:ROWS, :SIG] = (skip_w * d_f + grad_scaled * step_w) * slope[:, :SIG]
    part[TAIL + 3 :] = jnp.zeros((n - TAIL - 3, 1, STATE), F32)

    def small(at, row):
        part[at] = jnp.concatenate([row, jnp.zeros((1, STATE - HERE), F32)], axis=1)

    small(TAIL, nt(ones8, grad_log * step, HIGH)[0:1] * (-jnp.exp(alog_ref[...])))
    small(TAIL + 1, nt(ones8, grad_dt, HIGH)[0:1])
    small(TAIL + 2, nt(ones8, per_row(d_f * signal_f), HIGH)[0:1])

    def sums(cols, source, at):
        g = gpad[:ROWS, cols]
        for k in range(KSIZE):
            start = EDGE - RIM + k
            part[k * (OWN // STATE) + at] = jnp.sum(
                g * pad[start : start + ROWS, source], axis=0, keepdims=True
            )
        part[KSIZE * (OWN // STATE) + at] = jnp.sum(g, axis=0, keepdims=True)

    for q in range(SIG // STATE):
        sums(third(q), third(q), q)

    for k in range(2):

        @pl.when(first + k != f)
        def _():
            remote(
                mg.at[k], mgot.at[k], ms_sem.at[k], mr_sem.at[k], fsdp=first + k
            ).wait_recv()

    gpad[:ROWS, SIG:] = (mgot[0] + mgot[1]) * slope[:, SIG:]
    earlier = jnp.where(
        odd == 0, lax.rem(me + n - 2, n), jnp.where(me == n - 1, n - 2, lax.rem(me + 2, n))
    )
    earlier = jnp.where(me == 0, 1, earlier)
    rim_copy = remote(gpad.at[0:RIMS], rims, r_sem.at[0], r_sem.at[1], ctx=earlier)
    rim_copy.start()
    sums(slice(SIG, OWN), slice(SIG + 2 * STATE, WIDE), SIG // STATE)

    def p_copy(d):
        return remote(part.at[d], parts.at[me], ps_sem.at[d], pr_sem.at[me], ctx=d)

    def t_copy(d):
        return remote(mine_sum, total.at[me], ts_sem.at[d], tr_sem.at[me], ctx=d)

    def send_part(i, _):
        p_copy(other(me, i, n)).start()
        return 0

    lax.fori_loop(1, n, send_part, 0)
    parts[me] = part[me]

    rim_copy.wait()
    gpad[ROWS:] = jnp.where(me == 1, 0.0, rims[...])

    def raw(r):
        out = []
        for taps, cols in ((taps_ref, slice(0, SIG)), (mtaps_ref, slice(SIG, OWN))):
            acc = taps[RIM : RIM + 1] * gpad[r : r + BLK, cols]
            for k in range(RIM):
                acc = acc + taps[k : k + 1] * gpad[r + RIM - k : r + RIM - k + BLK, cols]
            out.append(acc)
        return jnp.concatenate(out, axis=1)

    swap[...] = raw(BLK)
    swap_copy = remote(swap, big.at[pl.ds(kept, BLK)], w_sem.at[2], w_sem.at[3], ctx=mate)
    swap_copy.start()

    def part_in(i, _):
        s = other(me, i, n)
        remote(part.at[s], parts.at[s], ps_sem.at[s], pr_sem.at[s], ctx=s).wait_recv()
        return 0

    lax.fori_loop(1, n, part_in, 0)
    mine_sum[...] = jnp.sum(parts[...], axis=0)

    def send_total(i, _):
        t_copy(other(me, i, n)).start()
        return 0

    lax.fori_loop(1, n, send_total, 0)
    total[me] = mine_sum[...]
    big[pl.ds(kept, BLK)] = raw(0)
    ddt_copy.wait()
    own, got = ddt_mine[...], ddt_got[...]
    ddt_low = jnp.where(odd == 0, own, turned(got))
    ddt_high = jnp.where(odd == 0, got, turned(own))
    ddt_ref[...] = jnp.where(lane < BLK, ddt_low, ddt_high)

    def done(i, _):
        d = other(me, i, n)
        h_copy(d).wait_send()
        c_copy(d).wait_send()
        p_copy(d).wait_send()
        t_copy(d).wait_send()
        remote(mine_sum, total.at[d], ts_sem.at[d], tr_sem.at[d], ctx=d).wait_recv()
        return 0

    lax.fori_loop(1, n, done, 0)
    for k in range(2):

        @pl.when(group + k * half != f)
        def _():
            m_copy(k).wait_send()

    swap_copy.wait()


def main(*operands):
    n = lax.axis_size("ctx")
    half = lax.axis_size("fsdp") // 2
    share = SIG // n
    dma = pltpu.SemaphoreType.DMA
    vm = pltpu.VMEM
    return pl.pallas_call(
        functools.partial(main_kernel, n, half),
        out_shape=(
            jax.ShapeDtypeStruct((ROWS, OWN), F32),
            jax.ShapeDtypeStruct((n, 1, STATE), F32),
            jax.ShapeDtypeStruct((HERE, ROWS), F32),
        ),
        in_specs=[pl.BlockSpec(memory_space=pl.ANY)] * len(operands),
        out_specs=(VM,) * 3,
        scratch_shapes=[
            vm((ROWS, SIG), BF16),
            vm((ROWS, 3 * STATE), BF16),
            vm((ROWS, SIG), BF16),
            vm((HERE, ROWS), F32),
            vm((HERE, ROWS), F32),
            vm((KSIZE, SIG), F32),
            vm((1, SIG), F32),
            vm((KSIZE, STATE), F32),
            vm((1, STATE), F32),
            vm((1, HERE), F32),
            vm((1, HERE), F32),
            vm((1, HERE), F32),
            vm((EDGE, WIDE), BF16),
            vm((EDGE, WIDE), BF16),
            vm((8, STATE), F32),
            vm((2, 8, STATE), F32),
            vm((EDGE + ROWS, WIDE), F32),
            vm((ROWS, OWN), F32),
            vm((ROWS, SIG), BF16),
            vm((ROWS, SIG), BF16),
            vm((ROWS, SIG), BF16),
            vm((ROWS, SIG), BF16),
            vm((ROWS, STATE), BF16),
            vm((ROWS, STATE), BF16),
            vm((ROWS, 3 * SIG), F32),
            vm((ROWS, SIG), F32),
            vm((ROWS, SIG), F32),
            vm((ROWS, SIG), F32),
            vm((HERE, ROWS), F32),
            vm((SIG, STATE), BF16),
            vm((SIG, STATE), F32),
            vm((HERE, 1, STATE), F32),
            vm((n, share, STATE), BF16),
            vm((n, share, STATE), F32),
            vm((n, 1, STATE), F32),
            vm((n, share, STATE), BF16),
            vm((n, share, STATE), F32),
            vm((SIG, STATE), BF16),
            vm((SIG, STATE), F32),
            vm((SIG, STATE), F32),
            vm((SIG, STATE), F32),
            vm((4, SIG, STATE), BF16),
            vm((2, ROWS, STATE), F32),
            vm((2, ROWS, STATE), F32),
            vm((ROWS + RIMS, OWN), F32),
            vm((RIMS, OWN), F32),
            vm((BLK, OWN), F32),
            vm((HERE, ROWS), F32),
            vm((HERE, ROWS), F32),
            vm((n, 1, STATE), F32),
            vm((n, 1, STATE), F32),
            vm((1, STATE), F32),
        ]
        + [dma((17,)), dma((6,)), dma((6,)), dma((1,)), dma((1,)), dma((2,)), dma((2,))]
        + [dma((n,))] * 10
        + [dma((2,)), dma((2,)), dma((2,)), dma((4,))]
        + [dma((n,))] * 4,
        compiler_params=pltpu.CompilerParams(
            collective_id=0, has_side_effects=True, vmem_limit_bytes=56 * 1024 * 1024
        ),
        name="main",
    )(*operands)


def last_kernel(
    scale, big, total, ddt,
    dsig, dmap, ddt_out, dtaps, dmtaps, dbias, dmbias, dalog, ddtb, dskip
):
    dsig[...] = big[:, :SIG]
    dmap[...] = big[:, SIG:]
    ddt_out[...] = ddt[...]
    for k in range(KSIZE + 1):
        for q in range(OWN // STATE):
            row = total[k * (OWN // STATE) + q] * scale
            cols = slice(q * STATE, (q + 1) * STATE)
            if q < SIG // STATE:
                if k < KSIZE:
                    dtaps[k : k + 1, cols] = row
                else:
                    dbias[:, cols] = row
            elif k < KSIZE:
                dmtaps[k : k + 1, :] = row
            else:
                dmbias[...] = row
    for k, out in enumerate((dalog, ddtb, dskip)):
        out[...] = total[TAIL + k][:, :HERE] * scale


def last(*operands):
    scale = 1.0 / math.sqrt(float(lax.axis_size("ctx") * ROWS))
    shapes = (
        (ROWS, SIG), (ROWS, STATE), (HERE, ROWS), (KSIZE, SIG), (KSIZE, STATE),
        (1, SIG), (1, STATE), (1, HERE), (1, HERE), (1, HERE),
    )
    return pl.pallas_call(
        functools.partial(last_kernel, scale),
        out_shape=tuple(jax.ShapeDtypeStruct(s, F32) for s in shapes),
        in_specs=[VM] * 3,
        out_specs=(VM,) * len(shapes),
        compiler_params=pltpu.CompilerParams(vmem_limit_bytes=8 * 1024 * 1024),
        name="last",
    )(*operands)


def shards(
    sig_raw,
    map_raw,
    step_size_logits,
    d_out,
    sig_taps,
    map_taps,
    sig_bias,
    map_bias,
    a_log,
    dt_bias,
    skip_gain,
):
    found = main(
        sig_raw, map_raw, step_size_logits.T, d_out, sig_taps, sig_bias[None, :], map_taps,
        map_bias[None, :], a_log[None, :], dt_bias[None, :], skip_gain[None, :],
    )
    out = last(*found)
    return out[:2] + (out[2].T,) + out[3:5] + tuple(a.reshape(-1) for a in out[5:])


def solution(mesh):
    return jax.shard_map(
        shards,
        mesh=mesh,
        in_specs=(
            P("ctx", "fsdp"),
            P("ctx", None),
            P("ctx", "fsdp"),
            P("ctx", "fsdp"),
            P(None, "fsdp"),
            P(None, "fsdp"),
            P("fsdp"),
            P("fsdp"),
            P("fsdp"),
            P("fsdp"),
            P("fsdp"),
        ),
        out_specs=(
            P("ctx", "fsdp"),
            P("ctx", "fsdp"),
            P("ctx", "fsdp"),
            P(None, "fsdp"),
            P(None, "fsdp"),
            P("fsdp"),
            P("fsdp"),
            P("fsdp"),
            P("fsdp"),
            P("fsdp"),
        ),
        check_vma=False,
    )
```

time: 123 us -> 92.3 us (0.75)
  the two profiles are of different devices: /device:TPU:26 before, /device:TPU:4 now
where the time goes in v3:
time: 92.3 us; the launch traced here: 92 us
  Pallas kernels  89 us (96%)
  local copies, waits for them, and re-layouts  2.36 us (3%)
    pallas_call x1, Pallas kernels, main(): pl.pallas_call(functools.partial(main_kernel, n, half), out_shape=(jax.Sh...  88.2 us
    unnamed x6, local copies, waits for them, and re-layouts  2.36 us

profile of v3, /device:TPU:4, one launch (start us, length us, event | category | flops | bytes accessed | tf_op | source)
XLA Modules:
  0.0 92.0 jit_solution(10517695437287500064)
XLA Ops:
  0.6 88.2 %main.1 = (f32[128,640]{1,0:T(8,128)}, f32[32,1,128]{2,1,0:T(1,128)}, f32[8,128]{1,0:T(8,128)}) custom-call(bf16[128,512]{1,0:T(8,128)(2,1)} %sig_hbm.1, bf16[128,2048]{1,0:T(8,128)(2,1)} %map_hbm.1, f32[8,128]{1,0:T(8,128)} %bitcast.12, bf16[128,512]{1,0:T(8,128)(2,1)} %dout_hbm.1, f32[4,512]{1,0:T(4,128)} %taps_hbm.1, f32[1,512]{1,0:T(1,128)} %bitcast.13, ...), custom_call_target="tpu_custom_call" | custom-call | tf_op jit(solution)/shard_map/main/pallas_call | solution.py:599
  88.9 0.0 copy-start.2
  88.9 0.7 copy-done.2
  89.6 0.0 copy-start
  89.6 1.0 %copy-done = f32[128,640]{1,0:T(8,128)S(1)} copy-done((f32[128,640]{1,0:T(8,128)S(1)}, f32[128,640]{1,0:T(8,128)}, u32[]{:S(2)}) %copy-start) | copy-done | bytes 327704
  90.6 0.0 copy-start.1
  90.6 0.7 copy-done.1
  91.3 0.8 last.1
Async XLA Ops:
  88.9 0.7 copy-start.2
  89.6 1.0 %copy-start = (f32[128,640]{1,0:T(8,128)S(1)}, f32[128,640]{1,0:T(8,128)}, u32[]{:S(2)}) copy-start(f32[128,640]{1,0:T(8,128)} %get-tuple-element.23.big) | copy-start | bytes 983044
  90.6 0.7 copy-start.1

commit v4 on v3

--- a/solution.py
+++ b/solution.py
@@ -84,15 +84,16 @@
 def main_kernel(
     n, half, sig_hbm, map_hbm, dt_hbm, dout_hbm, taps_hbm, bias_hbm, mtaps_hbm, mbias_hbm,
     alog_hbm, dtb_hbm, skip_hbm,
-    big, total, ddt_ref,
+    big, total_hbm, ddt_hbm,
     sig_in, map_in, dout_ref, dt_in, dt_got, taps_ref, bias_ref, mtaps_ref, mbias_ref,
     alog_ref, dtb_ref, skip_ref, tail_own, tail_got, tap_row, gtaps_ref,
     pad, slope, signal_ref, scaled_ref, weighted_ref, sgrad_ref, imap_ref, omap_ref, wide3, intra,
     oh, gw, drow, xs, gs, es, xr, gr, er, yh, yc, lh, lc, first_local, second_sg, lk,
-    mg, mgot, gpad, rims, swap, ddt_mine, ddt_got, part, parts, mine_sum,
+    mg, mgot, gpad, rims, swap, stay, ddt_mine, ddt_got, ddt_ref, part, near, far, total,
+    low_part, low_near,
     l_sem, n_send, n_recv, b_send, b_recv, tap_send, tap_recv,
     xs_sem, xr_sem, gs_sem, gr_sem, es_sem, er_sem, hs_sem, hr_sem, cs_sem, cr_sem,
-    ms_sem, mr_sem, r_sem, w_sem, ps_sem, pr_sem, ts_sem, tr_sem
+    ms_sem, mr_sem, r_sem, w_sem, q_send, q_near, q_far
 ):
     me = lax.axis_index("ctx")
     f = lax.axis_index("fsdp")
@@ -269,6 +270,16 @@
     both_ends = end_low8 * end_high8
     for h in range(HERE):
         es[h] = both_ends[h : h + 1]
+
+    def e_copy(d):
+        return remote(es.at[d // per_head], er.at[me], es_sem.at[d], er_sem.at[me], ctx=d)
+
+    def send_ends(i, _):
+        e_copy(other(me, i, n)).start()
+        return 0
+
+    lax.fori_loop(1, n, send_ends, 0)
+    er[me] = es[me // per_head]
 
     for k in range(2):
 
@@ -314,42 +325,42 @@
     low, high = slice(0, BLK), slice(BLK, ROWS)
     second_sg[...] = tn(sgrad_ref[high, :], omap_ref[high, :])
     gs[...] = tn(sgrad_ref[low, :], omap_ref[low, :])
+    for h in range(HERE):
+        at = slice(h * HDIM, (h + 1) * HDIM)
+        gs[at, :] = gs[at, :] + end_low8[h : h + 1] * second_sg[at, :]
+
+    def mine(d):
+        return pl.ds(pl.multiple_of(d * share, share), share)
+
+    def x_copy(d):
+        return remote(xs.at[mine(d)], xr.at[me], xs_sem.at[d], xr_sem.at[me], ctx=d)
+
+    def g_copy(d):
+        return remote(gs.at[mine(d)], gr.at[me], gs_sem.at[d], gr_sem.at[me], ctx=d)
+
+    def h_copy(d):
+        return remote(yh.at[d], lh.at[mine(me)], hs_sem.at[d], hr_sem.at[me], ctx=d)
+
+    def c_copy(d):
+        return remote(yc.at[d], lc.at[mine(me)], cs_sem.at[d], cr_sem.at[me], ctx=d)
+
+    def send_g(i, _):
+        g_copy(other(me, i, n)).start()
+        return 0
+
+    def send_x(i, _):
+        x_copy(other(me, i, n)).start()
+        return 0
+
+    lax.fori_loop(1, n, send_g, 0)
     first_local[...] = tn(weighted_ref[low, :], imap_ref[low, :])
     second_local = tn(weighted_ref[high, :], imap_ref[high, :])
     for h in range(HERE):
         at = slice(h * HDIM, (h + 1) * HDIM)
-        gs[at, :] = gs[at, :] + end_low8[h : h + 1] * second_sg[at, :]
         xs[at, :] = (end_high8[h : h + 1] * first_local[at, :] + second_local[at, :]).astype(BF16)
-
-    def mine(d):
-        return pl.ds(pl.multiple_of(d * share, share), share)
-
-    def x_copy(d):
-        return remote(xs.at[mine(d)], xr.at[me], xs_sem.at[d], xr_sem.at[me], ctx=d)
-
-    def g_copy(d):
-        return remote(gs.at[mine(d)], gr.at[me], gs_sem.at[d], gr_sem.at[me], ctx=d)
-
-    def e_copy(d):
-        return remote(es.at[d // per_head], er.at[me], es_sem.at[d], er_sem.at[me], ctx=d)
-
-    def h_copy(d):
-        return remote(yh.at[d], lh.at[mine(me)], hs_sem.at[d], hr_sem.at[me], ctx=d)
-
-    def c_copy(d):
-        return remote(yc.at[d], lc.at[mine(me)], cs_sem.at[d], cr_sem.at[me], ctx=d)
-
-    def send(i, _):
-        d = other(me, i, n)
-        g_copy(d).start()
-        x_copy(d).start()
-        e_copy(d).start()
-        return 0
-
-    lax.fori_loop(1, n, send, 0)
+    lax.fori_loop(1, n, send_x, 0)
     xr[me] = xs[mine(me)]
     gr[me] = gs[mine(me)]
-    er[me] = es[me // per_head]
 
     score = nt(omap_ref[...], imap_ref[...])
     lane_row = lax.broadcasted_iota(jnp.int32, (ROWS, STATE), 1)
@@ -380,129 +391,150 @@
     mg[0] = tn(grad_score, omap_ref[...])
     mg[1] = nn(grad_score, imap_ref[...])
 
-    def arrived(i, _):
+    def holder(i):
+        return jnp.where(i < n // 2, 2 * i, 2 * (n - 1 - i) + 1)
+
+    zero = jnp.zeros((share, STATE), F32)
+
+    def g_arrived(i, _):
         s = other(me, i, n)
         remote(es.at[s // per_head], er.at[s], es_sem.at[s], er_sem.at[s], ctx=s).wait_recv()
+        remote(gs.at[mine(s)], gr.at[s], gs_sem.at[s], gr_sem.at[s], ctx=s).wait_recv()
+        return 0
+
+    def to_front(i, g):
+        at = holder(n - 1 - i)
+        yc[at] = g
+        return er[at] * g + gr[at]
+
+    def send_c(i, _):
+        c_copy(other(me, i, n)).start()
+        return 0
+
+    def x_arrived(i, _):
+        s = other(me, i, n)
         remote(xs.at[mine(s)], xr.at[s], xs_sem.at[s], xr_sem.at[s], ctx=s).wait_recv()
-        remote(gs.at[mine(s)], gr.at[s], gs_sem.at[s], gr_sem.at[s], ctx=s).wait_recv()
-        return 0
-
-    lax.fori_loop(1, n, arrived, 0)
-    zero = jnp.zeros((share, STATE), F32)
-
-    def holder(i):
-        return jnp.where(i < n // 2, 2 * i, 2 * (n - 1 - i) + 1)
-
-    def chain(i, state):
-        h, g = state
-        up, down = holder(i), holder(n - 1 - i)
-        yh[up] = h.astype(BF16)
-        yc[down] = g
-        h = er[up] * h + xr[up].astype(F32)
-        g = er[down] * g + gr[down]
-        return h, g
-
-    lax.fori_loop(0, n, chain, (zero, zero))
-
-    def back(i, _):
-        d = other(me, i, n)
-        c_copy(d).start()
-        h_copy(d).start()
-        return 0
-
-    lax.fori_loop(1, n, back, 0)
+        return 0
+
+    def to_back(i, h):
+        at = holder(i)
+        yh[at] = h.astype(BF16)
+        return er[at] * h + xr[at].astype(F32)
+
+    def send_h(i, _):
+        h_copy(other(me, i, n)).start()
+        return 0
+
+    lax.fori_loop(1, n, g_arrived, 0)
+    lax.fori_loop(0, n, to_front, zero)
+    lax.fori_loop(1, n, send_c, 0)
+    lax.fori_loop(1, n, x_arrived, 0)
+    lax.fori_loop(0, n, to_back, zero)
+    lax.fori_loop(1, n, send_h, 0)
     lh[mine(me)] = yh[me]
     lc[mine(me)] = yc[me]
-
-    def linked(i, _):
+    step_w = wide3[:, :SIG]
+    end_w = wide3[:, SIG : 2 * SIG]
+    exp_w = wide3[:, 2 * SIG :]
+    d_f = dout_ref[...].astype(F32)
+    signal_f = signal_ref[...].astype(F32)
+    skip_w = nn(jnp.broadcast_to(skip_ref[...], (HERE, HERE)), spread1, HIGH)[0:1]
+    part[TAIL + 3 :] = jnp.zeros((n - TAIL - 3, STATE), F32)
+
+    def small(at, row):
+        part[at : at + 1] = jnp.concatenate([row, jnp.zeros((1, STATE - HERE), F32)], axis=1)
+
+    small(TAIL + 2, nt(ones8, per_row(d_f * signal_f), HIGH)[0:1])
+
+    def m_copy(k):
+        return remote(
+            mg.at[k], mgot.at[side], ms_sem.at[k], mr_sem.at[side], fsdp=group + k * half
+        )
+
+    def to_owner(k):
+        @pl.when(group + k * half != f)
+        def _():
+            m_copy(k).start()
+
+        @pl.when(group + k * half == f)
+        def _():
+            mgot[side] = mg[k]
+
+    def c_in(i, _):
         d = other(me, i, n)
         g_copy(d).wait_send()
+        e_copy(d).wait_send()
+        remote(yc.at[d], lc.at[mine(d)], cs_sem.at[d], cr_sem.at[d], ctx=d).wait_recv()
+        return 0
+
+    lax.fori_loop(1, n, c_in, 0)
+    lk[3] = lc[...].astype(BF16)
+    for h in range(HERE):
+        at = slice(h * HDIM, (h + 1) * HDIM)
+        lk[2, at, :] = (second_sg[at, :] + end_high8[h : h + 1] * lc[at, :]).astype(BF16)
+    for b, rows in enumerate((low, high)):
+        mg[0, rows, :] = mg[0, rows, :] + nn(weighted_ref[rows, :], lk[2 + b])
+    to_owner(0)
+    for b, rows in enumerate((low, high)):
+        gw[rows, :] = nt(imap_ref[rows, :], lk[2 + b])
+    gw_v = gw[...]
+    back_row = per_row(gw_v * scaled_ref[...].astype(F32)) * to_end
+    back_low = jnp.sum(jnp.where(lane < BLK, back_row, 0.0), axis=1, keepdims=True)
+    back_high = jnp.sum(jnp.where(lane < BLK, 0.0, back_row), axis=1, keepdims=True)
+    grad_scaled = gw_v * end_w + intra[...]
+    own_step = per_row(grad_scaled * signal_f)
+    gpad[:ROWS, :SIG] = (skip_w * d_f + grad_scaled * step_w) * slope[:, :SIG]
+
+    def sums(cols, source, at):
+        g = gpad[:ROWS, cols]
+        for k in range(KSIZE):
+            start = EDGE - RIM + k
+            row = k * (OWN // STATE) + at
+            part[row : row + 1] = jnp.sum(
+                g * pad[start : start + ROWS, source], axis=0, keepdims=True
+            )
+        row = KSIZE * (OWN // STATE) + at
+        part[row : row + 1] = jnp.sum(g, axis=0, keepdims=True)
+
+    for q in range(SIG // STATE):
+        sums(third(q), third(q), q)
+
+    def h_in(i, _):
+        d = other(me, i, n)
         x_copy(d).wait_send()
-        e_copy(d).wait_send()
         remote(yh.at[d], lh.at[mine(d)], hs_sem.at[d], hr_sem.at[d], ctx=d).wait_recv()
-        remote(yc.at[d], lc.at[mine(d)], cs_sem.at[d], cr_sem.at[d], ctx=d).wait_recv()
-        return 0
-
-    lax.fori_loop(1, n, linked, 0)
+        return 0
+
+    lax.fori_loop(1, n, h_in, 0)
     lk[0] = lh[...]
-    lk[3] = lc[...].astype(BF16)
     for h in range(HERE):
         at = slice(h * HDIM, (h + 1) * HDIM)
         lk[1, at, :] = (end_low8[h : h + 1] * lh[at, :].astype(F32) + first_local[at, :]).astype(
             BF16
         )
-        lk[2, at, :] = (second_sg[at, :] + end_high8[h : h + 1] * lc[at, :]).astype(BF16)
-
     for b, rows in enumerate((low, high)):
-        mg[0, rows, :] = mg[0, rows, :] + nn(weighted_ref[rows, :], lk[2 + b])
         mg[1, rows, :] = mg[1, rows, :] + nn(sgrad_ref[rows, :], lk[b])
-
-    def m_copy(k):
-        return remote(
-            mg.at[k], mgot.at[side], ms_sem.at[k], mr_sem.at[side], fsdp=group + k * half
-        )
-
-    for k in range(2):
-
-        @pl.when(group + k * half != f)
-        def _():
-            m_copy(k).start()
-
-        @pl.when(group + k * half == f)
-        def _():
-            mgot[side] = mg[k]
-
+    to_owner(1)
     end_terms = []
     for b, rows in enumerate((low, high)):
         oh[rows, :] = nt(omap_ref[rows, :], lk[b])
-        gw[rows, :] = nt(imap_ref[rows, :], lk[2 + b])
         both = lk[b].astype(F32) * lk[2 + b].astype(F32)
         both = jnp.sum(both.reshape(HERE, HDIM, STATE), axis=1)
         end_terms.append(jnp.sum(both, axis=1, keepdims=True))
-    step_w = wide3[:, :SIG]
-    end_w = wide3[:, SIG : 2 * SIG]
-    exp_w = wide3[:, 2 * SIG :]
-    d_f = dout_ref[...].astype(F32)
-    signal_f = signal_ref[...].astype(F32)
-    gw_v = gw[...]
-    back_row = per_row(gw_v * scaled_ref[...].astype(F32)) * to_end
     grad_sum = per_row(d_f * exp_w * oh[...]) - back_row + drow[...]
-    back_low = jnp.sum(jnp.where(lane < BLK, back_row, 0.0), axis=1, keepdims=True)
-    back_high = jnp.sum(jnp.where(lane < BLK, 0.0, back_row), axis=1, keepdims=True)
     last_low = back_low + end_low * end_terms[0]
     last_high = back_high + end_high * end_terms[1]
     grad_sum = grad_sum + jnp.where(
         lane == BLK - 1, last_low, jnp.where(lane == ROWS - 1, last_high, 0.0)
     )
     grad_log = nn(grad_sum, lower_f, HIGH)
-    grad_scaled = gw_v * end_w + intra[...]
-    grad_step = grad_log * rate + per_row(grad_scaled * signal_f)
+    grad_step = grad_log * rate + own_step
     grad_dt = grad_step * sigmoid(logits)
     ddt_mine[...] = grad_dt
     ddt_copy = remote(ddt_mine, ddt_got, w_sem.at[0], w_sem.at[1], ctx=mate)
     ddt_copy.start()
-    skip_w = nn(jnp.broadcast_to(skip_ref[...], (HERE, HERE)), spread1, HIGH)[0:1]
-    gpad[:ROWS, :SIG] = (skip_w * d_f + grad_scaled * step_w) * slope[:, :SIG]
-    part[TAIL + 3 :] = jnp.zeros((n - TAIL - 3, 1, STATE), F32)
-
-    def small(at, row):
-        part[at] = jnp.concatenate([row, jnp.zeros((1, STATE - HERE), F32)], axis=1)
-
     small(TAIL, nt(ones8, grad_log * step, HIGH)[0:1] * (-jnp.exp(alog_ref[...])))
     small(TAIL + 1, nt(ones8, grad_dt, HIGH)[0:1])
-    small(TAIL + 2, nt(ones8, per_row(d_f * signal_f), HIGH)[0:1])
-
-    def sums(cols, source, at):
-        g = gpad[:ROWS, cols]
-        for k in range(KSIZE):
-            start = EDGE - RIM + k
-            part[k * (OWN // STATE) + at] = jnp.sum(
-                g * pad[start : start + ROWS, source], axis=0, keepdims=True
-            )
-        part[KSIZE * (OWN // STATE) + at] = jnp.sum(g, axis=0, keepdims=True)
-
-    for q in range(SIG // STATE):
-        sums(third(q), third(q), q)
 
     for k in range(2):
 
@@ -521,63 +553,84 @@
     rim_copy.start()
     sums(slice(SIG, OWN), slice(SIG + 2 * STATE, WIDE), SIG // STATE)
 
-    def p_copy(d):
-        return remote(part.at[d], parts.at[me], ps_sem.at[d], pr_sem.at[me], ctx=d)
-
-    def t_copy(d):
-        return remote(mine_sum, total.at[me], ts_sem.at[d], tr_sem.at[me], ctx=d)
-
-    def send_part(i, _):
-        p_copy(other(me, i, n)).start()
-        return 0
-
-    lax.fori_loop(1, n, send_part, 0)
-    parts[me] = part[me]
+    heads_at, rest_at = slice(TAIL, TAIL + 3), slice(TAIL + 3, TAIL + 6)
+
+    def narrow(ref):
+        value = ref[heads_at]
+        ref[rest_at] = value - value.astype(BF16).astype(F32)
+        return ref[...].astype(BF16)
+
+    planes = n // 2
+    y = me // planes
+    z = me - y * planes
+    z_high = z // 4
+    z_low = z - 4 * z_high
+    here = 4 * y + z_low
+
+    def near_at(k):
+        s = lax.rem(here + k, 8)
+        y_of = s // 4
+        return y_of * planes + z_high * 4 + s - 4 * y_of, s
+
+    def far_at(k):
+        s = lax.rem(z_high + k, 4)
+        return y * planes + 4 * s + z_low, s
+
+    low_part[...] = narrow(part)
+    sent = []
+    for k in range(1, 8):
+        d, _ = near_at(k)
+        copy = remote(low_part, near.at[here], q_send.at[k], q_near.at[here], ctx=d)
+        copy.start()
+        sent.append(copy)
+    near[here] = low_part[...]
 
     rim_copy.wait()
     gpad[ROWS:] = jnp.where(me == 1, 0.0, rims[...])
 
-    def raw(r):
-        out = []
+    def raw(r, out):
         for taps, cols in ((taps_ref, slice(0, SIG)), (mtaps_ref, slice(SIG, OWN))):
             acc = taps[RIM : RIM + 1] * gpad[r : r + BLK, cols]
             for k in range(RIM):
                 acc = acc + taps[k : k + 1] * gpad[r + RIM - k : r + RIM - k + BLK, cols]
-            out.append(acc)
-        return jnp.concatenate(out, axis=1)
-
-    swap[...] = raw(BLK)
+            out[:, cols] = acc
+
+    raw(BLK, swap)
     swap_copy = remote(swap, big.at[pl.ds(kept, BLK)], w_sem.at[2], w_sem.at[3], ctx=mate)
     swap_copy.start()
-
-    def part_in(i, _):
-        s = other(me, i, n)
-        remote(part.at[s], parts.at[s], ps_sem.at[s], pr_sem.at[s], ctx=s).wait_recv()
-        return 0
-
-    lax.fori_loop(1, n, part_in, 0)
-    mine_sum[...] = jnp.sum(parts[...], axis=0)
-
-    def send_total(i, _):
-        t_copy(other(me, i, n)).start()
-        return 0
-
-    lax.fori_loop(1, n, send_total, 0)
-    total[me] = mine_sum[...]
-    big[pl.ds(kept, BLK)] = raw(0)
+    for k in range(1, 8):
+        d, s = near_at(k)
+        remote(low_part, near.at[s], q_send.at[k], q_near.at[s], ctx=d).wait_recv()
+    part[...] = jnp.sum(near[...].astype(F32), axis=0)
+    part[heads_at] = part[heads_at] + part[rest_at]
+    low_near[...] = narrow(part)
+    for k in range(1, 4):
+        d, _ = far_at(k)
+        copy = remote(low_near, far.at[z_high], q_send.at[7 + k], q_far.at[z_high], ctx=d)
+        copy.start()
+        sent.append(copy)
+    far[z_high] = low_near[...]
+    raw(0, stay)
+    stay_copy = fetch(0, stay, big.at[pl.ds(kept, BLK)])
     ddt_copy.wait()
     own, got = ddt_mine[...], ddt_got[...]
     ddt_low = jnp.where(odd == 0, own, turned(got))
     ddt_high = jnp.where(odd == 0, got, turned(own))
     ddt_ref[...] = jnp.where(lane < BLK, ddt_low, ddt_high)
+    ddt_out = fetch(1, ddt_ref, ddt_hbm)
+    for k in range(1, 4):
+        d, s = far_at(k)
+        remote(low_near, far.at[s], q_send.at[7 + k], q_far.at[s], ctx=d).wait_recv()
+    total[...] = jnp.sum(far[...].astype(F32), axis=0)
+    total[heads_at] = total[heads_at] + total[rest_at]
+    total_out = fetch(2, total, total_hbm)
+    for copy in sent:
+        copy.wait_send()
 
     def done(i, _):
         d = other(me, i, n)
         h_copy(d).wait_send()
         c_copy(d).wait_send()
-        p_copy(d).wait_send()
-        t_copy(d).wait_send()
-        remote(mine_sum, total.at[d], ts_sem.at[d], tr_sem.at[d], ctx=d).wait_recv()
         return 0
 
     lax.fori_loop(1, n, done, 0)
@@ -587,6 +640,9 @@
         def _():
             m_copy(k).wait_send()
 
+    stay_copy.wait()
+    ddt_out.wait()
+    total_out.wait()
     swap_copy.wait()
 
 
@@ -600,11 +656,11 @@
         functools.partial(main_kernel, n, half),
         out_shape=(
             jax.ShapeDtypeStruct((ROWS, OWN), F32),
-            jax.ShapeDtypeStruct((n, 1, STATE), F32),
+            jax.ShapeDtypeStruct((n, STATE), F32),
             jax.ShapeDtypeStruct((HERE, ROWS), F32),
         ),
         in_specs=[pl.BlockSpec(memory_space=pl.ANY)] * len(operands),
-        out_specs=(VM,) * 3,
+        out_specs=(pl.BlockSpec(memory_space=pl.ANY),) * 3,
         scratch_shapes=[
             vm((ROWS, SIG), BF16),
             vm((ROWS, 3 * STATE), BF16),
@@ -653,16 +709,20 @@
             vm((ROWS + RIMS, OWN), F32),
             vm((RIMS, OWN), F32),
             vm((BLK, OWN), F32),
+            vm((BLK, OWN), F32),
             vm((HERE, ROWS), F32),
             vm((HERE, ROWS), F32),
-            vm((n, 1, STATE), F32),
-            vm((n, 1, STATE), F32),
-            vm((1, STATE), F32),
+            vm((HERE, ROWS), F32),
+            vm((n, STATE), F32),
+            vm((8, n, STATE), BF16),
+            vm((4, n, STATE), BF16),
+            vm((n, STATE), F32),
+            vm((n, STATE), BF16),
+            vm((n, STATE), BF16),
         ]
         + [dma((17,)), dma((6,)), dma((6,)), dma((1,)), dma((1,)), dma((2,)), dma((2,))]
         + [dma((n,))] * 10
-        + [dma((2,)), dma((2,)), dma((2,)), dma((4,))]
-        + [dma((n,))] * 4,
+        + [dma((2,)), dma((2,)), dma((2,)), dma((4,)), dma((11,)), dma((8,)), dma((4,))],
         compiler_params=pltpu.CompilerParams(
             collective_id=0, has_side_effects=True, vmem_limit_bytes=56 * 1024 * 1024
         ),
@@ -679,7 +739,8 @@
     ddt_out[...] = ddt[...]
     for k in range(KSIZE + 1):
         for q in range(OWN // STATE):
-            row = total[k * (OWN // STATE) + q] * scale
+            at = k * (OWN // STATE) + q
+            row = total[at : at + 1] * scale
             cols = slice(q * STATE, (q + 1) * STATE)
             if q < SIG // STATE:
                 if k < KSIZE:
@@ -691,7 +752,7 @@
             else:
                 dmbias[...] = row
     for k, out in enumerate((dalog, ddtb, dskip)):
-        out[...] = total[TAIL + k][:, :HERE] * scale
+        out[...] = total[TAIL + k : TAIL + k + 1, :HERE] * scale
 
 
 def last(*operands):

time: 92.3 us -> 86.9 us (0.941)
  the two profiles are of different devices: /device:TPU:4 before, /device:TPU:58 now
where the time goes in v4:
time: 86.9 us; the launch traced here: 86.6 us
  Pallas kernels  83.6 us (96%)
  local copies, waits for them, and re-layouts  2.36 us (3%)
    pallas_call x1, Pallas kernels, main(): pl.pallas_call(functools.partial(main_kernel, n, half), out_shape=(jax.Sh...  82.8 us
    unnamed x6, local copies, waits for them, and re-layouts  2.36 us

profile of v4, /device:TPU:58, one launch (start us, length us, event | category | flops | bytes accessed | tf_op | source)
XLA Modules:
  0.0 86.6 jit_solution(8952244169844783509)
XLA Ops:
  0.6 82.8 %main.1 = (f32[128,640]{1,0:T(8,128)}, f32[32,128]{1,0:T(8,128)}, f32[8,128]{1,0:T(8,128)}) custom-call(bf16[128,512]{1,0:T(8,128)(2,1)} %sig_hbm.1, bf16[128,2048]{1,0:T(8,128)(2,1)} %map_hbm.1, f32[8,128]{1,0:T(8,128)} %bitcast.12, bf16[128,512]{1,0:T(8,128)(2,1)} %dout_hbm.1, f32[4,512]{1,0:T(4,128)} %taps_hbm.1, f32[1,512]{1,0:T(1,128)} %bitcast.13, ...), custom_call_target="tpu_custom_call" | custom-call | tf_op jit(solution)/shard_map/main/pallas_call | solution.py:655
  83.5 0.0 copy-start.2
  83.5 0.7 copy-done.2
  84.2 0.0 copy-start
  84.2 1.0 %copy-done = f32[128,640]{1,0:T(8,128)S(1)} copy-done((f32[128,640]{1,0:T(8,128)S(1)}, f32[128,640]{1,0:T(8,128)}, u32[]{:S(2)}) %copy-start) | copy-done | bytes 327704
  85.1 0.0 copy-start.1
  85.1 0.7 copy-done.1
  85.8 0.8 last.1
Async XLA Ops:
  83.5 0.7 copy-start.2
  84.2 1.0 %copy-start = (f32[128,640]{1,0:T(8,128)S(1)}, f32[128,640]{1,0:T(8,128)}, u32[]{:S(2)}) copy-start(f32[128,640]{1,0:T(8,128)} %get-tuple-element.23.big) | copy-start | bytes 983044
  85.1 0.7 copy-start.1

commit v5 on v4

--- a/solution.py
+++ b/solution.py
@@ -22,9 +22,12 @@
 OWN = SIG + STATE
 EDGE = 16
 RIMS = 8
-TAIL = (KSIZE + 1) * OWN // STATE
+QUADS = SIG // STATE
+SUMS = 24
+FINE = 10
 MESH = pl.DeviceIdType.MESH
 VM = pl.BlockSpec(memory_space=pltpu.VMEM)
+HBM = pl.BlockSpec(memory_space=pltpu.HBM)
 HIGH = lax.Precision.HIGHEST
 F32 = jnp.float32
 BF16 = jnp.bfloat16
@@ -81,19 +84,39 @@
     return jnp.where(e < 0.03, series, jnp.log(1.0 + e))
 
 
+def pack(v):
+    n, rows, _ = v.shape
+    high = v.astype(BF16)
+    value = high.astype(F32)
+    tiny = jnp.abs(value) < 1e-30
+    ratio = jnp.where(tiny, 0.0, (v - value) / jnp.where(tiny, 1.0, value))
+    steps = jnp.clip(jnp.round(ratio * (256.0 * FINE)), -FINE, FINE)
+    both = steps[:, : rows // 2] * (2.0 * FINE + 1.0) + steps[:, rows // 2 :]
+    return high, both.astype(BF16)
+
+
+def unpack(high, both):
+    value = high.astype(F32)
+    both = both.astype(F32)
+    first = jnp.floor((both + (FINE + 0.5)) * (1.0 / (2.0 * FINE + 1.0)))
+    second = both - first * (2.0 * FINE + 1.0)
+    steps = jnp.concatenate([first, second], axis=-2)
+    return value + value * steps * (1.0 / (256.0 * FINE))
+
+
 def main_kernel(
     n, half, sig_hbm, map_hbm, dt_hbm, dout_hbm, taps_hbm, bias_hbm, mtaps_hbm, mbias_hbm,
     alog_hbm, dtb_hbm, skip_hbm,
-    big, total_hbm, ddt_hbm,
+    dsig_hbm, dmap_hbm, sums_hbm, small_hbm, ddt_hbm,
     sig_in, map_in, dout_ref, dt_in, dt_got, taps_ref, bias_ref, mtaps_ref, mbias_ref,
     alog_ref, dtb_ref, skip_ref, tail_own, tail_got, tap_row, gtaps_ref,
     pad, slope, signal_ref, scaled_ref, weighted_ref, sgrad_ref, imap_ref, omap_ref, wide3, intra,
     oh, gw, drow, xs, gs, es, xr, gr, er, yh, yc, lh, lc, first_local, second_sg, lk,
-    mg, mgot, gpad, rims, swap, stay, ddt_mine, ddt_got, ddt_ref, part, near, far, total,
-    low_part, low_near,
+    mg, mgot, gpad, rims, swap, stay, ddt_mine, ddt_got, ddt_ref,
+    part, low_part, near, low_near, far, total, part_b, near_b, sum_b, far_b, total_b,
     l_sem, n_send, n_recv, b_send, b_recv, tap_send, tap_recv,
     xs_sem, xr_sem, gs_sem, gr_sem, es_sem, er_sem, hs_sem, hr_sem, cs_sem, cr_sem,
-    ms_sem, mr_sem, r_sem, w_sem, q_send, q_near, q_far
+    ms_sem, mr_sem, r_sem, w_sem, q_send, q_near, q_far, q_near_b, q_far_b
 ):
     me = lax.axis_index("ctx")
     f = lax.axis_index("fsdp")
@@ -205,8 +228,8 @@
         )
         for k, start in enumerate(starts)
     ]
+    dout_copy = to_mate(5, dout_hbm.at[pl.ds(given, BLK)], dout_ref.at[BLK:ROWS])
     sig_copy = to_mate(4, sig_hbm.at[pl.ds(given, BLK)], sig_in.at[BLK:ROWS])
-    dout_copy = to_mate(5, dout_hbm.at[pl.ds(given, BLK)], dout_ref.at[BLK:ROWS])
 
     lane = lax.broadcasted_iota(jnp.int32, (HERE, ROWS), 1)
     row_id = lax.broadcasted_iota(jnp.int32, (ROWS, ROWS), 0)
@@ -249,7 +272,6 @@
 
     pad[EDGE : EDGE + BLK, :SIG] = sig_in[:BLK, :].astype(F32)
     pad[EDGE : EDGE + BLK, SIG:] = map_in[:BLK, :].astype(F32)
-    sig_rows(EDGE, BLK - EDGE)
     dt_copy.wait()
     own, got = dt_in[...], dt_got[...]
     own = jnp.where(odd == 0, own, turned(own))
@@ -302,57 +324,64 @@
     before = jnp.where(me == n - 1, tail_own[...].astype(F32), tail_got[...].astype(F32))
     pad[:EDGE] = before * keep
     pad[EDGE + BLK :, SIG:] = map_in[BLK:, :].astype(F32)
-    for k, out in enumerate((imap_ref, omap_ref)):
+    def map_rows(k, out):
         cols = slice(SIG + k * STATE, SIG + (k + 1) * STATE)
         v = preact(0, ROWS, cols, gtaps_ref[k, :KSIZE], gtaps_ref[k, KSIZE : KSIZE + 1])
         out[...] = (v * sigmoid(v)).astype(BF16)
+
+    def mine(d):
+        return pl.ds(pl.multiple_of(d * share, share), share)
+
+    def x_copy(d):
+        return remote(xs.at[mine(d)], xr.at[me], xs_sem.at[d], xr_sem.at[me], ctx=d)
+
+    def g_copy(d):
+        return remote(gs.at[d], gr.at[me], gs_sem.at[d], gr_sem.at[me], ctx=d)
+
+    def h_copy(d):
+        return remote(yh.at[d], lh.at[mine(me)], hs_sem.at[d], hr_sem.at[me], ctx=d)
+
+    def c_copy(d):
+        return remote(yc.at[d], lc.at[me], cs_sem.at[d], cr_sem.at[me], ctx=d)
+
+    def send_g(i, _):
+        g_copy(other(me, i, n)).start()
+        return 0
+
+    def send_x(i, _):
+        x_copy(other(me, i, n)).start()
+        return 0
+
+    map_rows(1, omap_ref)
+    dout_copy.wait()
+    low, high = slice(0, BLK), slice(BLK, ROWS)
+    for q in range(QUADS):
+        cols3 = slice(2 * SIG + q * STATE, 2 * SIG + (q + 1) * STATE)
+        sgrad_ref[:, third(q)] = (dout_ref[:, third(q)].astype(F32) * wide3[:, cols3]).astype(BF16)
+    second_sg[...] = tn(sgrad_ref[high, :], omap_ref[high, :])
+    first_sg = tn(sgrad_ref[low, :], omap_ref[low, :])
+    for h in range(HERE):
+        at = slice(h * HDIM, (h + 1) * HDIM)
+        link = first_sg[at, :] + end_low8[h : h + 1] * second_sg[at, :]
+        top, rest = pack(link.reshape(per_head, share, STATE))
+        gs[h * per_head : (h + 1) * per_head, :share, :] = top
+        gs[h * per_head : (h + 1) * per_head, share:, :] = rest
+    lax.fori_loop(1, n, send_g, 0)
+    gr[me] = gs[me]
+
+    map_rows(0, imap_ref)
     v = preact(0, ROWS, slice(SIG + 2 * STATE, WIDE), mtaps_ref[...], mbias_ref[...])
     s = sigmoid(v)
     slope[:, SIG:] = s * (1.0 + v * (1.0 - s))
     sig_copy.wait()
     pad[EDGE + BLK :, :SIG] = sig_in[BLK:, :].astype(F32)
-    sig_rows(0, EDGE)
-    sig_rows(BLK, BLK)
-    dout_copy.wait()
-    for q in range(SIG // STATE):
+    sig_rows(0, ROWS)
+    for q in range(QUADS):
         cols = third(q)
         cols2 = slice(SIG + q * STATE, SIG + (q + 1) * STATE)
-        cols3 = slice(2 * SIG + q * STATE, 2 * SIG + (q + 1) * STATE)
         scaled_b = (signal_ref[:, cols].astype(F32) * wide3[:, cols]).astype(BF16)
         scaled_ref[:, cols] = scaled_b
         weighted_ref[:, cols] = (scaled_b.astype(F32) * wide3[:, cols2]).astype(BF16)
-        sgrad_ref[:, cols] = (dout_ref[:, cols].astype(F32) * wide3[:, cols3]).astype(BF16)
-    low, high = slice(0, BLK), slice(BLK, ROWS)
-    second_sg[...] = tn(sgrad_ref[high, :], omap_ref[high, :])
-    gs[...] = tn(sgrad_ref[low, :], omap_ref[low, :])
-    for h in range(HERE):
-        at = slice(h * HDIM, (h + 1) * HDIM)
-        gs[at, :] = gs[at, :] + end_low8[h : h + 1] * second_sg[at, :]
-
-    def mine(d):
-        return pl.ds(pl.multiple_of(d * share, share), share)
-
-    def x_copy(d):
-        return remote(xs.at[mine(d)], xr.at[me], xs_sem.at[d], xr_sem.at[me], ctx=d)
-
-    def g_copy(d):
-        return remote(gs.at[mine(d)], gr.at[me], gs_sem.at[d], gr_sem.at[me], ctx=d)
-
-    def h_copy(d):
-        return remote(yh.at[d], lh.at[mine(me)], hs_sem.at[d], hr_sem.at[me], ctx=d)
-
-    def c_copy(d):
-        return remote(yc.at[d], lc.at[mine(me)], cs_sem.at[d], cr_sem.at[me], ctx=d)
-
-    def send_g(i, _):
-        g_copy(other(me, i, n)).start()
-        return 0
-
-    def send_x(i, _):
-        x_copy(other(me, i, n)).start()
-        return 0
-
-    lax.fori_loop(1, n, send_g, 0)
     first_local[...] = tn(weighted_ref[low, :], imap_ref[low, :])
     second_local = tn(weighted_ref[high, :], imap_ref[high, :])
     for h in range(HERE):
@@ -360,7 +389,6 @@
         xs[at, :] = (end_high8[h : h + 1] * first_local[at, :] + second_local[at, :]).astype(BF16)
     lax.fori_loop(1, n, send_x, 0)
     xr[me] = xs[mine(me)]
-    gr[me] = gs[mine(me)]
 
     score = nt(omap_ref[...], imap_ref[...])
     lane_row = lax.broadcasted_iota(jnp.int32, (ROWS, STATE), 1)
@@ -399,13 +427,16 @@
     def g_arrived(i, _):
         s = other(me, i, n)
         remote(es.at[s // per_head], er.at[s], es_sem.at[s], er_sem.at[s], ctx=s).wait_recv()
-        remote(gs.at[mine(s)], gr.at[s], gs_sem.at[s], gr_sem.at[s], ctx=s).wait_recv()
+        remote(gs.at[s], gr.at[s], gs_sem.at[s], gr_sem.at[s], ctx=s).wait_recv()
         return 0
 
     def to_front(i, g):
         at = holder(n - 1 - i)
-        yc[at] = g
-        return er[at] * g + gr[at]
+        top, rest = pack(g[None])
+        yc[at, :share, :] = top[0]
+        yc[at, share:, :] = rest[0]
+        got = gr[at]
+        return er[at] * g + unpack(got[:share], got[share:])
 
     def send_c(i, _):
         c_copy(other(me, i, n)).start()
@@ -432,19 +463,20 @@
     lax.fori_loop(0, n, to_back, zero)
     lax.fori_loop(1, n, send_h, 0)
     lh[mine(me)] = yh[me]
-    lc[mine(me)] = yc[me]
+    lc[me] = yc[me]
     step_w = wide3[:, :SIG]
     end_w = wide3[:, SIG : 2 * SIG]
     exp_w = wide3[:, 2 * SIG :]
     d_f = dout_ref[...].astype(F32)
     signal_f = signal_ref[...].astype(F32)
     skip_w = nn(jnp.broadcast_to(skip_ref[...], (HERE, HERE)), spread1, HIGH)[0:1]
-    part[TAIL + 3 :] = jnp.zeros((n - TAIL - 3, STATE), F32)
+    part[(KSIZE + 1) * QUADS :] = jnp.zeros((SUMS - (KSIZE + 1) * QUADS, STATE), F32)
 
     def small(at, row):
-        part[at : at + 1] = jnp.concatenate([row, jnp.zeros((1, STATE - HERE), F32)], axis=1)
-
-    small(TAIL + 2, nt(ones8, per_row(d_f * signal_f), HIGH)[0:1])
+        at = KSIZE + 1 + at
+        part_b[at : at + 1] = jnp.concatenate([row, jnp.zeros((1, STATE - HERE), F32)], axis=1)
+
+    small(2, nt(ones8, per_row(d_f * signal_f), HIGH)[0:1])
 
     def m_copy(k):
         return remote(
@@ -464,14 +496,16 @@
         d = other(me, i, n)
         g_copy(d).wait_send()
         e_copy(d).wait_send()
-        remote(yc.at[d], lc.at[mine(d)], cs_sem.at[d], cr_sem.at[d], ctx=d).wait_recv()
+        remote(yc.at[d], lc.at[d], cs_sem.at[d], cr_sem.at[d], ctx=d).wait_recv()
         return 0
 
     lax.fori_loop(1, n, c_in, 0)
-    lk[3] = lc[...].astype(BF16)
     for h in range(HERE):
         at = slice(h * HDIM, (h + 1) * HDIM)
-        lk[2, at, :] = (second_sg[at, :] + end_high8[h : h + 1] * lc[at, :]).astype(BF16)
+        got = lc[h * per_head : (h + 1) * per_head]
+        state = unpack(got[:, :share], got[:, share:]).reshape(HDIM, STATE)
+        lk[3, at, :] = state.astype(BF16)
+        lk[2, at, :] = (second_sg[at, :] + end_high8[h : h + 1] * state).astype(BF16)
     for b, rows in enumerate((low, high)):
         mg[0, rows, :] = mg[0, rows, :] + nn(weighted_ref[rows, :], lk[2 + b])
     to_owner(0)
@@ -485,19 +519,91 @@
     own_step = per_row(grad_scaled * signal_f)
     gpad[:ROWS, :SIG] = (skip_w * d_f + grad_scaled * step_w) * slope[:, :SIG]
 
-    def sums(cols, source, at):
+    def sums(cols, source, into, every, at):
         g = gpad[:ROWS, cols]
         for k in range(KSIZE):
             start = EDGE - RIM + k
-            row = k * (OWN // STATE) + at
-            part[row : row + 1] = jnp.sum(
+            row = k * every + at
+            into[row : row + 1] = jnp.sum(
                 g * pad[start : start + ROWS, source], axis=0, keepdims=True
             )
-        row = KSIZE * (OWN // STATE) + at
-        part[row : row + 1] = jnp.sum(g, axis=0, keepdims=True)
-
-    for q in range(SIG // STATE):
-        sums(third(q), third(q), q)
+        row = KSIZE * every + at
+        into[row : row + 1] = jnp.sum(g, axis=0, keepdims=True)
+
+    earlier = jnp.where(
+        odd == 0, lax.rem(me + n - 2, n), jnp.where(me == n - 1, n - 2, lax.rem(me + 2, n))
+    )
+    earlier = jnp.where(me == 0, 1, earlier)
+
+    def rim(i, cols):
+        copy = remote(
+            gpad.at[0:RIMS, cols], rims.at[:, cols], r_sem.at[2 * i], r_sem.at[2 * i + 1],
+            ctx=earlier,
+        )
+        copy.start()
+        return copy
+
+    sig_cols, map_cols = slice(0, SIG), slice(SIG, OWN)
+    sig_rim = rim(0, sig_cols)
+    for q in range(QUADS):
+        sums(third(q), third(q), part, QUADS, q)
+
+    planes = n // 2
+    y = me // planes
+    z = me - y * planes
+    z_high = z // 4
+    z_low = z - 4 * z_high
+    here = 4 * y + z_low
+    sent = []
+
+    def to_near(src, dst, at, recv_sem):
+        for k in range(1, 8):
+            s = lax.rem(here + k, 8)
+            d = s // 4 * planes + z_high * 4 + s - s // 4 * 4
+            copy = remote(src, dst.at[here], q_send.at[at + k], recv_sem.at[here], ctx=d)
+            copy.start()
+            sent.append(copy)
+        dst[here] = src[...]
+
+    def near_in(src, dst, recv_sem):
+        for k in range(1, 8):
+            s = lax.rem(here + k, 8)
+            remote(src, dst.at[s], q_send.at[k], recv_sem.at[s], ctx=mate).wait_recv()
+
+    def to_far(src, dst, at, recv_sem):
+        for k in range(1, 4):
+            s = lax.rem(z_high + k, 4)
+            d = y * planes + 4 * s + z_low
+            copy = remote(src, dst.at[z_high], q_send.at[at + k], recv_sem.at[z_high], ctx=d)
+            copy.start()
+            sent.append(copy)
+        dst[z_high] = src[...]
+
+    def far_in(src, dst, recv_sem):
+        for k in range(1, 4):
+            s = lax.rem(z_high + k, 4)
+            remote(src, dst.at[s], q_send.at[k], recv_sem.at[s], ctx=mate).wait_recv()
+
+    low_part[...] = part[...].astype(BF16)
+    to_near(low_part, near, 0, q_near)
+
+    def raw(r, out, taps, cols):
+        acc = taps[RIM : RIM + 1] * gpad[r : r + BLK, cols]
+        for k in range(RIM):
+            acc = acc + taps[k : k + 1] * gpad[r + RIM - k : r + RIM - k + BLK, cols]
+        out[:, cols] = acc
+
+    def transposed(i, rim_copy, taps, cols, out):
+        rim_copy.wait()
+        gpad[ROWS:, cols] = jnp.where(me == 1, 0.0, rims[:, cols])
+        raw(BLK, swap, taps, cols)
+        away = remote(
+            swap.at[:, cols], out.at[pl.ds(kept, BLK)], w_sem.at[2 * i], w_sem.at[2 * i + 1],
+            ctx=mate,
+        )
+        away.start()
+        raw(0, stay, taps, cols)
+        return away, fetch(i, stay.at[:, cols], out.at[pl.ds(kept, BLK)])
 
     def h_in(i, _):
         d = other(me, i, n)
@@ -533,8 +639,11 @@
     ddt_mine[...] = grad_dt
     ddt_copy = remote(ddt_mine, ddt_got, w_sem.at[0], w_sem.at[1], ctx=mate)
     ddt_copy.start()
-    small(TAIL, nt(ones8, grad_log * step, HIGH)[0:1] * (-jnp.exp(alog_ref[...])))
-    small(TAIL + 1, nt(ones8, grad_dt, HIGH)[0:1])
+    small(0, nt(ones8, grad_log * step, HIGH)[0:1] * (-jnp.exp(alog_ref[...])))
+    small(1, nt(ones8, grad_dt, HIGH)[0:1])
+    near_in(low_part, near, q_near)
+    low_near[...] = jnp.sum(near[...].astype(F32), axis=0).astype(BF16)
+    to_far(low_near, far, 7, q_far)
 
     for k in range(2):
 
@@ -545,87 +654,23 @@
             ).wait_recv()
 
     gpad[:ROWS, SIG:] = (mgot[0] + mgot[1]) * slope[:, SIG:]
-    earlier = jnp.where(
-        odd == 0, lax.rem(me + n - 2, n), jnp.where(me == n - 1, n - 2, lax.rem(me + 2, n))
-    )
-    earlier = jnp.where(me == 0, 1, earlier)
-    rim_copy = remote(gpad.at[0:RIMS], rims, r_sem.at[0], r_sem.at[1], ctx=earlier)
-    rim_copy.start()
-    sums(slice(SIG, OWN), slice(SIG + 2 * STATE, WIDE), SIG // STATE)
-
-    heads_at, rest_at = slice(TAIL, TAIL + 3), slice(TAIL + 3, TAIL + 6)
-
-    def narrow(ref):
-        value = ref[heads_at]
-        ref[rest_at] = value - value.astype(BF16).astype(F32)
-        return ref[...].astype(BF16)
-
-    planes = n // 2
-    y = me // planes
-    z = me - y * planes
-    z_high = z // 4
-    z_low = z - 4 * z_high
-    here = 4 * y + z_low
-
-    def near_at(k):
-        s = lax.rem(here + k, 8)
-        y_of = s // 4
-        return y_of * planes + z_high * 4 + s - 4 * y_of, s
-
-    def far_at(k):
-        s = lax.rem(z_high + k, 4)
-        return y * planes + 4 * s + z_low, s
-
-    low_part[...] = narrow(part)
-    sent = []
-    for k in range(1, 8):
-        d, _ = near_at(k)
-        copy = remote(low_part, near.at[here], q_send.at[k], q_near.at[here], ctx=d)
-        copy.start()
-        sent.append(copy)
-    near[here] = low_part[...]
-
-    rim_copy.wait()
-    gpad[ROWS:] = jnp.where(me == 1, 0.0, rims[...])
-
-    def raw(r, out):
-        for taps, cols in ((taps_ref, slice(0, SIG)), (mtaps_ref, slice(SIG, OWN))):
-            acc = taps[RIM : RIM + 1] * gpad[r : r + BLK, cols]
-            for k in range(RIM):
-                acc = acc + taps[k : k + 1] * gpad[r + RIM - k : r + RIM - k + BLK, cols]
-            out[:, cols] = acc
-
-    raw(BLK, swap)
-    swap_copy = remote(swap, big.at[pl.ds(kept, BLK)], w_sem.at[2], w_sem.at[3], ctx=mate)
-    swap_copy.start()
-    for k in range(1, 8):
-        d, s = near_at(k)
-        remote(low_part, near.at[s], q_send.at[k], q_near.at[s], ctx=d).wait_recv()
-    part[...] = jnp.sum(near[...].astype(F32), axis=0)
-    part[heads_at] = part[heads_at] + part[rest_at]
-    low_near[...] = narrow(part)
-    for k in range(1, 4):
-        d, _ = far_at(k)
-        copy = remote(low_near, far.at[z_high], q_send.at[7 + k], q_far.at[z_high], ctx=d)
-        copy.start()
-        sent.append(copy)
-    far[z_high] = low_near[...]
-    raw(0, stay)
-    stay_copy = fetch(0, stay, big.at[pl.ds(kept, BLK)])
+    map_rim = rim(1, map_cols)
+    sums(map_cols, slice(SIG + 2 * STATE, WIDE), part_b, 1, 0)
+    to_near(part_b, near_b, 10, q_near_b)
+    sig_out = transposed(1, sig_rim, taps_ref, sig_cols, dsig_hbm)
+    map_out = transposed(2, map_rim, mtaps_ref, map_cols, dmap_hbm)
+    near_in(part_b, near_b, q_near_b)
+    sum_b[...] = jnp.sum(near_b[...], axis=0)
+    to_far(sum_b, far_b, 17, q_far_b)
     ddt_copy.wait()
     own, got = ddt_mine[...], ddt_got[...]
     ddt_low = jnp.where(odd == 0, own, turned(got))
     ddt_high = jnp.where(odd == 0, got, turned(own))
     ddt_ref[...] = jnp.where(lane < BLK, ddt_low, ddt_high)
-    ddt_out = fetch(1, ddt_ref, ddt_hbm)
-    for k in range(1, 4):
-        d, s = far_at(k)
-        remote(low_near, far.at[s], q_send.at[7 + k], q_far.at[s], ctx=d).wait_recv()
+    ddt_out = fetch(3, ddt_ref, ddt_hbm)
+    far_in(low_near, far, q_far)
     total[...] = jnp.sum(far[...].astype(F32), axis=0)
-    total[heads_at] = total[heads_at] + total[rest_at]
-    total_out = fetch(2, total, total_hbm)
-    for copy in sent:
-        copy.wait_send()
+    sums_out = fetch(4, total, sums_hbm)
 
     def done(i, _):
         d = other(me, i, n)
@@ -640,10 +685,13 @@
         def _():
             m_copy(k).wait_send()
 
-    stay_copy.wait()
-    ddt_out.wait()
-    total_out.wait()
-    swap_copy.wait()
+    far_in(sum_b, far_b, q_far_b)
+    total_b[...] = jnp.sum(far_b[...], axis=0)
+    small_out = fetch(5, total_b, small_hbm)
+    for copy in sent:
+        copy.wait_send()
+    for copy in sig_out + map_out + (ddt_out, sums_out, small_out):
+        copy.wait()
 
 
 def main(*operands):
@@ -655,12 +703,14 @@
     return pl.pallas_call(
         functools.partial(main_kernel, n, half),
         out_shape=(
-            jax.ShapeDtypeStruct((ROWS, OWN), F32),
-            jax.ShapeDtypeStruct((n, STATE), F32),
+            jax.ShapeDtypeStruct((ROWS, SIG), F32),
+            jax.ShapeDtypeStruct((ROWS, STATE), F32),
+            jax.ShapeDtypeStruct((SUMS, STATE), F32),
+            jax.ShapeDtypeStruct((8, STATE), F32),
             jax.ShapeDtypeStruct((HERE, ROWS), F32),
         ),
         in_specs=[pl.BlockSpec(memory_space=pl.ANY)] * len(operands),
-        out_specs=(pl.BlockSpec(memory_space=pl.ANY),) * 3,
+        out_specs=(HBM,) * 5,
         scratch_shapes=[
             vm((ROWS, SIG), BF16),
             vm((ROWS, 3 * STATE), BF16),
@@ -692,15 +742,15 @@
             vm((ROWS, SIG), F32),
             vm((HERE, ROWS), F32),
             vm((SIG, STATE), BF16),
-            vm((SIG, STATE), F32),
+            vm((n, 3 * share // 2, STATE), BF16),
             vm((HERE, 1, STATE), F32),
             vm((n, share, STATE), BF16),
-            vm((n, share, STATE), F32),
+            vm((n, 3 * share // 2, STATE), BF16),
             vm((n, 1, STATE), F32),
             vm((n, share, STATE), BF16),
-            vm((n, share, STATE), F32),
+            vm((n, 3 * share // 2, STATE), BF16),
             vm((SIG, STATE), BF16),
-            vm((SIG, STATE), F32),
+            vm((n, 3 * share // 2, STATE), BF16),
             vm((SIG, STATE), F32),
             vm((SIG, STATE), F32),
             vm((4, SIG, STATE), BF16),
@@ -713,16 +763,21 @@
             vm((HERE, ROWS), F32),
             vm((HERE, ROWS), F32),
             vm((HERE, ROWS), F32),
-            vm((n, STATE), F32),
-            vm((8, n, STATE), BF16),
-            vm((4, n, STATE), BF16),
-            vm((n, STATE), F32),
-            vm((n, STATE), BF16),
-            vm((n, STATE), BF16),
+            vm((SUMS, STATE), F32),
+            vm((SUMS, STATE), BF16),
+            vm((8, SUMS, STATE), BF16),
+            vm((SUMS, STATE), BF16),
+            vm((4, SUMS, STATE), BF16),
+            vm((SUMS, STATE), F32),
+            vm((8, STATE), F32),
+            vm((8, 8, STATE), F32),
+            vm((8, STATE), F32),
+            vm((4, 8, STATE), F32),
+            vm((8, STATE), F32),
         ]
         + [dma((17,)), dma((6,)), dma((6,)), dma((1,)), dma((1,)), dma((2,)), dma((2,))]
         + [dma((n,))] * 10
-        + [dma((2,)), dma((2,)), dma((2,)), dma((4,)), dma((11,)), dma((8,)), dma((4,))],
+        + [dma((2,)), dma((2,)), dma((4,)), dma((6,)), dma((21,)), dma((8,)), dma((4,)), dma((8,)), dma((4,))],
         compiler_params=pltpu.CompilerParams(
             collective_id=0, has_side_effects=True, vmem_limit_bytes=56 * 1024 * 1024
         ),
@@ -731,28 +786,26 @@
 
 
 def last_kernel(
-    scale, big, total, ddt,
-    dsig, dmap, ddt_out, dtaps, dmtaps, dbias, dmbias, dalog, ddtb, dskip
+    scale, dsig_in, dmap_in, sums_in, small_in, ddt_in,
+    dsig, dmap, ddt, dtaps, dmtaps, dbias, dmbias, dalog, ddtb, dskip
 ):
-    dsig[...] = big[:, :SIG]
-    dmap[...] = big[:, SIG:]
-    ddt_out[...] = ddt[...]
+    dsig[...] = dsig_in[...]
+    dmap[...] = dmap_in[...]
+    ddt[...] = ddt_in[...]
     for k in range(KSIZE + 1):
-        for q in range(OWN // STATE):
-            at = k * (OWN // STATE) + q
-            row = total[at : at + 1] * scale
+        for q in range(QUADS):
+            at = k * QUADS + q
             cols = slice(q * STATE, (q + 1) * STATE)
-            if q < SIG // STATE:
-                if k < KSIZE:
-                    dtaps[k : k + 1, cols] = row
-                else:
-                    dbias[:, cols] = row
-            elif k < KSIZE:
-                dmtaps[k : k + 1, :] = row
+            row = sums_in[at : at + 1] * scale
+            if k < KSIZE:
+                dtaps[k : k + 1, cols] = row
             else:
-                dmbias[...] = row
+                dbias[:, cols] = row
+    dmtaps[...] = small_in[:KSIZE] * scale
+    dmbias[...] = small_in[KSIZE : KSIZE + 1] * scale
     for k, out in enumerate((dalog, ddtb, dskip)):
-        out[...] = total[TAIL + k : TAIL + k + 1, :HERE] * scale
+        at = KSIZE + 1 + k
+        out[...] = small_in[at : at + 1, :HERE] * scale
 
 
 def last(*operands):
@@ -764,7 +817,7 @@
     return pl.pallas_call(
         functools.partial(last_kernel, scale),
         out_shape=tuple(jax.ShapeDtypeStruct(s, F32) for s in shapes),
-        in_specs=[VM] * 3,
+        in_specs=[VM] * 5,
         out_specs=(VM,) * len(shapes),
         compiler_params=pltpu.CompilerParams(vmem_limit_bytes=8 * 1024 * 1024),
         name="last",

time: 86.9 us -> 81 us (0.932)
  the two profiles are of different devices: /device:TPU:58 before, /device:TPU:18 now
where the time goes in v5:
time: 81 us; the launch traced here: 80.7 us
  Pallas kernels  76.8 us (95%)
  local copies, waits for them, and re-layouts  3.16 us (4%)
    pallas_call x1, Pallas kernels, main(): pl.pallas_call(functools.partial(main_kernel, n, half), out_shape=(jax.Sh...  76.1 us
    unnamed x10, local copies, waits for them, and re-layouts  3.16 us

profile of v5, /device:TPU:18, one launch (start us, length us, event | category | flops | bytes accessed | tf_op | source)
XLA Modules:
  0.0 80.7 jit_solution(4248612460115734689)
XLA Ops:
  0.6 76.1 %main.1 = (f32[128,512]{1,0:T(8,128)}, f32[128,128]{1,0:T(8,128)}, f32[24,128]{1,0:T(8,128)}, f32[8,128]{1,0:T(8,128)}, f32[8,128]{1,0:T(8,128)}) custom-call(bf16[128,512]{1,0:T(8,128)(2,1)} %sig_hbm.1, bf16[128,2048]{1,0:T(8,128)(2,1)} %map_hbm.1, f32[8,128]{1,0:T(8,128)} %bitcast.12, bf16[128,512]{1,0:T(8,128)(2,1)} %dout_hbm.1, f32[4,512]{1,0:T(4,128)} %taps_hbm.1, ...), custom_call_target="tpu_custom_call" | custom-call | tf_op jit(solution)/shard_map/main/pallas_call | solution.py:703
  76.7 0.0 copy-start.4
  76.7 0.0 copy-start.3
  76.7 0.7 copy-done.4
  77.4 0.0 copy-done.3
  77.4 0.0 copy-start
  77.4 0.9 %copy-done = f32[128,512]{1,0:T(8,128)S(1)} copy-done((f32[128,512]{1,0:T(8,128)S(1)}, f32[128,512]{1,0:T(8,128)}, u32[]{:S(2)}) %copy-start) | copy-done | bytes 262168
  78.4 0.0 copy-start.1
  78.4 0.8 %copy-done.1 = f32[128,128]{1,0:T(8,128)S(1)} copy-done((f32[128,128]{1,0:T(8,128)S(1)}, f32[128,128]{1,0:T(8,128)}, u32[]{:S(2)}) %copy-start.1) | copy-done | bytes 65560
  79.2 0.0 copy-start.2
  79.2 0.7 copy-done.2
  79.9 0.8 last.1
Async XLA Ops:
  76.7 0.7 copy-start.4
  76.7 0.7 copy-start.3
  77.4 0.9 %copy-start = (f32[128,512]{1,0:T(8,128)S(1)}, f32[128,512]{1,0:T(8,128)}, u32[]{:S(2)}) copy-start(f32[128,512]{1,0:T(8,128)} %get-tuple-element.25.dsig_in) | copy-start | bytes 786436
  78.4 0.8 %copy-start.1 = (f32[128,128]{1,0:T(8,128)S(1)}, f32[128,128]{1,0:T(8,128)}, u32[]{:S(2)}) copy-start(f32[128,128]{1,0:T(8,128)} %get-tuple-element.26.dmap_in) | copy-start | bytes 196612
  79.2 0.7 copy-start.2

commit v6 on v5

--- a/solution.py
+++ b/solution.py
@@ -111,7 +111,7 @@
     sig_in, map_in, dout_ref, dt_in, dt_got, taps_ref, bias_ref, mtaps_ref, mbias_ref,
     alog_ref, dtb_ref, skip_ref, tail_own, tail_got, tap_row, gtaps_ref,
     pad, slope, signal_ref, scaled_ref, weighted_ref, sgrad_ref, imap_ref, omap_ref, wide3, intra,
-    oh, gw, drow, xs, gs, es, xr, gr, er, yh, yc, lh, lc, first_local, second_sg, lk,
+    oh, gw, drow, m_out, xs, gs, es, xr, gr, er, yh, yc, lh, lc, first_local, second_sg, lk,
     mg, mgot, gpad, rims, swap, stay, ddt_mine, ddt_got, ddt_ref,
     part, low_part, near, low_near, far, total, part_b, near_b, sum_b, far_b, total_b,
     l_sem, n_send, n_recv, b_send, b_recv, tap_send, tap_recv,
@@ -134,6 +134,21 @@
     ending = pl.multiple_of((1 - odd) * BLK + BLK - EDGE, EDGE)
     starts = (group, GROUPS + group, f)
     barrier = pltpu.get_barrier_semaphore()
+
+    def greet(i, _):
+        signal(barrier, ctx=other(me, i, n))
+        return 0
+
+    lax.fori_loop(1, n, greet, 0)
+    for k in range(2):
+
+        @pl.when(group + k * half != f)
+        def _():
+            signal(barrier, fsdp=group + k * half)
+
+        @pl.when(first + k != f)
+        def _():
+            signal(barrier, fsdp=first + k)
 
     def fetch(i, src, dst):
         copy = pltpu.make_async_copy(src, dst, l_sem.at[i])
@@ -172,21 +187,6 @@
             )
         )
 
-    def greet(i, _):
-        signal(barrier, ctx=other(me, i, n))
-        return 0
-
-    lax.fori_loop(1, n, greet, 0)
-    for k in range(2):
-
-        @pl.when(group + k * half != f)
-        def _():
-            signal(barrier, fsdp=group + k * half)
-
-        @pl.when(first + k != f)
-        def _():
-            signal(barrier, fsdp=first + k)
-
     for copy in local:
         copy.wait()
     tap_row[0:KSIZE] = mtaps_ref[...]
@@ -220,15 +220,18 @@
         copy.start()
         return copy
 
+    def map_copy(k):
+        return to_mate(
+            1 + k, map_hbm.at[pl.ds(given, BLK), columns(starts[k])], map_in.at[BLK:ROWS, third(k)]
+        )
+
     dt_copy = to_mate(0, dt_hbm, dt_got)
-    tail_copy = to_side(0, slice(0, WIDE))
-    map_copies = [
-        to_mate(
-            1 + k, map_hbm.at[pl.ds(given, BLK), columns(start)], map_in.at[BLK:ROWS, third(k)]
-        )
-        for k, start in enumerate(starts)
-    ]
+    out_cols = slice(SIG + STATE, SIG + 2 * STATE)
+    out_tail = to_side(0, out_cols)
+    out_copy = map_copy(1)
     dout_copy = to_mate(5, dout_hbm.at[pl.ds(given, BLK)], dout_ref.at[BLK:ROWS])
+    tails = [to_side(1, slice(0, SIG + STATE)), to_side(2, slice(SIG + 2 * STATE, WIDE))]
+    map_copies = [map_copy(0), map_copy(2)]
     sig_copy = to_mate(4, sig_hbm.at[pl.ds(given, BLK)], sig_in.at[BLK:ROWS])
 
     lane = lax.broadcasted_iota(jnp.int32, (HERE, ROWS), 1)
@@ -272,6 +275,12 @@
 
     pad[EDGE : EDGE + BLK, :SIG] = sig_in[:BLK, :].astype(F32)
     pad[EDGE : EDGE + BLK, SIG:] = map_in[:BLK, :].astype(F32)
+    keep = jnp.where(me == 0, 0.0, 1.0).astype(F32)
+
+    def before(cols):
+        mine_then = tail_own[:, cols].astype(F32)
+        pad[:EDGE, cols] = keep * jnp.where(me == n - 1, mine_then, tail_got[:, cols].astype(F32))
+
     dt_copy.wait()
     own, got = dt_in[...], dt_got[...]
     own = jnp.where(odd == 0, own, turned(own))
@@ -317,13 +326,10 @@
                 tap_row, gtaps_ref.at[slot], tap_send.at[k], tap_recv.at[slot], fsdp=first + k
             ).wait_send()
 
-    tail_copy.wait()
-    for copy in map_copies:
-        copy.wait()
-    keep = jnp.where(me == 0, 0.0, 1.0).astype(F32)
-    before = jnp.where(me == n - 1, tail_own[...].astype(F32), tail_got[...].astype(F32))
-    pad[:EDGE] = before * keep
-    pad[EDGE + BLK :, SIG:] = map_in[BLK:, :].astype(F32)
+    out_tail.wait()
+    out_copy.wait()
+    before(out_cols)
+    pad[EDGE + BLK :, out_cols] = map_in[BLK:, third(1)].astype(F32)
     def map_rows(k, out):
         cols = slice(SIG + k * STATE, SIG + (k + 1) * STATE)
         v = preact(0, ROWS, cols, gtaps_ref[k, :KSIZE], gtaps_ref[k, KSIZE : KSIZE + 1])
@@ -369,6 +375,12 @@
     lax.fori_loop(1, n, send_g, 0)
     gr[me] = gs[me]
 
+    for copy in tails + map_copies:
+        copy.wait()
+    for cols in (slice(0, SIG + STATE), slice(SIG + 2 * STATE, WIDE)):
+        before(cols)
+    pad[EDGE + BLK :, SIG : SIG + STATE] = map_in[BLK:, third(0)].astype(F32)
+    pad[EDGE + BLK :, SIG + 2 * STATE :] = map_in[BLK:, third(2)].astype(F32)
     map_rows(0, imap_ref)
     v = preact(0, ROWS, slice(SIG + 2 * STATE, WIDE), mtaps_ref[...], mbias_ref[...])
     s = sigmoid(v)
@@ -457,10 +469,10 @@
         return 0
 
     lax.fori_loop(1, n, g_arrived, 0)
-    lax.fori_loop(0, n, to_front, zero)
+    lax.fori_loop(0, n, to_front, zero, unroll=4)
     lax.fori_loop(1, n, send_c, 0)
     lax.fori_loop(1, n, x_arrived, 0)
-    lax.fori_loop(0, n, to_back, zero)
+    lax.fori_loop(0, n, to_back, zero, unroll=4)
     lax.fori_loop(1, n, send_h, 0)
     lh[mine(me)] = yh[me]
     lc[me] = yc[me]
@@ -480,17 +492,19 @@
 
     def m_copy(k):
         return remote(
-            mg.at[k], mgot.at[side], ms_sem.at[k], mr_sem.at[side], fsdp=group + k * half
+            m_out.at[k], mgot.at[side], ms_sem.at[k], mr_sem.at[side], fsdp=group + k * half
         )
 
     def to_owner(k):
+        m_out[k] = mg[k].astype(BF16)
+
         @pl.when(group + k * half != f)
         def _():
             m_copy(k).start()
 
         @pl.when(group + k * half == f)
         def _():
-            mgot[side] = mg[k]
+            mgot[side] = m_out[k]
 
     def c_in(i, _):
         d = other(me, i, n)
@@ -650,10 +664,10 @@
         @pl.when(first + k != f)
         def _():
             remote(
-                mg.at[k], mgot.at[k], ms_sem.at[k], mr_sem.at[k], fsdp=first + k
+                m_out.at[k], mgot.at[k], ms_sem.at[k], mr_sem.at[k], fsdp=first + k
             ).wait_recv()
 
-    gpad[:ROWS, SIG:] = (mgot[0] + mgot[1]) * slope[:, SIG:]
+    gpad[:ROWS, SIG:] = (mgot[0].astype(F32) + mgot[1].astype(F32)) * slope[:, SIG:]
     map_rim = rim(1, map_cols)
     sums(map_cols, slice(SIG + 2 * STATE, WIDE), part_b, 1, 0)
     to_near(part_b, near_b, 10, q_near_b)
@@ -741,6 +755,7 @@
             vm((ROWS, SIG), F32),
             vm((ROWS, SIG), F32),
             vm((HERE, ROWS), F32),
+            vm((2, ROWS, STATE), BF16),
             vm((SIG, STATE), BF16),
             vm((n, 3 * share // 2, STATE), BF16),
             vm((HERE, 1, STATE), F32),
@@ -755,7 +770,7 @@
             vm((SIG, STATE), F32),
             vm((4, SIG, STATE), BF16),
             vm((2, ROWS, STATE), F32),
-            vm((2, ROWS, STATE), F32),
+            vm((2, ROWS, STATE), BF16),
             vm((ROWS + RIMS, OWN), F32),
             vm((RIMS, OWN), F32),
             vm((BLK, OWN), F32),
@@ -775,7 +790,7 @@
             vm((4, 8, STATE), F32),
             vm((8, STATE), F32),
         ]
-        + [dma((17,)), dma((6,)), dma((6,)), dma((1,)), dma((1,)), dma((2,)), dma((2,))]
+        + [dma((17,)), dma((6,)), dma((6,)), dma((3,)), dma((3,)), dma((2,)), dma((2,))]
         + [dma((n,))] * 10
         + [dma((2,)), dma((2,)), dma((4,)), dma((6,)), dma((21,)), dma((8,)), dma((4,)), dma((8,)), dma((4,))],
         compiler_params=pltpu.CompilerParams(
@@ -786,12 +801,18 @@
 
 
 def last_kernel(
-    scale, dsig_in, dmap_in, sums_in, small_in, ddt_in,
-    dsig, dmap, ddt, dtaps, dmtaps, dbias, dmbias, dalog, ddtb, dskip
+    scale, dsig_in, dmap_in, sums_hbm, small_hbm, ddt_in,
+    dsig, dmap, ddt, dtaps, dmtaps, dbias, dmbias, dalog, ddtb, dskip,
+    sums_in, small_in, sem
 ):
-    dsig[...] = dsig_in[...]
-    dmap[...] = dmap_in[...]
-    ddt[...] = ddt_in[...]
+    copies = []
+    for src, dst in (
+        (sums_hbm, sums_in), (small_hbm, small_in), (dsig_in, dsig), (dmap_in, dmap), (ddt_in, ddt)
+    ):
+        copies.append(pltpu.make_async_copy(src, dst, sem.at[len(copies)]))
+        copies[-1].start()
+    copies[0].wait()
+    copies[1].wait()
     for k in range(KSIZE + 1):
         for q in range(QUADS):
             at = k * QUADS + q
@@ -806,6 +827,8 @@
     for k, out in enumerate((dalog, ddtb, dskip)):
         at = KSIZE + 1 + k
         out[...] = small_in[at : at + 1, :HERE] * scale
+    for copy in copies[2:]:
+        copy.wait()
 
 
 def last(*operands):
@@ -817,9 +840,14 @@
     return pl.pallas_call(
         functools.partial(last_kernel, scale),
         out_shape=tuple(jax.ShapeDtypeStruct(s, F32) for s in shapes),
-        in_specs=[VM] * 5,
-        out_specs=(VM,) * len(shapes),
-        compiler_params=pltpu.CompilerParams(vmem_limit_bytes=8 * 1024 * 1024),
+        in_specs=[HBM] * 5,
+        out_specs=(HBM,) * 3 + (VM,) * (len(shapes) - 3),
+        scratch_shapes=[
+            pltpu.VMEM((SUMS, STATE), F32),
+            pltpu.VMEM((8, STATE), F32),
+            pltpu.SemaphoreType.DMA((5,)),
+        ],
+        compiler_params=pltpu.CompilerParams(vmem_limit_bytes=60 * 1024 * 1024),
         name="last",
     )(*operands)
 

time: 81 us -> 87.6 us (1.081)
  the two profiles are of different devices: /device:TPU:18 before, /device:TPU:26 now
where the time goes in v6:
time: 87.6 us; the launch traced here: 87.3 us
  Pallas kernels  86.7 us (99%)
    pallas_call x1, Pallas kernels, main(): pl.pallas_call(functools.partial(main_kernel, n, half), out_shape=(jax.Sh...  74.9 us
    pallas_call x1, Pallas kernels, last(): pl.pallas_call(functools.partial(last_kernel, scale), out_shape=tuple((ja...  11.8 us

profile of v6, /device:TPU:26, one launch (start us, length us, event | category | flops | bytes accessed | tf_op | source)
XLA Modules:
  0.0 87.3 jit_solution(10983159974312686314)
XLA Ops:
  0.6 74.9 %main.1 = (f32[128,512]{1,0:T(8,128)}, f32[128,128]{1,0:T(8,128)}, f32[24,128]{1,0:T(8,128)}, f32[8,128]{1,0:T(8,128)}, f32[8,128]{1,0:T(8,128)}) custom-call(bf16[128,512]{1,0:T(8,128)(2,1)} %sig_hbm.1, bf16[128,2048]{1,0:T(8,128)(2,1)} %map_hbm.1, f32[8,128]{1,0:T(8,128)} %bitcast.12, bf16[128,512]{1,0:T(8,128)(2,1)} %dout_hbm.1, f32[4,512]{1,0:T(4,128)} %taps_hbm.1, ...), custom_call_target="tpu_custom_call" | custom-call | tf_op jit(solution)/shard_map/main/pallas_call | solution.py:717
  75.5 11.8 %last.1 = (f32[128,512]{1,0:T(8,128)}, f32[128,128]{1,0:T(8,128)}, f32[8,128]{1,0:T(8,128)}, f32[4,512]{1,0:T(4,128)}, f32[4,128]{1,0:T(4,128)}, /*index=5*/f32[...) custom-call(f32[128,512]{1,0:T(8,128)} %get-tuple-element.25.dsig_in, ...), custom_call_target="tpu_custom_call" | custom-call | tf_op jit(solution)/shard_map/last/pallas_call | solution.py:840

commit v7 on v6

--- a/solution.py
+++ b/solution.py
@@ -111,7 +111,7 @@
     sig_in, map_in, dout_ref, dt_in, dt_got, taps_ref, bias_ref, mtaps_ref, mbias_ref,
     alog_ref, dtb_ref, skip_ref, tail_own, tail_got, tap_row, gtaps_ref,
     pad, slope, signal_ref, scaled_ref, weighted_ref, sgrad_ref, imap_ref, omap_ref, wide3, intra,
-    oh, gw, drow, m_out, xs, gs, es, xr, gr, er, yh, yc, lh, lc, first_local, second_sg, lk,
+    oh, gw, drow, m_out, xs, gs, es, xr, gr, er, yh, yc, lh, lc, first_local, first_sg, second_sg, lk,
     mg, mgot, gpad, rims, swap, stay, ddt_mine, ddt_got, ddt_ref,
     part, low_part, near, low_near, far, total, part_b, near_b, sum_b, far_b, total_b,
     l_sem, n_send, n_recv, b_send, b_recv, tap_send, tap_recv,
@@ -327,13 +327,18 @@
             ).wait_send()
 
     out_tail.wait()
-    out_copy.wait()
     before(out_cols)
-    pad[EDGE + BLK :, out_cols] = map_in[BLK:, third(1)].astype(F32)
-    def map_rows(k, out):
+    def map_rows(k, out, r, count):
         cols = slice(SIG + k * STATE, SIG + (k + 1) * STATE)
-        v = preact(0, ROWS, cols, gtaps_ref[k, :KSIZE], gtaps_ref[k, KSIZE : KSIZE + 1])
-        out[...] = (v * sigmoid(v)).astype(BF16)
+        v = preact(r, count, cols, gtaps_ref[k, :KSIZE], gtaps_ref[k, KSIZE : KSIZE + 1])
+        out[r : r + count, :] = (v * sigmoid(v)).astype(BF16)
+
+    def sgrad_rows(rows):
+        for q in range(QUADS):
+            cols3 = slice(2 * SIG + q * STATE, 2 * SIG + (q + 1) * STATE)
+            grad = dout_ref[rows, third(q)].astype(F32) * wide3[rows, cols3]
+            sgrad_ref[rows, third(q)] = grad.astype(BF16)
+        return tn(sgrad_ref[rows, :], omap_ref[rows, :])
 
     def mine(d):
         return pl.ds(pl.multiple_of(d * share, share), share)
@@ -358,14 +363,14 @@
         x_copy(other(me, i, n)).start()
         return 0
 
-    map_rows(1, omap_ref)
+    low, high = slice(0, BLK), slice(BLK, ROWS)
+    map_rows(1, omap_ref, 0, BLK)
+    first_sg[...] = sgrad_rows(low)
+    out_copy.wait()
+    pad[EDGE + BLK :, out_cols] = map_in[BLK:, third(1)].astype(F32)
+    map_rows(1, omap_ref, BLK, BLK)
     dout_copy.wait()
-    low, high = slice(0, BLK), slice(BLK, ROWS)
-    for q in range(QUADS):
-        cols3 = slice(2 * SIG + q * STATE, 2 * SIG + (q + 1) * STATE)
-        sgrad_ref[:, third(q)] = (dout_ref[:, third(q)].astype(F32) * wide3[:, cols3]).astype(BF16)
-    second_sg[...] = tn(sgrad_ref[high, :], omap_ref[high, :])
-    first_sg = tn(sgrad_ref[low, :], omap_ref[low, :])
+    second_sg[...] = sgrad_rows(high)
     for h in range(HERE):
         at = slice(h * HDIM, (h + 1) * HDIM)
         link = first_sg[at, :] + end_low8[h : h + 1] * second_sg[at, :]
@@ -381,7 +386,7 @@
         before(cols)
     pad[EDGE + BLK :, SIG : SIG + STATE] = map_in[BLK:, third(0)].astype(F32)
     pad[EDGE + BLK :, SIG + 2 * STATE :] = map_in[BLK:, third(2)].astype(F32)
-    map_rows(0, imap_ref)
+    map_rows(0, imap_ref, 0, ROWS)
     v = preact(0, ROWS, slice(SIG + 2 * STATE, WIDE), mtaps_ref[...], mbias_ref[...])
     s = sigmoid(v)
     slope[:, SIG:] = s * (1.0 + v * (1.0 - s))
@@ -768,6 +773,7 @@
             vm((n, 3 * share // 2, STATE), BF16),
             vm((SIG, STATE), F32),
             vm((SIG, STATE), F32),
+            vm((SIG, STATE), F32),
             vm((4, SIG, STATE), BF16),
             vm((2, ROWS, STATE), F32),
             vm((2, ROWS, STATE), BF16),
@@ -801,18 +807,12 @@
 
 
 def last_kernel(
-    scale, dsig_in, dmap_in, sums_hbm, small_hbm, ddt_in,
-    dsig, dmap, ddt, dtaps, dmtaps, dbias, dmbias, dalog, ddtb, dskip,
-    sums_in, small_in, sem
+    scale, dsig_in, dmap_in, sums_in, small_in, ddt_in,
+    dsig, dmap, ddt, dtaps, dmtaps, dbias, dmbias, dalog, ddtb, dskip
 ):
-    copies = []
-    for src, dst in (
-        (sums_hbm, sums_in), (small_hbm, small_in), (dsig_in, dsig), (dmap_in, dmap), (ddt_in, ddt)
-    ):
-        copies.append(pltpu.make_async_copy(src, dst, sem.at[len(copies)]))
-        copies[-1].start()
-    copies[0].wait()
-    copies[1].wait()
+    dsig[...] = dsig_in[...]
+    dmap[...] = dmap_in[...]
+    ddt[...] = ddt_in[...]
     for k in range(KSIZE + 1):
         for q in range(QUADS):
             at = k * QUADS + q
@@ -827,8 +827,6 @@
     for k, out in enumerate((dalog, ddtb, dskip)):
         at = KSIZE + 1 + k
         out[...] = small_in[at : at + 1, :HERE] * scale
-    for copy in copies[2:]:
-        copy.wait()
 
 
 def last(*operands):
@@ -840,13 +838,8 @@
     return pl.pallas_call(
         functools.partial(last_kernel, scale),
         out_shape=tuple(jax.ShapeDtypeStruct(s, F32) for s in shapes),
-        in_specs=[HBM] * 5,
-        out_specs=(HBM,) * 3 + (VM,) * (len(shapes) - 3),
-        scratch_shapes=[
-            pltpu.VMEM((SUMS, STATE), F32),
-            pltpu.VMEM((8, STATE), F32),
-            pltpu.SemaphoreType.DMA((5,)),
-        ],
+        in_specs=[VM] * 5,
+        out_specs=(VM,) * len(shapes),
         compiler_params=pltpu.CompilerParams(vmem_limit_bytes=60 * 1024 * 1024),
         name="last",
     )(*operands)

time: 87.6 us -> 77.8 us (0.89)
  Pallas kernels: 86.7 us -> 76.9 us
    pallas_call x1, Pallas kernels: 11.8 us -> 1.76 us  [last(): pl.pallas_call(functools.partial(last_kernel, scale), out_shape=tuple((ja...]
where the time goes in v7:
time: 77.8 us; the launch traced here: 77.6 us
  Pallas kernels  76.9 us (99%)
    pallas_call x1, Pallas kernels, main(): pl.pallas_call(functools.partial(main_kernel, n, half), out_shape=(jax.Sh...  75.2 us
    pallas_call x1, Pallas kernels, last(): pl.pallas_call(functools.partial(last_kernel, scale), out_shape=tuple((ja...  1.76 us

profile of v7, /device:TPU:26, one launch (start us, length us, event | category | flops | bytes accessed | tf_op | source)
XLA Modules:
  0.0 77.6 jit_solution(15341168725603203911)
XLA Ops:
  0.6 75.2 %main.1 = (f32[128,512]{1,0:T(8,128)}, f32[128,128]{1,0:T(8,128)}, f32[24,128]{1,0:T(8,128)}, f32[8,128]{1,0:T(8,128)}, f32[8,128]{1,0:T(8,128)}) custom-call(bf16[128,512]{1,0:T(8,128)(2,1)} %sig_hbm.1, bf16[128,2048]{1,0:T(8,128)(2,1)} %map_hbm.1, f32[8,128]{1,0:T(8,128)} %bitcast.12, bf16[128,512]{1,0:T(8,128)(2,1)} %dout_hbm.1, f32[4,512]{1,0:T(4,128)} %taps_hbm.1, ...), custom_call_target="tpu_custom_call" | custom-call | tf_op jit(solution)/shard_map/main/pallas_call | solution.py:722
  75.8 1.8 %last.1 = (f32[128,512]{1,0:T(8,128)}, f32[128,128]{1,0:T(8,128)}, f32[8,128]{1,0:T(8,128)}, f32[4,512]{1,0:T(4,128)}, f32[4,128]{1,0:T(4,128)}, /*index=5*/f32[...) custom-call(f32[128,512]{1,0:T(8,128)} %get-tuple-element.25.dsig_in, ...), custom_call_target="tpu_custom_call" | custom-call | tf_op jit(solution)/shard_map/last/pallas_call | solution.py:838

commit v8 on v7

--- a/solution.py
+++ b/solution.py
@@ -135,11 +135,8 @@
     starts = (group, GROUPS + group, f)
     barrier = pltpu.get_barrier_semaphore()
 
-    def greet(i, _):
-        signal(barrier, ctx=other(me, i, n))
-        return 0
-
-    lax.fori_loop(1, n, greet, 0)
+    for i in range(1, n):
+        signal(barrier, ctx=lax.rem(me + (i + 1) // 2 if i % 2 else me + n - i // 2, n))
     for k in range(2):
 
         @pl.when(group + k * half != f)
@@ -187,14 +184,27 @@
             )
         )
 
+    tap_row[KSIZE + 1 :] = jnp.zeros((8 - KSIZE - 1, STATE), F32)
+    selves = jnp.where(group == f, 1, 0) + jnp.where(group + half == f, 1, 0)
+    pl.semaphore_wait(barrier, n - 1 + 4 - 2 * selves)
+
+    def to_mate(i, src, dst):
+        copy = remote(src, dst, n_send.at[i], n_recv.at[i], ctx=mate)
+        copy.start()
+        return copy
+
+    def map_copy(k):
+        return to_mate(
+            1 + k, map_hbm.at[pl.ds(given, BLK), columns(starts[k])], map_in.at[BLK:ROWS, third(k)]
+        )
+
+    dt_copy = to_mate(0, dt_hbm, dt_got)
+    out_copy = map_copy(1)
+    dout_copy = to_mate(5, dout_hbm.at[pl.ds(given, BLK)], dout_ref.at[BLK:ROWS])
     for copy in local:
         copy.wait()
     tap_row[0:KSIZE] = mtaps_ref[...]
     tap_row[KSIZE : KSIZE + 1] = mbias_ref[...]
-    tap_row[KSIZE + 1 :] = jnp.zeros((8 - KSIZE - 1, STATE), F32)
-    selves = jnp.where(group == f, 1, 0) + jnp.where(group + half == f, 1, 0)
-    pl.semaphore_wait(barrier, n - 1 + 4 - 2 * selves)
-
     for k in range(2):
 
         @pl.when(first + k != f)
@@ -206,11 +216,6 @@
         @pl.when(group + k * half == f)
         def _():
             gtaps_ref[k] = tap_row[...]
-
-    def to_mate(i, src, dst):
-        copy = remote(src, dst, n_send.at[i], n_recv.at[i], ctx=mate)
-        copy.start()
-        return copy
 
     def to_side(i, dst_cols):
         copy = remote(
@@ -220,16 +225,8 @@
         copy.start()
         return copy
 
-    def map_copy(k):
-        return to_mate(
-            1 + k, map_hbm.at[pl.ds(given, BLK), columns(starts[k])], map_in.at[BLK:ROWS, third(k)]
-        )
-
-    dt_copy = to_mate(0, dt_hbm, dt_got)
     out_cols = slice(SIG + STATE, SIG + 2 * STATE)
     out_tail = to_side(0, out_cols)
-    out_copy = map_copy(1)
-    dout_copy = to_mate(5, dout_hbm.at[pl.ds(given, BLK)], dout_ref.at[BLK:ROWS])
     tails = [to_side(1, slice(0, SIG + STATE)), to_side(2, slice(SIG + 2 * STATE, WIDE))]
     map_copies = [map_copy(0), map_copy(2)]
     sig_copy = to_mate(4, sig_hbm.at[pl.ds(given, BLK)], sig_in.at[BLK:ROWS])
@@ -295,7 +292,7 @@
     to_end = jnp.exp(end - ds)
     col4 = nt(eye, jnp.concatenate([step, to_end, jnp.exp(ds), ds], axis=0), HIGH)
     ds_col = col4[:, 3 * HERE :]
-    wide3[...] = nn(col4[:, : 3 * HERE], spread3, HIGH)
+    wide3[:, 2 * SIG :] = nn(col4[:, 2 * HERE : 3 * HERE], spread1, HIGH)
     end_low8 = jnp.broadcast_to(end_low, (HERE, STATE))
     end_high8 = jnp.broadcast_to(end_high, (HERE, STATE))
     both_ends = end_low8 * end_high8
@@ -380,6 +377,7 @@
     lax.fori_loop(1, n, send_g, 0)
     gr[me] = gs[me]
 
+    wide3[:, : 2 * SIG] = nn(col4[:, : 2 * HERE], spread3[: 2 * HERE, : 2 * SIG], HIGH)
     for copy in tails + map_copies:
         copy.wait()
     for cols in (slice(0, SIG + STATE), slice(SIG + 2 * STATE, WIDE)):

time: 77.8 us -> 77.6 us (level)
  the two profiles are of different devices: /device:TPU:26 before, /device:TPU:18 now
where the time goes in v8:
time: 77.6 us; the launch traced here: 77.4 us
  Pallas kernels  76.8 us (99%)
    pallas_call x1, Pallas kernels, main(): pl.pallas_call(functools.partial(main_kernel, n, half), out_shape=(jax.Sh...  75 us
    pallas_call x1, Pallas kernels, last(): pl.pallas_call(functools.partial(last_kernel, scale), out_shape=tuple((ja...  1.76 us

profile of v8, /device:TPU:18, one launch (start us, length us, event | category | flops | bytes accessed | tf_op | source)
XLA Modules:
  0.0 77.4 jit_solution(16054740870041849610)
XLA Ops:
  0.6 75.0 %main.1 = (f32[128,512]{1,0:T(8,128)}, f32[128,128]{1,0:T(8,128)}, f32[24,128]{1,0:T(8,128)}, f32[8,128]{1,0:T(8,128)}, f32[8,128]{1,0:T(8,128)}) custom-call(bf16[128,512]{1,0:T(8,128)(2,1)} %sig_hbm.1, bf16[128,2048]{1,0:T(8,128)(2,1)} %map_hbm.1, f32[8,128]{1,0:T(8,128)} %bitcast.12, bf16[128,512]{1,0:T(8,128)(2,1)} %dout_hbm.1, f32[4,512]{1,0:T(4,128)} %taps_hbm.1, ...), custom_call_target="tpu_custom_call" | custom-call | tf_op jit(solution)/shard_map/main/pallas_call | solution.py:720
  75.7 1.8 %last.1 = (f32[128,512]{1,0:T(8,128)}, f32[128,128]{1,0:T(8,128)}, f32[8,128]{1,0:T(8,128)}, f32[4,512]{1,0:T(4,128)}, f32[4,128]{1,0:T(4,128)}, /*index=5*/f32[...) custom-call(f32[128,512]{1,0:T(8,128)} %get-tuple-element.25.dsig_in, ...), custom_call_target="tpu_custom_call" | custom-call | tf_op jit(solution)/shard_map/last/pallas_call | solution.py:836

commit v9 on v8

--- a/solution.py
+++ b/solution.py
@@ -239,17 +239,27 @@
     eye = jnp.where(row_id == col_id, 1.0, 0.0).astype(F32)
     eye8 = eye[:HERE, :HERE]
     ones8 = jnp.ones((HERE, ROWS), F32)
-    head3 = lax.broadcasted_iota(jnp.int32, (3 * HERE, 3 * SIG), 0)
-    spread3 = jnp.where(
-        lax.broadcasted_iota(jnp.int32, (3 * HERE, 3 * SIG), 1) // HDIM == head3, 1.0, 0.0
+    head1 = lax.broadcasted_iota(jnp.int32, (HERE, SIG), 0)
+    spread1 = jnp.where(
+        lax.broadcasted_iota(jnp.int32, (HERE, SIG), 1) // HDIM == head1, 1.0, 0.0
     ).astype(F32)
-    spread1 = spread3[:HERE, :SIG]
 
     def in_rows(ref):
         return nt(eye8, jnp.broadcast_to(ref[...], (ROWS, HERE)), HIGH)
 
+    spread_low = spread1.astype(BF16)
+
+    def halves(y):
+        top = y.astype(BF16)
+        return top, (y - top.astype(F32)).astype(BF16)
+
     def per_row(y):
-        return nt(spread1, y, HIGH)
+        top, rest = halves(y)
+        return nt(spread_low, top) + nt(spread_low, rest)
+
+    def widened(x):
+        top, rest = halves(x)
+        return nn(top, spread_low) + nn(rest, spread_low)
 
     def turned(x):
         return pltpu.roll(x, BLK, 1)
@@ -292,7 +302,7 @@
     to_end = jnp.exp(end - ds)
     col4 = nt(eye, jnp.concatenate([step, to_end, jnp.exp(ds), ds], axis=0), HIGH)
     ds_col = col4[:, 3 * HERE :]
-    wide3[:, 2 * SIG :] = nn(col4[:, 2 * HERE : 3 * HERE], spread1, HIGH)
+    wide3[:, 2 * SIG :] = widened(col4[:, 2 * HERE : 3 * HERE])
     end_low8 = jnp.broadcast_to(end_low, (HERE, STATE))
     end_high8 = jnp.broadcast_to(end_high, (HERE, STATE))
     both_ends = end_low8 * end_high8
@@ -377,7 +387,8 @@
     lax.fori_loop(1, n, send_g, 0)
     gr[me] = gs[me]
 
-    wide3[:, : 2 * SIG] = nn(col4[:, : 2 * HERE], spread3[: 2 * HERE, : 2 * SIG], HIGH)
+    wide3[:, :SIG] = widened(col4[:, :HERE])
+    wide3[:, SIG : 2 * SIG] = widened(col4[:, HERE : 2 * HERE])
     for copy in tails + map_copies:
         copy.wait()
     for cols in (slice(0, SIG + STATE), slice(SIG + 2 * STATE, WIDE)):
@@ -562,9 +573,6 @@
 
     sig_cols, map_cols = slice(0, SIG), slice(SIG, OWN)
     sig_rim = rim(0, sig_cols)
-    for q in range(QUADS):
-        sums(third(q), third(q), part, QUADS, q)
-
     planes = n // 2
     y = me // planes
     z = me - y * planes
@@ -600,9 +608,6 @@
         for k in range(1, 4):
             s = lax.rem(z_high + k, 4)
             remote(src, dst.at[s], q_send.at[k], recv_sem.at[s], ctx=mate).wait_recv()
-
-    low_part[...] = part[...].astype(BF16)
-    to_near(low_part, near, 0, q_near)
 
     def raw(r, out, taps, cols):
         acc = taps[RIM : RIM + 1] * gpad[r : r + BLK, cols]
@@ -638,6 +643,11 @@
     for b, rows in enumerate((low, high)):
         mg[1, rows, :] = mg[1, rows, :] + nn(sgrad_ref[rows, :], lk[b])
     to_owner(1)
+    for q in range(QUADS):
+        sums(third(q), third(q), part, QUADS, q)
+    low_part[...] = part[...].astype(BF16)
+    to_near(low_part, near, 0, q_near)
+
     end_terms = []
     for b, rows in enumerate((low, high)):
         oh[rows, :] = nt(omap_ref[rows, :], lk[b])
@@ -658,10 +668,6 @@
     ddt_copy.start()
     small(0, nt(ones8, grad_log * step, HIGH)[0:1] * (-jnp.exp(alog_ref[...])))
     small(1, nt(ones8, grad_dt, HIGH)[0:1])
-    near_in(low_part, near, q_near)
-    low_near[...] = jnp.sum(near[...].astype(F32), axis=0).astype(BF16)
-    to_far(low_near, far, 7, q_far)
-
     for k in range(2):
 
         @pl.when(first + k != f)
@@ -675,6 +681,9 @@
     sums(map_cols, slice(SIG + 2 * STATE, WIDE), part_b, 1, 0)
     to_near(part_b, near_b, 10, q_near_b)
     sig_out = transposed(1, sig_rim, taps_ref, sig_cols, dsig_hbm)
+    near_in(low_part, near, q_near)
+    low_near[...] = jnp.sum(near[...].astype(F32), axis=0).astype(BF16)
+    to_far(low_near, far, 7, q_far)
     map_out = transposed(2, map_rim, mtaps_ref, map_cols, dmap_hbm)
     near_in(part_b, near_b, q_near_b)
     sum_b[...] = jnp.sum(near_b[...], axis=0)

time: 77.6 us -> 78.1 us (level)
  the two profiles are of different devices: /device:TPU:18 before, /device:TPU:26 now
where the time goes in v9:
time: 78.1 us; the launch traced here: 78 us
  Pallas kernels  77.3 us (99%)
    pallas_call x1, Pallas kernels, main(): pl.pallas_call(functools.partial(main_kernel, n, half), out_shape=(jax.Sh...  75.6 us
    pallas_call x1, Pallas kernels, last(): pl.pallas_call(functools.partial(last_kernel, scale), out_shape=tuple((ja...  1.76 us

profile of v9, /device:TPU:26, one launch (start us, length us, event | category | flops | bytes accessed | tf_op | source)
XLA Modules:
  0.0 78.0 jit_solution(17053128700989370169)
XLA Ops:
  0.6 75.6 %main.1 = (f32[128,512]{1,0:T(8,128)}, f32[128,128]{1,0:T(8,128)}, f32[24,128]{1,0:T(8,128)}, f32[8,128]{1,0:T(8,128)}, f32[8,128]{1,0:T(8,128)}) custom-call(bf16[128,512]{1,0:T(8,128)(2,1)} %sig_hbm.1, bf16[128,2048]{1,0:T(8,128)(2,1)} %map_hbm.1, f32[8,128]{1,0:T(8,128)} %bitcast.12, bf16[128,512]{1,0:T(8,128)(2,1)} %dout_hbm.1, f32[4,512]{1,0:T(4,128)} %taps_hbm.1, ...), custom_call_target="tpu_custom_call" | custom-call | tf_op jit(solution)/shard_map/main/pallas_call | solution.py:729
  76.2 1.8 %last.1 = (f32[128,512]{1,0:T(8,128)}, f32[128,128]{1,0:T(8,128)}, f32[8,128]{1,0:T(8,128)}, f32[4,512]{1,0:T(4,128)}, f32[4,128]{1,0:T(4,128)}, /*index=5*/f32[...) custom-call(f32[128,512]{1,0:T(8,128)} %get-tuple-element.25.dsig_in, ...), custom_call_target="tpu_custom_call" | custom-call | tf_op jit(solution)/shard_map/last/pallas_call | solution.py:845

commit v10 on v9

--- a/solution.py
+++ b/solution.py
@@ -573,6 +573,9 @@
 
     sig_cols, map_cols = slice(0, SIG), slice(SIG, OWN)
     sig_rim = rim(0, sig_cols)
+    for q in range(QUADS):
+        sums(third(q), third(q), part, QUADS, q)
+
     planes = n // 2
     y = me // planes
     z = me - y * planes
@@ -608,6 +611,9 @@
         for k in range(1, 4):
             s = lax.rem(z_high + k, 4)
             remote(src, dst.at[s], q_send.at[k], recv_sem.at[s], ctx=mate).wait_recv()
+
+    low_part[...] = part[...].astype(BF16)
+    to_near(low_part, near, 0, q_near)
 
     def raw(r, out, taps, cols):
         acc = taps[RIM : RIM + 1] * gpad[r : r + BLK, cols]
@@ -643,11 +649,6 @@
     for b, rows in enumerate((low, high)):
         mg[1, rows, :] = mg[1, rows, :] + nn(sgrad_ref[rows, :], lk[b])
     to_owner(1)
-    for q in range(QUADS):
-        sums(third(q), third(q), part, QUADS, q)
-    low_part[...] = part[...].astype(BF16)
-    to_near(low_part, near, 0, q_near)
-
     end_terms = []
     for b, rows in enumerate((low, high)):
         oh[rows, :] = nt(omap_ref[rows, :], lk[b])
@@ -668,6 +669,10 @@
     ddt_copy.start()
     small(0, nt(ones8, grad_log * step, HIGH)[0:1] * (-jnp.exp(alog_ref[...])))
     small(1, nt(ones8, grad_dt, HIGH)[0:1])
+    near_in(low_part, near, q_near)
+    low_near[...] = jnp.sum(near[...].astype(F32), axis=0).astype(BF16)
+    to_far(low_near, far, 7, q_far)
+
     for k in range(2):
 
         @pl.when(first + k != f)
@@ -681,9 +686,6 @@
     sums(map_cols, slice(SIG + 2 * STATE, WIDE), part_b, 1, 0)
     to_near(part_b, near_b, 10, q_near_b)
     sig_out = transposed(1, sig_rim, taps_ref, sig_cols, dsig_hbm)
-    near_in(low_part, near, q_near)
-    low_near[...] = jnp.sum(near[...].astype(F32), axis=0).astype(BF16)
-    to_far(low_near, far, 7, q_far)
     map_out = transposed(2, map_rim, mtaps_ref, map_cols, dmap_hbm)
     near_in(part_b, near_b, q_near_b)
     sum_b[...] = jnp.sum(near_b[...], axis=0)

time: 78.1 us -> 77.5 us (level)
  no operation moved by 1% of the time
where the time goes in v10:
time: 77.5 us; the launch traced here: 77.4 us
  Pallas kernels  76.7 us (99%)
    pallas_call x1, Pallas kernels, main(): pl.pallas_call(functools.partial(main_kernel, n, half), out_shape=(jax.Sh...  74.9 us
    pallas_call x1, Pallas kernels, last(): pl.pallas_call(functools.partial(last_kernel, scale), out_shape=tuple((ja...  1.76 us

profile of v10, /device:TPU:26, one launch (start us, length us, event | category | flops | bytes accessed | tf_op | source)
XLA Modules:
  0.0 77.4 jit_solution(3450983101581887640)
XLA Ops:
  0.6 74.9 %main.1 = (f32[128,512]{1,0:T(8,128)}, f32[128,128]{1,0:T(8,128)}, f32[24,128]{1,0:T(8,128)}, f32[8,128]{1,0:T(8,128)}, f32[8,128]{1,0:T(8,128)}) custom-call(bf16[128,512]{1,0:T(8,128)(2,1)} %sig_hbm.1, bf16[128,2048]{1,0:T(8,128)(2,1)} %map_hbm.1, f32[8,128]{1,0:T(8,128)} %bitcast.12, bf16[128,512]{1,0:T(8,128)(2,1)} %dout_hbm.1, f32[4,512]{1,0:T(4,128)} %taps_hbm.1, ...), custom_call_target="tpu_custom_call" | custom-call | tf_op jit(solution)/shard_map/main/pallas_call | solution.py:731
  75.6 1.8 %last.1 = (f32[128,512]{1,0:T(8,128)}, f32[128,128]{1,0:T(8,128)}, f32[8,128]{1,0:T(8,128)}, f32[4,512]{1,0:T(4,128)}, f32[4,128]{1,0:T(4,128)}, /*index=5*/f32[...) custom-call(f32[128,512]{1,0:T(8,128)} %get-tuple-element.25.dsig_in, ...), custom_call_target="tpu_custom_call" | custom-call | tf_op jit(solution)/shard_map/last/pallas_call | solution.py:847
